TPU v7x, 32 devices: a whole 2x2x4 slice. The times are simulated.
32 devices in a mesh: dp: 8 (over y, x, core), seq: 4 (over z).
Axes of the slice: x: 2, y: 2, z: 4, core: 2. Of those that a mesh axis runs over, the one named last changes fastest.
Arguments:
- hidden_in: bfloat16 [8, 1024, 768], P('dp', 'seq'), may hold values from -8 to 8, as said below
- encoder_in: bfloat16 [8, 1024, 768], P('dp', 'seq'), may hold values from -6 to 6
- prefix_len: int32 [8], P('dp'), may hold values from 102 to 512, as said below
- exit_flags: int32 [8, 1024], P('dp', 'seq'), may hold values 0 or 1
- target_ids: int32 [8, 1024], P('dp', 'seq'), may hold values from 0 to 32127
- out_cotangent: float32 [8, 1024, 768], P('dp', 'seq'), may hold values from -6 to 6
- self_gain: bfloat16 [768], P('dp'), may hold values from 0.5 to 1.5
- self_query: bfloat16 [768, 768], P('dp', 'seq'), may hold values from -0.4375 to 0.4375
- self_key: bfloat16 [768, 768], P('dp', 'seq'), may hold values from -0.21875 to 0.21875
- self_value: bfloat16 [768, 768], P('dp', 'seq'), may hold values from -0.21875 to 0.21875
- self_output: bfloat16 [768, 768], P('dp', 'seq'), may hold values from -0.875 to 0.875
- cross_gain: bfloat16 [768], P('dp'), may hold values from 0.5 to 1.5
- cross_query: bfloat16 [768, 768], P('dp', 'seq'), may hold values from -0.4375 to 0.4375
- cross_key: bfloat16 [768, 768], P('dp', 'seq'), may hold values from -0.21875 to 0.21875
- cross_value: bfloat16 [768, 768], P('dp', 'seq'), may hold values from -0.21875 to 0.21875
- cross_output: bfloat16 [768, 768], P('dp', 'seq'), may hold values from -0.875 to 0.875
- feed_gain: bfloat16 [768], P('dp'), may hold values from 0.5 to 1.5
- feed_gate: bfloat16 [768, 2048], P('dp', 'seq'), may hold values from -0.21875 to 0.21875
- feed_up: bfloat16 [768, 2048], P('dp', 'seq'), may hold values from -0.21875 to 0.21875
- feed_down: bfloat16 [2048, 768], P('dp', 'seq'), may hold values from -0.25 to 0.25
- exit_gain: bfloat16 [768], P('dp'), may hold values from 0.5 to 1.5
- embedding: bfloat16 [32128, 768], P('dp', 'seq'), may hold values from -0.21875 to 0.21875
Outputs:
- block_output: bfloat16 [8, 1024, 768], P('dp', 'seq')
- token_losses: float32 [8, 1024], P('dp', 'seq')
- hidden_grad: float32 [8, 1024, 768], P('dp', 'seq')
- encoder_grad: float32 [8, 1024, 768], P('dp', 'seq')
- self_gain_grad: float32 [768], P('dp')
- self_query_grad: float32 [768, 768], P('dp', 'seq')
- self_key_grad: float32 [768, 768], P('dp', 'seq')
- self_value_grad: float32 [768, 768], P('dp', 'seq')
- self_output_grad: float32 [768, 768], P('dp', 'seq')
- cross_gain_grad: float32 [768], P('dp')
- cross_query_grad: float32 [768, 768], P('dp', 'seq')
- cross_key_grad: float32 [768, 768], P('dp', 'seq')
- cross_value_grad: float32 [768, 768], P('dp', 'seq')
- cross_output_grad: float32 [768, 768], P('dp', 'seq')
- feed_gain_grad: float32 [768], P('dp')
- feed_gate_grad: float32 [768, 2048], P('dp', 'seq')
- feed_up_grad: float32 [768, 2048], P('dp', 'seq')
- feed_down_grad: float32 [2048, 768], P('dp', 'seq')
- exit_gain_grad: float32 [768], P('dp')
- embedding_grad: float32 [32128, 768], P('dp', 'seq')
Inputs may be any that keep to these rules, and one draw needn't show every extreme that they name: `prefix_len`: each sequence's prefix length; both the shortest and the longest allowed value occur in every draw. `hidden_in`: the layer's input.
All inputs are finite; a program needn't handle non-finite values. No bound on the sum of `exit_flags` on one device may be relied on, other than what follows from the above.
Results may differ from a plain program's by a relative error of at most 0.033.
Values may be sent and summed in bfloat16 or wider, within the bound.
No kernel may reach another device: no remote copies, remote signals or barrier semaphores. Data moves between devices by JAX's collectives and lax.ppermute only.
A program may use at most 320 MiB of HBM per device.

v0:
```python
import jax
import jax.numpy as jnp
from jax import lax
from jax.sharding import PartitionSpec as P

HD = 64


norm_eps = 1e-06
masked_score = -1000000000.0


def product(first_op, second_op):
    return jnp.dot(first_op, second_op, preferred_element_type=jnp.float32)


def grad_product(first_op, second_op):
    return lax.dot_general(
        first_op, second_op, (((0,), (0,)), ((), ())), preferred_element_type=jnp.float32
    )


def back_product(first_op, second_op):
    return lax.dot_general(
        first_op, second_op, (((1,), (1,)), ((), ())), preferred_element_type=jnp.float32
    )


def norm_rows(inputs, scaling):
    return (
        inputs * lax.rsqrt(jnp.mean(inputs * inputs, axis=-1, keepdims=True) + norm_eps) * scaling
    )


def norm_back(inputs, scaling, upstream):
    unused, pullback = jax.vjp(norm_rows, inputs, scaling)
    return pullback(upstream)


def gated_unit(gate_in, upward):
    return jax.nn.gelu(gate_in, approximate=True) * upward


def split_heads(matrix):
    return matrix.reshape(matrix.shape[0], matrix.shape[1] // HD, HD)


def fetch_weights(shards):
    rows = (
        lax.all_gather(shards[0], "dp", axis=0, tiled=True),
        lax.all_gather(shards[1], "dp", axis=0, tiled=True),
        lax.all_gather(shards[2], "dp", axis=0, tiled=True),
        lax.all_gather(shards[3], "dp", axis=0, tiled=True),
        lax.all_gather(shards[4], "dp", axis=0, tiled=True),
        lax.all_gather(shards[5], "dp", axis=0, tiled=True),
        lax.all_gather(shards[6], "dp", axis=0, tiled=True),
        lax.all_gather(shards[7], "dp", axis=0, tiled=True),
        lax.all_gather(shards[8], "dp", axis=0, tiled=True),
        lax.all_gather(shards[9], "dp", axis=0, tiled=True),
        lax.all_gather(shards[10], "dp", axis=0, tiled=True),
        lax.all_gather(shards[11], "dp", axis=0, tiled=True),
        lax.all_gather(shards[12], "dp", axis=0, tiled=True),
        lax.all_gather(shards[13], "dp", axis=0, tiled=True),
        lax.all_gather(shards[14], "dp", axis=0, tiled=True),
        lax.all_gather(shards[15], "dp", axis=0, tiled=True),
    )
    whole = (
        lax.all_gather(rows[4], "seq", axis=1, tiled=True),
        lax.all_gather(rows[5], "seq", axis=1, tiled=True),
        lax.all_gather(rows[6], "seq", axis=1, tiled=True),
        lax.all_gather(rows[7], "seq", axis=1, tiled=True),
        lax.all_gather(rows[8], "seq", axis=1, tiled=True),
        lax.all_gather(rows[9], "seq", axis=1, tiled=True),
        lax.all_gather(rows[10], "seq", axis=1, tiled=True),
        lax.all_gather(rows[11], "seq", axis=1, tiled=True),
        lax.all_gather(rows[12], "seq", axis=1, tiled=True),
        lax.all_gather(rows[13], "seq", axis=1, tiled=True),
        lax.all_gather(rows[14], "seq", axis=1, tiled=True),
        lax.all_gather(rows[15], "seq", axis=1, tiled=True),
    )
    return ([piece.astype(jnp.float32) for piece in rows[:4]], list(whole))


def fetch_again(shards):
    rows = (
        lax.all_gather(shards[0], "dp", axis=0, tiled=True),
        lax.all_gather(shards[1], "dp", axis=0, tiled=True),
        lax.all_gather(shards[2], "dp", axis=0, tiled=True),
        lax.all_gather(shards[3], "dp", axis=0, tiled=True),
        lax.all_gather(shards[4], "dp", axis=0, tiled=True),
        lax.all_gather(shards[5], "dp", axis=0, tiled=True),
        lax.all_gather(shards[6], "dp", axis=0, tiled=True),
        lax.all_gather(shards[7], "dp", axis=0, tiled=True),
        lax.all_gather(shards[8], "dp", axis=0, tiled=True),
        lax.all_gather(shards[9], "dp", axis=0, tiled=True),
        lax.all_gather(shards[10], "dp", axis=0, tiled=True),
        lax.all_gather(shards[11], "dp", axis=0, tiled=True),
        lax.all_gather(shards[12], "dp", axis=0, tiled=True),
        lax.all_gather(shards[13], "dp", axis=0, tiled=True),
        lax.all_gather(shards[14], "dp", axis=0, tiled=True),
        lax.all_gather(shards[15], "dp", axis=0, tiled=True),
    )
    whole = (
        lax.all_gather(rows[4], "seq", axis=1, tiled=True),
        lax.all_gather(rows[5], "seq", axis=1, tiled=True),
        lax.all_gather(rows[6], "seq", axis=1, tiled=True),
        lax.all_gather(rows[7], "seq", axis=1, tiled=True),
        lax.all_gather(rows[8], "seq", axis=1, tiled=True),
        lax.all_gather(rows[9], "seq", axis=1, tiled=True),
        lax.all_gather(rows[10], "seq", axis=1, tiled=True),
        lax.all_gather(rows[11], "seq", axis=1, tiled=True),
        lax.all_gather(rows[12], "seq", axis=1, tiled=True),
        lax.all_gather(rows[13], "seq", axis=1, tiled=True),
        lax.all_gather(rows[14], "seq", axis=1, tiled=True),
        lax.all_gather(rows[15], "seq", axis=1, tiled=True),
    )
    return ([piece.astype(jnp.float32) for piece in rows[:4]], list(whole))


def score_block(queries, key_rows, allowed):
    scores = jnp.einsum(
        "qhe,khe->hqk", queries, key_rows, preferred_element_type=jnp.float32
    ) * HD ** (-0.5)
    if allowed is None:
        return scores
    return jnp.where(allowed[None], scores, masked_score)


def attend(queries, key_rows, values, allowed):
    scores = score_block(queries, key_rows, allowed)
    row_max = jnp.max(scores, axis=-1, keepdims=True)
    exponent = jnp.exp(scores - row_max)
    row_sum = jnp.sum(exponent, axis=-1, keepdims=True)
    shares = exponent / row_sum
    mixture = jnp.einsum(
        "hqk,khe->qhe", shares.astype(jnp.bfloat16), values, preferred_element_type=jnp.float32
    )
    return (mixture, row_max + jnp.log(row_sum))


def attend_back(queries, key_rows, values, allowed, log_total, upstream):
    scores = score_block(queries, key_rows, allowed)
    shares = jnp.exp(scores - log_total)
    share_grads = jnp.einsum("qhe,khe->hqk", upstream, values, preferred_element_type=jnp.float32)
    centre = jnp.sum(shares * share_grads, axis=-1, keepdims=True)
    score_grads = (shares * (share_grads - centre) * HD ** (-0.5)).astype(jnp.bfloat16)
    query_grads = jnp.einsum(
        "hqk,khe->qhe", score_grads, key_rows, preferred_element_type=jnp.float32
    )
    key_grads = jnp.einsum("hqk,qhe->khe", score_grads, queries, preferred_element_type=jnp.float32)
    value_grads = jnp.einsum(
        "hqk,qhe->khe", shares.astype(jnp.bfloat16), upstream, preferred_element_type=jnp.float32
    )
    return (query_grads, key_grads, value_grads)


def per_device(
    hidden_in,
    encoder_in,
    prefix_len,
    exit_flags,
    target_ids,
    out_cotangent,
    self_gain,
    self_query,
    self_key,
    self_value,
    self_output,
    cross_gain,
    cross_query,
    cross_key,
    cross_value,
    cross_output,
    feed_gain,
    feed_gate,
    feed_up,
    feed_down,
    exit_gain,
    embedding,
):
    seq_count, local_len, width = hidden_in.shape
    token_count = seq_count * local_len
    group_size = lax.axis_size("seq")
    shard_list = (
        self_gain,
        cross_gain,
        feed_gain,
        exit_gain,
        self_query,
        self_key,
        self_value,
        self_output,
        cross_query,
        cross_key,
        cross_value,
        cross_output,
        feed_gate,
        feed_up,
        feed_down,
        embedding,
    )
    gains, matrices = fetch_weights(shard_list)
    gain_one, gain_two, gain_three, gain_exit = gains
    (
        query_one,
        key_one,
        value_one,
        output_one,
        query_two,
        key_two,
        value_two,
        output_two,
        gate_full,
        up_full,
        down_full,
        vocab_table,
    ) = matrices
    query_pos = lax.axis_index("seq") * local_len + jnp.arange(local_len)
    key_pos = jnp.arange(local_len * group_size)
    allowed = (key_pos[None, None, :] <= query_pos[None, :, None]) | (
        key_pos[None, None, :] < prefix_len[:, None, None]
    )
    residual_in = hidden_in.astype(jnp.float32).reshape(token_count, width)
    normed_one = norm_rows(residual_in, gain_one).astype(jnp.bfloat16)
    queries_one = (
        product(normed_one, query_one).astype(jnp.bfloat16).reshape(seq_count, local_len, width)
    )
    keys_local = (
        product(normed_one, key_one).astype(jnp.bfloat16).reshape(seq_count, local_len, width)
    )
    values_local = (
        product(normed_one, value_one).astype(jnp.bfloat16).reshape(seq_count, local_len, width)
    )
    keys_all, values_all = (
        lax.all_gather(keys_local, "seq", axis=1, tiled=True),
        lax.all_gather(values_local, "seq", axis=1, tiled=True),
    )

    def self_forward(element):
        queries, key_rows, values, mask_rows = element
        return attend(split_heads(queries), split_heads(key_rows), split_heads(values), mask_rows)

    mixture_one, log_one = lax.map(self_forward, (queries_one, keys_all, values_all, allowed))
    mixture_one = mixture_one.reshape(token_count, width).astype(jnp.bfloat16)
    after_self = residual_in + product(mixture_one, output_one)
    normed_two = norm_rows(after_self, gain_two).astype(jnp.bfloat16)
    queries_two = (
        product(normed_two, query_two).astype(jnp.bfloat16).reshape(seq_count, local_len, width)
    )
    states_flat = encoder_in.reshape(-1, width)
    keys_mine = product(states_flat, key_two).astype(jnp.bfloat16).reshape(seq_count, -1, width)
    values_mine = product(states_flat, value_two).astype(jnp.bfloat16).reshape(seq_count, -1, width)
    cross_keys, cross_values = (
        lax.all_gather(keys_mine, "seq", axis=1, tiled=True),
        lax.all_gather(values_mine, "seq", axis=1, tiled=True),
    )

    def cross_forward(element):
        queries, key_rows, values = element
        return attend(split_heads(queries), split_heads(key_rows), split_heads(values), None)

    mixture_two, log_two = lax.map(cross_forward, (queries_two, cross_keys, cross_values))
    mixture_two = mixture_two.reshape(token_count, width).astype(jnp.bfloat16)
    after_cross = after_self + product(mixture_two, output_two)
    normed_three = norm_rows(after_cross, gain_three).astype(jnp.bfloat16)
    gate_pre = product(normed_three, gate_full)
    up_pre = product(normed_three, up_full)
    hidden_mid = gated_unit(gate_pre, up_pre).astype(jnp.bfloat16)
    after_feed = after_cross + product(hidden_mid, down_full)
    block_output = after_feed.astype(jnp.bfloat16).reshape(seq_count, local_len, width)
    normed_exit = norm_rows(after_feed, gain_exit).astype(jnp.bfloat16)
    logits = back_product(normed_exit, vocab_table)
    row_max = jnp.max(logits, axis=1, keepdims=True)
    log_total = row_max + jnp.log(jnp.sum(jnp.exp(logits - row_max), axis=1, keepdims=True))
    target_hits = jnp.arange(logits.shape[1])[None, :] == target_ids.reshape(token_count, 1)
    picked = jnp.sum(jnp.where(target_hits, logits, 0.0), axis=1, keepdims=True)
    flag_rows = exit_flags.reshape(token_count, 1).astype(jnp.float32)
    token_losses = (flag_rows * (log_total - picked)).reshape(seq_count, local_len)
    logit_grads = (
        flag_rows * (jnp.exp(logits - log_total) - target_hits.astype(jnp.float32))
    ).astype(jnp.bfloat16)
    table_terms = grad_product(logit_grads, normed_exit)
    gains, matrices = fetch_again(shard_list)
    gain_one, gain_two, gain_three, gain_exit = gains
    (
        query_one,
        key_one,
        value_one,
        output_one,
        query_two,
        key_two,
        value_two,
        output_two,
        gate_full,
        up_full,
        down_full,
        back_table,
    ) = matrices
    exit_in_grad = product(logit_grads, back_table)
    feed_grad, full_exit_gain = norm_back(after_feed, gain_exit, exit_in_grad)
    feed_grad = feed_grad + out_cotangent.reshape(token_count, width)
    branch_three = feed_grad.astype(jnp.bfloat16)
    full_feed_down = grad_product(hidden_mid, branch_three)
    hidden_mid_grad = back_product(branch_three, down_full)
    unused, gated_pull = jax.vjp(gated_unit, gate_pre, up_pre)
    gate_grad, up_grad = gated_pull(hidden_mid_grad)
    gate_grad = gate_grad.astype(jnp.bfloat16)
    up_grad = up_grad.astype(jnp.bfloat16)
    full_feed_gate = grad_product(normed_three, gate_grad)
    full_feed_up = grad_product(normed_three, up_grad)
    normed_three_grad = back_product(gate_grad, gate_full) + back_product(up_grad, up_full)
    cross_grad, full_feed_gain = norm_back(after_cross, gain_three, normed_three_grad)
    cross_grad = cross_grad + feed_grad
    branch_two = cross_grad.astype(jnp.bfloat16)
    full_cross_output = grad_product(mixture_two, branch_two)
    mixture_two_grad = (
        back_product(branch_two, output_two)
        .astype(jnp.bfloat16)
        .reshape(seq_count, local_len, width)
    )

    def cross_backward(element):
        queries, key_rows, values, log_rows, upstream = element
        return attend_back(
            split_heads(queries),
            split_heads(key_rows),
            split_heads(values),
            None,
            log_rows,
            split_heads(upstream),
        )

    query_two_grad, key_two_grad, value_two_grad = lax.map(
        cross_backward, (queries_two, cross_keys, cross_values, log_two, mixture_two_grad)
    )
    key_share, value_share = (
        lax.psum_scatter(
            key_two_grad.reshape(seq_count, -1, width).astype(jnp.bfloat16),
            "seq",
            scatter_dimension=1,
            tiled=True,
        ).astype(jnp.float32),
        lax.psum_scatter(
            value_two_grad.reshape(seq_count, -1, width).astype(jnp.bfloat16),
            "seq",
            scatter_dimension=1,
            tiled=True,
        ).astype(jnp.float32),
    )
    key_low = key_share.reshape(-1, width).astype(jnp.bfloat16)
    value_low = value_share.reshape(-1, width).astype(jnp.bfloat16)
    full_cross_key = grad_product(states_flat, key_low)
    full_cross_value = grad_product(states_flat, value_low)
    encoder_grad = (back_product(key_low, key_two) + back_product(value_low, value_two)).reshape(
        encoder_in.shape
    )
    query_low = query_two_grad.reshape(token_count, width).astype(jnp.bfloat16)
    full_cross_query = grad_product(normed_two, query_low)
    self_grad, full_cross_gain = norm_back(after_self, gain_two, back_product(query_low, query_two))
    self_grad = self_grad + cross_grad
    branch_one = self_grad.astype(jnp.bfloat16)
    full_self_output = grad_product(mixture_one, branch_one)
    mixture_one_grad = (
        back_product(branch_one, output_one)
        .astype(jnp.bfloat16)
        .reshape(seq_count, local_len, width)
    )

    def self_backward(element):
        queries, key_rows, values, mask_rows, log_rows, upstream = element
        return attend_back(
            split_heads(queries),
            split_heads(key_rows),
            split_heads(values),
            mask_rows,
            log_rows,
            split_heads(upstream),
        )

    query_one_grad, key_one_grad, value_one_grad = lax.map(
        self_backward, (queries_one, keys_all, values_all, allowed, log_one, mixture_one_grad)
    )
    key_mine, value_mine = (
        lax.psum_scatter(
            key_one_grad.reshape(seq_count, -1, width).astype(jnp.bfloat16),
            "seq",
            scatter_dimension=1,
            tiled=True,
        ).astype(jnp.float32),
        lax.psum_scatter(
            value_one_grad.reshape(seq_count, -1, width).astype(jnp.bfloat16),
            "seq",
            scatter_dimension=1,
            tiled=True,
        ).astype(jnp.float32),
    )
    key_own = key_mine.reshape(token_count, width).astype(jnp.bfloat16)
    value_own = value_mine.reshape(token_count, width).astype(jnp.bfloat16)
    query_own = query_one_grad.reshape(token_count, width).astype(jnp.bfloat16)
    full_self_query = grad_product(normed_one, query_own)
    full_self_key = grad_product(normed_one, key_own)
    full_self_value = grad_product(normed_one, value_own)
    normed_one_grad = (
        back_product(query_own, query_one)
        + back_product(key_own, key_one)
        + back_product(value_own, value_one)
    )
    input_grad, full_self_gain = norm_back(residual_in, gain_one, normed_one_grad)
    hidden_grad = (input_grad + self_grad).reshape(hidden_in.shape)
    column_sums = (
        lax.psum_scatter(
            full_self_query.astype(jnp.bfloat16), "seq", scatter_dimension=1, tiled=True
        ).astype(jnp.float32),
        lax.psum_scatter(
            full_self_key.astype(jnp.bfloat16), "seq", scatter_dimension=1, tiled=True
        ).astype(jnp.float32),
        lax.psum_scatter(
            full_self_value.astype(jnp.bfloat16), "seq", scatter_dimension=1, tiled=True
        ).astype(jnp.float32),
        lax.psum_scatter(
            full_self_output.astype(jnp.bfloat16), "seq", scatter_dimension=1, tiled=True
        ).astype(jnp.float32),
        lax.psum_scatter(
            full_cross_query.astype(jnp.bfloat16), "seq", scatter_dimension=1, tiled=True
        ).astype(jnp.float32),
        lax.psum_scatter(
            full_cross_key.astype(jnp.bfloat16), "seq", scatter_dimension=1, tiled=True
        ).astype(jnp.float32),
        lax.psum_scatter(
            full_cross_value.astype(jnp.bfloat16), "seq", scatter_dimension=1, tiled=True
        ).astype(jnp.float32),
        lax.psum_scatter(
            full_cross_output.astype(jnp.bfloat16), "seq", scatter_dimension=1, tiled=True
        ).astype(jnp.float32),
        lax.psum_scatter(
            full_feed_gate.astype(jnp.bfloat16), "seq", scatter_dimension=1, tiled=True
        ).astype(jnp.float32),
        lax.psum_scatter(
            full_feed_up.astype(jnp.bfloat16), "seq", scatter_dimension=1, tiled=True
        ).astype(jnp.float32),
        lax.psum_scatter(
            full_feed_down.astype(jnp.bfloat16), "seq", scatter_dimension=1, tiled=True
        ).astype(jnp.float32),
        lax.psum_scatter(
            table_terms.astype(jnp.bfloat16), "seq", scatter_dimension=1, tiled=True
        ).astype(jnp.float32),
    )
    gain_totals = lax.psum((full_self_gain, full_cross_gain, full_feed_gain, full_exit_gain), "seq")
    (
        self_gain_grad,
        cross_gain_grad,
        feed_gain_grad,
        exit_gain_grad,
        self_query_grad,
        self_key_grad,
        self_value_grad,
        self_output_grad,
        cross_query_grad,
        cross_key_grad,
        cross_value_grad,
        cross_output_grad,
        feed_gate_grad,
        feed_up_grad,
        feed_down_grad,
        embedding_grad,
    ) = (
        lax.psum_scatter(gain_totals[0], "dp", scatter_dimension=0, tiled=True),
        lax.psum_scatter(gain_totals[1], "dp", scatter_dimension=0, tiled=True),
        lax.psum_scatter(gain_totals[2], "dp", scatter_dimension=0, tiled=True),
        lax.psum_scatter(gain_totals[3], "dp", scatter_dimension=0, tiled=True),
        lax.psum_scatter(column_sums[0], "dp", scatter_dimension=0, tiled=True),
        lax.psum_scatter(column_sums[1], "dp", scatter_dimension=0, tiled=True),
        lax.psum_scatter(column_sums[2], "dp", scatter_dimension=0, tiled=True),
        lax.psum_scatter(column_sums[3], "dp", scatter_dimension=0, tiled=True),
        lax.psum_scatter(column_sums[4], "dp", scatter_dimension=0, tiled=True),
        lax.psum_scatter(column_sums[5], "dp", scatter_dimension=0, tiled=True),
        lax.psum_scatter(column_sums[6], "dp", scatter_dimension=0, tiled=True),
        lax.psum_scatter(column_sums[7], "dp", scatter_dimension=0, tiled=True),
        lax.psum_scatter(column_sums[8], "dp", scatter_dimension=0, tiled=True),
        lax.psum_scatter(column_sums[9], "dp", scatter_dimension=0, tiled=True),
        lax.psum_scatter(column_sums[10], "dp", scatter_dimension=0, tiled=True),
        lax.psum_scatter(column_sums[11], "dp", scatter_dimension=0, tiled=True),
    )
    return (
        block_output,
        token_losses,
        hidden_grad,
        encoder_grad,
        self_gain_grad,
        self_query_grad,
        self_key_grad,
        self_value_grad,
        self_output_grad,
        cross_gain_grad,
        cross_query_grad,
        cross_key_grad,
        cross_value_grad,
        cross_output_grad,
        feed_gain_grad,
        feed_gate_grad,
        feed_up_grad,
        feed_down_grad,
        exit_gain_grad,
        embedding_grad,
    )


def solution(mesh):
    placed = (
        P("dp", "seq", None),
        P("dp", "seq", None),
        P("dp"),
        P("dp", "seq"),
        P("dp", "seq"),
        P("dp", "seq", None),
        P("dp"),
        P("dp", "seq"),
        P("dp", "seq"),
        P("dp", "seq"),
        P("dp", "seq"),
        P("dp"),
        P("dp", "seq"),
        P("dp", "seq"),
        P("dp", "seq"),
        P("dp", "seq"),
        P("dp"),
        P("dp", "seq"),
        P("dp", "seq"),
        P("dp", "seq"),
        P("dp"),
        P("dp", "seq"),
    )
    return jax.shard_map(
        per_device,
        mesh=mesh,
        in_specs=placed,
        out_specs=(
            P("dp", "seq", None),
            P("dp", "seq"),
            P("dp", "seq", None),
            P("dp", "seq", None),
            P("dp"),
            P("dp", "seq"),
            P("dp", "seq"),
            P("dp", "seq"),
            P("dp", "seq"),
            P("dp"),
            P("dp", "seq"),
            P("dp", "seq"),
            P("dp", "seq"),
            P("dp", "seq"),
            P("dp"),
            P("dp", "seq"),
            P("dp", "seq"),
            P("dp", "seq"),
            P("dp"),
            P("dp", "seq"),
        ),
        check_vma=False,
    )
```

profile of v0, /device:TPU:8, one launch (start us, length us, event | category | flops | bytes accessed | tf_op | source)
XLA Modules:
  0.0 3669.7 jit_solution(6305153730843046321)
XLA Ops:
  114.5 28.9 all-gather.31.cloned.1.call-done
  183.3 21.6 all_gather.151
  205.0 19.6 all-gather.55.cloned.1.call-done
  239.0 27.3 reshape.507
  270.0 23.8 all-gather.49.cloned.1.call-done
  296.4 35.5 all-gather.47.cloned.1.call-done
  346.5 16.7 all-gather.29.cloned.1.call-done
  365.1 29.0 all-gather.33.cloned.1.call-done
  396.1 35.8 all-gather.53.cloned.1.call-done
  434.6 35.3 all-gather.51.cloned.1.call-done
  483.8 17.5 all-gather.37.cloned.1.call-done
  503.9 59.5 %all-gather.39.cloned.1.call-done = bf16[768,2048]{1,0:T(8,128)(2,1)} async-done(((bf16[768,512]{1,0:T(8,128)(2,1)}), bf16[768,2048]{1,0:T(8,128)(2,1)}) %all-gather.39.cloned.1.call-update) | async-done | bytes 3145744 | tf_op jit(solution)/shard_map/all_gather | solution.py:76
  567.7 59.3 %all-gather.41.cloned.1.call-done = bf16[768,2048]{1,0:T(8,128)(2,1)} async-done(((bf16[768,512]{1,0:T(8,128)(2,1)}), bf16[768,2048]{1,0:T(8,128)(2,1)}) %all-gather.41.cloned.1.call-update) | async-done | bytes 3145744 | tf_op jit(solution)/shard_map/all_gather | solution.py:77
  632.4 58.1 %all-gather.43.cloned.1.call-done = bf16[2048,768]{0,1:T(8,128)(2,1)} async-done(((bf16[2048,192]{0,1:T(8,128)(2,1)}), bf16[2048,768]{0,1:T(8,128)(2,1)}) %all-gather.43.cloned.1.call-update) | async-done | bytes 3145744 | tf_op jit(solution)/shard_map/all_gather | solution.py:78
  693.9 815.9 %all-gather.45.cloned.1.call-done = bf16[32128,768]{0,1:T(8,128)(2,1)} async-done(((bf16[32128,192]{0,1:T(8,128)(2,1)}), bf16[32128,768]{0,1:T(8,128)(2,1)}) %all-gather.45.cloned.1.call-update) | async-done | bytes 49348624 | tf_op jit(solution)/shard_map/all_gather | solution.py:79
  1509.8 32.4 fusion.163
  1542.2 16.1 select_reduce_fusion
  1559.0 30.7 multiply_reduce_fusion.3
  1617.6 35.4 fusion.68
  1653.7 26.9 fusion.83
  1703.6 35.2 fusion.74
  1738.9 31.8 convolution_convert_fusion
  1777.7 34.0 fusion.80
  1836.2 743.7 %reduce-scatter.83.cloned.1.call-done = bf16[32128,192]{0,1:T(8,128)(2,1)} async-done(((bf16[32128,768]{0,1:T(8,128)(2,1)}), bf16[32128,192]{0,1:T(8,128)(2,1)}) %reduce-scatter.83.cloned.1.call-update) | async-done | bytes 12337168 | tf_op jit(solution)/shard_map/reduce_scatter | solution.py:444
  2579.9 20.8 copy.149
  2614.9 28.0 reduce-scatter.63.cloned.1.call-done
  2645.0 28.2 reduce-scatter.61.cloned.1.call-done
  2675.2 28.1 reduce-scatter.55.cloned.1.call-done
  2705.4 28.0 reduce-scatter.67.cloned.1.call-done
  2735.5 28.2 reduce-scatter.65.cloned.1.call-done
  2765.8 28.2 reduce-scatter.59.cloned.1.call-done
  2796.3 27.8 reduce-scatter.57.cloned.1.call-done
  2826.2 60.6 %reduce-scatter.79.cloned.1.call-done = bf16[2048,192]{0,1:T(8,128)(2,1)} async-done(((bf16[2048,768]{0,1:T(8,128)(2,1)}), bf16[2048,192]{0,1:T(8,128)(2,1)}) %reduce-scatter.79.cloned.1.call-update) | async-done | bytes 786448 | tf_op jit(solution)/shard_map/reduce_scatter | solution.py:441
  2889.3 60.1 %reduce-scatter.75.cloned.1.call-done = bf16[768,512]{1,0:T(8,128)(2,1)} async-done(((bf16[768,2048]{1,0:T(8,128)(2,1)}), bf16[768,512]{1,0:T(8,128)(2,1)}) %reduce-scatter.75.cloned.1.call-update) | async-done | bytes 786448 | tf_op jit(solution)/shard_map/reduce_scatter | solution.py:438
  2952.1 60.5 %reduce-scatter.71.cloned.1.call-done = bf16[768,512]{1,0:T(8,128)(2,1)} async-done(((bf16[768,2048]{1,0:T(8,128)(2,1)}), bf16[768,512]{1,0:T(8,128)(2,1)}) %reduce-scatter.71.cloned.1.call-update) | async-done | bytes 786448 | tf_op jit(solution)/shard_map/reduce_scatter | solution.py:435
  3023.4 24.5 all-reduce.8
  3068.6 158.6 %reduce-scatter.101.cloned.1.call-done = f32[4016,192]{1,0:T(8,128)} async-done(((f32[32128,192]{1,0:T(8,128)}), f32[4016,192]{1,0:T(8,128)}) %reduce-scatter.101.cloned.1.call-update) | async-done | bytes 3084304
  3232.4 33.5 reduce-scatter.99.cloned.1.call-done
  3265.9 38.6 %reduce-scatter.93.cloned.1.call-done = f32[96,192]{1,0:T(8,128)} async-done(((f32[768,192]{1,0:T(8,128)}), f32[96,192]{1,0:T(8,128)}) %reduce-scatter.93.cloned.1.call-update) | async-done | bytes 73744
  3304.5 38.6 %reduce-scatter.91.cloned.1.call-done = f32[96,192]{1,0:T(8,128)} async-done(((f32[768,192]{1,0:T(8,128)}), f32[96,192]{1,0:T(8,128)}) %reduce-scatter.91.cloned.1.call-update) | async-done | bytes 73744
  3343.0 38.7 %reduce-scatter.85.cloned.1.call-done = f32[96,192]{1,0:T(8,128)} async-done(((f32[768,192]{1,0:T(8,128)}), f32[96,192]{1,0:T(8,128)}) %reduce-scatter.85.cloned.1.call-update) | async-done | bytes 73744
  3381.8 38.6 %reduce-scatter.97.cloned.1.call-done = f32[96,192]{1,0:T(8,128)} async-done(((f32[768,192]{1,0:T(8,128)}), f32[96,192]{1,0:T(8,128)}) %reduce-scatter.97.cloned.1.call-update) | async-done | bytes 73744
  3420.3 38.7 %reduce-scatter.95.cloned.1.call-done = f32[96,192]{1,0:T(8,128)} async-done(((f32[768,192]{1,0:T(8,128)}), f32[96,192]{1,0:T(8,128)}) %reduce-scatter.95.cloned.1.call-update) | async-done | bytes 73744
  3459.0 38.7 %reduce-scatter.89.cloned.1.call-done = f32[96,192]{1,0:T(8,128)} async-done(((f32[768,192]{1,0:T(8,128)}), f32[96,192]{1,0:T(8,128)}) %reduce-scatter.89.cloned.1.call-update) | async-done | bytes 73744
  3497.7 38.7 %reduce-scatter.87.cloned.1.call-done = f32[96,192]{1,0:T(8,128)} async-done(((f32[768,192]{1,0:T(8,128)}), f32[96,192]{1,0:T(8,128)}) %reduce-scatter.87.cloned.1.call-update) | async-done | bytes 73744
  3536.4 42.1 %reduce-scatter.81.cloned.1.call-done = f32[256,192]{0,1:T(8,128)} async-done(((f32[2048,192]{0,1:T(8,128)}), f32[256,192]{0,1:T(8,128)}) %reduce-scatter.81.cloned.1.call-update) | async-done | bytes 196624 | tf_op jit(solution)/shard_map/reduce_scatter | solution.py:481
  3578.5 42.2 %reduce-scatter.77.cloned.1.call-done = f32[96,512]{1,0:T(8,128)} async-done(((f32[768,512]{1,0:T(8,128)}), f32[96,512]{1,0:T(8,128)}) %reduce-scatter.77.cloned.1.call-update) | async-done | bytes 196624 | tf_op jit(solution)/shard_map/reduce_scatter | solution.py:480
  3620.7 42.1 %reduce-scatter.73.cloned.1.call-done = f32[96,512]{1,0:T(8,128)} async-done(((f32[768,512]{1,0:T(8,128)}), f32[96,512]{1,0:T(8,128)}) %reduce-scatter.73.cloned.1.call-update) | async-done | bytes 196624 | tf_op jit(solution)/shard_map/reduce_scatter | solution.py:479
  (354 shorter events, 369.7 us)
Async XLA Ops:
  7.3 68.0 %all-gather.27.cloned.1.call-start = ((), (), s32[]{:S(2)}) async-start(), calls=%async_computation.30 | async-start | bytes 1474560 | tf_op jit(solution)/shard_map/all_gather | solution.py:69
  18.2 62.0 %all-gather.23.cloned.1.call-start = ((), (), s32[]{:S(2)}) async-start(), calls=%async_computation.28 | async-start | bytes 1474560 | tf_op jit(solution)/shard_map/all_gather | solution.py:70
  28.4 83.4 %all-gather.35.cloned.1.call-start = ((), (), s32[]{:S(2)}) async-start(), calls=%async_computation.34 | async-start | bytes 1474560 | tf_op jit(solution)/shard_map/all_gather | solution.py:73
  38.2 105.1 %all-gather.31.cloned.1.call-start = ((), (), s32[]{:S(2)}) async-start(), calls=%async_computation.32 | async-start | bytes 1474560 | tf_op jit(solution)/shard_map/all_gather | solution.py:74
  48.5 176.0 %all-gather.55.cloned.1.call-start = ((), (), s32[]{:S(2)}) async-start(), calls=%async_computation.63 | async-start | bytes 14155776 | tf_op jit(solution)/shard_map/all_gather | solution.py:65
  49.1 218.8 %all-gather.25.cloned.1.call-start = ((), (), s32[]{:S(2)}) async-start(), calls=%async_computation.29 | async-start | bytes 1474560 | tf_op jit(solution)/shard_map/all_gather | solution.py:68
  58.9 234.9 %all-gather.49.cloned.1.call-start = ((), (), s32[]{:S(2)}) async-start(), calls=%async_computation.60 | async-start | bytes 1966080 | tf_op jit(solution)/shard_map/all_gather | solution.py:235
  75.1 192.8 %copy-start.29 = (f32[768]{0:T(1024)}, f32[768]{0:T(1024)S(1)}, u32[]{:S(2)}) copy-start(f32[768]{0:T(1024)S(1)} %convert_element_type.335) | copy-start | bytes 9220
  75.3 192.6 %copy-start.44 = (f32[256]{0:T(256)}, f32[256]{0:T(256)S(1)}, u32[]{:S(2)}) copy-start(f32[256]{0:T(256)S(1)} %fusion.127) | copy-start | bytes 3076
  77.9 253.9 %all-gather.47.cloned.1.call-start = ((), (), s32[]{:S(2)}) async-start(), calls=%async_computation.59 | async-start | bytes 1966080 | tf_op jit(solution)/shard_map/all_gather | solution.py:236
  82.8 280.4 %all-gather.29.cloned.1.call-start = ((), (), s32[]{:S(2)}) async-start(), calls=%async_computation.31 | async-start | bytes 1474560 | tf_op jit(solution)/shard_map/all_gather | solution.py:71
  93.3 300.9 %all-gather.33.cloned.1.call-start = ((), (), s32[]{:S(2)}) async-start(), calls=%async_computation.33 | async-start | bytes 1474560 | tf_op jit(solution)/shard_map/all_gather | solution.py:72
  103.7 328.2 %all-gather.53.cloned.1.call-start = ((), (), s32[]{:S(2)}) async-start(), calls=%async_computation.62 | async-start | bytes 1966080 | tf_op jit(solution)/shard_map/all_gather | solution.py:254
  114.4 355.5 %all-gather.51.cloned.1.call-start = ((), (), s32[]{:S(2)}) async-start(), calls=%async_computation.61 | async-start | bytes 1966080 | tf_op jit(solution)/shard_map/all_gather | solution.py:255
  145.9 355.3 %all-gather.37.cloned.1.call-start = ((), (), s32[]{:S(2)}) async-start(), calls=%async_computation.35 | async-start | bytes 1474560 | tf_op jit(solution)/shard_map/all_gather | solution.py:75
  156.4 407.1 %all-gather.39.cloned.1.call-start = ((), (), s32[]{:S(2)}) async-start(), calls=%async_computation.36 | async-start | bytes 3932160 | tf_op jit(solution)/shard_map/all_gather | solution.py:76
  172.1 454.9 %all-gather.41.cloned.1.call-start = ((), (), s32[]{:S(2)}) async-start(), calls=%async_computation.37 | async-start | bytes 3932160 | tf_op jit(solution)/shard_map/all_gather | solution.py:77
  183.2 507.3 %all-gather.43.cloned.1.call-start = ((), (), s32[]{:S(2)}) async-start(), calls=%async_computation.38 | async-start | bytes 3932160 | tf_op jit(solution)/shard_map/all_gather | solution.py:78
  204.9 1304.9 %all-gather.45.cloned.1.call-start = ((), (), s32[]{:S(2)}) async-start(), calls=%async_computation.39 | async-start | bytes 61685760 | tf_op jit(solution)/shard_map/all_gather | solution.py:79
  266.3 1547.1 %reduce-scatter.53.cloned.1.call-start = ((), (), s32[]{:S(2)}) async-start(), calls=%async_computation.43 | async-start | bytes 1966080 | tf_op jit(solution)/shard_map/reduce_scatter | solution.py:343
  693.8 815.9 %copy-start.60 = (f32[256]{0:T(256)}, f32[256]{0:T(256)S(1)}, u32[]{:S(2)}) copy-start(f32[256]{0:T(256)S(1)} %get-tuple-element.236) | copy-start | bytes 3076
  1609.7 206.4 %reduce-scatter.51.cloned.1.call-start = ((), (), s32[]{:S(2)}) async-start(), calls=%async_computation.42 | async-start | bytes 1966080 | tf_op jit(solution)/shard_map/reduce_scatter | solution.py:337
  1653.0 165.7 %reduce-scatter.49.cloned.1.call-start = ((), (), s32[]{:S(2)}) async-start(), calls=%async_computation.41 | async-start | bytes 1966080 | tf_op jit(solution)/shard_map/reduce_scatter | solution.py:390
  1695.7 125.7 %reduce-scatter.47.cloned.1.call-start = ((), (), s32[]{:S(2)}) async-start(), calls=%async_computation.40 | async-start | bytes 1966080 | tf_op jit(solution)/shard_map/reduce_scatter | solution.py:384
  1738.8 841.1 %reduce-scatter.83.cloned.1.call-start = ((), (), s32[]{:S(2)}) async-start(), calls=%async_computation.58 | async-start | bytes 61685760 | tf_op jit(solution)/shard_map/reduce_scatter | solution.py:444
  1770.7 842.0 %reduce-scatter.69.cloned.1.call-start = ((), (), s32[]{:S(2)}) async-start(), calls=%async_computation.51 | async-start | bytes 1474560 | tf_op jit(solution)/shard_map/reduce_scatter | solution.py:432
  1773.2 869.7 %reduce-scatter.63.cloned.1.call-start = ((), (), s32[]{:S(2)}) async-start(), calls=%async_computation.48 | async-start | bytes 1474560 | tf_op jit(solution)/shard_map/reduce_scatter | solution.py:423
  1775.9 897.3 %reduce-scatter.61.cloned.1.call-start = ((), (), s32[]{:S(2)}) async-start(), calls=%async_computation.47 | async-start | bytes 1474560 | tf_op jit(solution)/shard_map/reduce_scatter | solution.py:420
  1777.6 925.7 %reduce-scatter.55.cloned.1.call-start = ((), (), s32[]{:S(2)}) async-start(), calls=%async_computation.44 | async-start | bytes 1474560 | tf_op jit(solution)/shard_map/reduce_scatter | solution.py:411
  1813.4 920.1 %reduce-scatter.67.cloned.1.call-start = ((), (), s32[]{:S(2)}) async-start(), calls=%async_computation.50 | async-start | bytes 1474560 | tf_op jit(solution)/shard_map/reduce_scatter | solution.py:429
  1816.0 947.7 %reduce-scatter.65.cloned.1.call-start = ((), (), s32[]{:S(2)}) async-start(), calls=%async_computation.49 | async-start | bytes 1474560 | tf_op jit(solution)/shard_map/reduce_scatter | solution.py:426
  1818.6 975.4 %reduce-scatter.59.cloned.1.call-start = ((), (), s32[]{:S(2)}) async-start(), calls=%async_computation.46 | async-start | bytes 1474560 | tf_op jit(solution)/shard_map/reduce_scatter | solution.py:417
  1821.3 1002.8 %reduce-scatter.57.cloned.1.call-start = ((), (), s32[]{:S(2)}) async-start(), calls=%async_computation.45 | async-start | bytes 1474560 | tf_op jit(solution)/shard_map/reduce_scatter | solution.py:414
  1824.1 1062.7 %reduce-scatter.79.cloned.1.call-start = ((), (), s32[]{:S(2)}) async-start(), calls=%async_computation.56 | async-start | bytes 3932160 | tf_op jit(solution)/shard_map/reduce_scatter | solution.py:441
  1828.2 1121.3 %reduce-scatter.75.cloned.1.call-start = ((), (), s32[]{:S(2)}) async-start(), calls=%async_computation.54 | async-start | bytes 3932160 | tf_op jit(solution)/shard_map/reduce_scatter | solution.py:438
  1832.2 1180.3 %reduce-scatter.71.cloned.1.call-start = ((), (), s32[]{:S(2)}) async-start(), calls=%async_computation.52 | async-start | bytes 3932160 | tf_op jit(solution)/shard_map/reduce_scatter | solution.py:435
  1836.2 1391.0 %reduce-scatter.101.cloned.1.call-start = ((), (), s32[]{:S(2)}) async-start(), calls=%async_computation.72 | async-start | bytes 37011456
  2600.8 665.2 %reduce-scatter.99.cloned.1.call-start = ((), (), s32[]{:S(2)}) async-start(), calls=%async_computation.71 | async-start | bytes 884736
  2614.8 689.7 %reduce-scatter.93.cloned.1.call-start = ((), (), s32[]{:S(2)}) async-start(), calls=%async_computation.68 | async-start | bytes 884736
  2645.0 698.1 %reduce-scatter.91.cloned.1.call-start = ((), (), s32[]{:S(2)}) async-start(), calls=%async_computation.67 | async-start | bytes 884736
  2675.2 706.6 %reduce-scatter.85.cloned.1.call-start = ((), (), s32[]{:S(2)}) async-start(), calls=%async_computation.64 | async-start | bytes 884736
  2705.4 715.0 %reduce-scatter.97.cloned.1.call-start = ((), (), s32[]{:S(2)}) async-start(), calls=%async_computation.70 | async-start | bytes 884736
  2735.5 723.6 %reduce-scatter.95.cloned.1.call-start = ((), (), s32[]{:S(2)}) async-start(), calls=%async_computation.69 | async-start | bytes 884736
  2765.7 732.0 %reduce-scatter.89.cloned.1.call-start = ((), (), s32[]{:S(2)}) async-start(), calls=%async_computation.66 | async-start | bytes 884736
  2796.0 740.4 %reduce-scatter.87.cloned.1.call-start = ((), (), s32[]{:S(2)}) async-start(), calls=%async_computation.65 | async-start | bytes 884736
  2826.1 752.4 %reduce-scatter.81.cloned.1.call-start = ((), (), s32[]{:S(2)}) async-start(), calls=%async_computation.57 | async-start | bytes 1769472 | tf_op jit(solution)/shard_map/reduce_scatter | solution.py:481
  2889.3 731.4 %reduce-scatter.77.cloned.1.call-start = ((), (), s32[]{:S(2)}) async-start(), calls=%async_computation.55 | async-start | bytes 1769472 | tf_op jit(solution)/shard_map/reduce_scatter | solution.py:480
  2952.0 710.8 %reduce-scatter.73.cloned.1.call-start = ((), (), s32[]{:S(2)}) async-start(), calls=%async_computation.53 | async-start | bytes 1769472 | tf_op jit(solution)/shard_map/reduce_scatter | solution.py:479
  (63 other events, 2706.5 us)
Sparse Core Ops, SparseCore 0:
  18.3 30.1 all-gather.26
  50.7 29.4 all-gather.22
  82.3 29.4 all-gather.34
  113.9 29.4 all-gather.30
  145.1 79.3 all-gather.54
  226.0 29.9 all-gather.24
  258.1 35.6 all-gather.48
  295.9 35.8 all-gather.46
  333.4 29.7 all-gather.28
  364.6 29.4 all-gather.32
  396.3 35.6 all-gather.52
  434.0 35.8 all-gather.50
  471.5 29.7 all-gather.36
  502.7 60.7 all-gather.38
  564.9 62.0 all-gather.40
  628.4 62.0 all-gather.42
  692.0 817.7 all-gather.44
  1609.8 35.2 reduce-scatter.52
  1653.1 35.2 reduce-scatter.50
  1695.8 35.2 reduce-scatter.48
  1739.0 35.2 reduce-scatter.46
  1776.6 803.2 reduce-scatter.82
  2582.2 30.4 reduce-scatter.68
  2614.9 27.9 reduce-scatter.62
  2645.2 27.9 reduce-scatter.60
  2675.3 27.9 reduce-scatter.54
  2705.5 27.9 reduce-scatter.66
  2735.7 27.9 reduce-scatter.64
  2766.0 27.9 reduce-scatter.58
  2796.1 27.9 reduce-scatter.56
  2826.4 60.3 reduce-scatter.78
  2889.1 60.3 reduce-scatter.74
  2952.2 60.3 reduce-scatter.70
  3016.3 210.8 reduce-scatter.100
  3230.9 34.9 reduce-scatter.98
  3269.5 34.9 reduce-scatter.92
  3308.1 34.9 reduce-scatter.90
  3346.8 34.9 reduce-scatter.84
  3385.3 34.9 reduce-scatter.96
  3424.1 34.9 reduce-scatter.94
  3462.7 34.9 reduce-scatter.88
  3501.4 34.9 reduce-scatter.86
  3540.1 38.2 reduce-scatter.80
  3582.3 38.3 reduce-scatter.76
  3624.4 38.3 reduce-scatter.72
where the time goes:
time: 3680 us; the launch traced here: 3670 us
  waiting for transfers between devices  2970 us (81%)
  matrix products  358 us (10%)
  blocking collectives  172 us (5%)
  local copies, waits for them, and re-layouts  111 us (3%)
  other arithmetic  39.4 us (1%)
    all_gather x1, waiting for transfers between devices, fetch_weights(): lax.all_gather(rows[15], 'seq', axis=1, tiled=True)  816 us
    reduce_scatter x1, waiting for transfers between devices, per_device(): lax.psum_scatter(table_terms.astype(jnp.bfloat16), 'seq', scatter_dimensi...  744 us
    unnamed x54, waiting for transfers between devices  464 us
    unnamed x156, local copies, waits for them, and re-layouts  79 us
  transfers between devices with their start and end apart: 45, of which 39 were waited for; matrix products, arithmetic and copies ran while one was open for 11% of the time, Pallas kernels for 0%

commit v1 on v0

v1 whole, which is shorter than its diff:
```python
import functools

import jax
import jax.numpy as jnp
from jax import lax
from jax.experimental import pallas as pl
from jax.experimental.pallas import tpu as pltpu
from jax.sharding import PartitionSpec as P

HD = 64
QUERY_ROWS = 256
GAIN_LANES = 128

norm_eps = 1e-06
masked_score = -1000000000.0
both = ("seq", "dp")


def contract(first_op, second_op, first_dim, second_dim):
    return lax.dot_general(
        first_op,
        second_op,
        (((first_dim,), (second_dim,)), ((), ())),
        preferred_element_type=jnp.float32,
    )


def mix(spec, first_op, second_op):
    return jnp.einsum(spec, first_op, second_op, preferred_element_type=jnp.float32)


def norm_rows(inputs, scaling):
    return (
        inputs * lax.rsqrt(jnp.mean(inputs * inputs, axis=-1, keepdims=True) + norm_eps) * scaling
    )


def norm_back(inputs, scaling, upstream):
    unused, pullback = jax.vjp(norm_rows, inputs, scaling)
    return pullback(upstream)


def gated_unit(gate_in, upward):
    return jax.nn.gelu(gate_in, approximate=True) * upward


def swap(pieces):
    return lax.all_to_all(pieces, "seq", 0, 0, tiled=True)


def head_lanes(width, head):
    lanes = lax.broadcasted_iota(jnp.int32, (1, width), 1)
    return (lanes >= head * HD) & (lanes < (head + 1) * HD)


def attend_kernel(prefix_ref, *refs, places, width, causal):
    out_ref = refs[-1]
    step = pl.program_id(0)
    (q_at, q_lane), (k_at, k_lane), (v_at, v_lane) = places
    rows = out_ref.shape[0]
    queries = refs[q_at][pl.ds(pl.multiple_of(step * rows, rows), rows), q_lane : q_lane + width]
    key_rows = refs[k_at][:, k_lane : k_lane + width]
    values = refs[v_at][:, v_lane : v_lane + width]
    count = key_rows.shape[0]
    queries = queries * jnp.asarray(HD**-0.5, queries.dtype)
    if causal:
        query_pos = step * rows + lax.broadcasted_iota(jnp.int32, (rows, count), 0)
        key_pos = lax.broadcasted_iota(jnp.int32, (rows, count), 1)
        allowed = (key_pos <= query_pos) | (key_pos < prefix_ref[0])
    total = jnp.zeros((rows, width), jnp.float32)
    for head in range(width // HD):
        mine = head_lanes(width, head)
        scores = contract(jnp.where(mine, queries, jnp.zeros_like(queries)), key_rows, 1, 1)
        if causal:
            scores = jnp.where(allowed, scores, masked_score)
        exponent = jnp.exp(scores - jnp.max(scores, axis=1, keepdims=True))
        shares = exponent * (1.0 / jnp.sum(exponent, axis=1, keepdims=True))
        total = jnp.where(mine, contract(shares.astype(values.dtype), values, 1, 0), total)
    out_ref[...] = total.astype(out_ref.dtype)


def attend_back_kernel(prefix_ref, *refs, places, spots, width, causal):
    count_in = 1 + max(at for at, lane in places)
    upstream_ref = refs[count_in]
    outs = refs[count_in + 1 : -2]
    key_sum, value_sum = refs[-2:]
    step = pl.program_id(0)
    (q_at, q_lane), (k_at, k_lane), (v_at, v_lane) = places
    (dq_at, dq_lane), (dk_at, dk_lane), (dv_at, dv_lane) = spots
    rows = upstream_ref.shape[0]
    block = pl.ds(pl.multiple_of(step * rows, rows), rows)
    queries = refs[q_at][block, q_lane : q_lane + width]
    key_rows = refs[k_at][:, k_lane : k_lane + width]
    values = refs[v_at][:, v_lane : v_lane + width]
    upstream = upstream_ref[...]
    count = key_rows.shape[0]
    queries = queries * jnp.asarray(HD**-0.5, queries.dtype)
    if causal:
        key_pos = lax.broadcasted_iota(jnp.int32, (count, rows), 0)
        query_pos = step * rows + lax.broadcasted_iota(jnp.int32, (count, rows), 1)
        allowed = (key_pos <= query_pos) | (key_pos < prefix_ref[0])
    query_grads = jnp.zeros((rows, width), jnp.float32)
    key_grads = jnp.zeros((count, width), jnp.float32)
    value_grads = jnp.zeros((count, width), jnp.float32)
    for head in range(width // HD):
        mine = head_lanes(width, head)
        scores = contract(key_rows, jnp.where(mine, queries, jnp.zeros_like(queries)), 1, 1)
        if causal:
            scores = jnp.where(allowed, scores, masked_score)
        exponent = jnp.exp(scores - jnp.max(scores, axis=0, keepdims=True))
        shares = exponent * (1.0 / jnp.sum(exponent, axis=0, keepdims=True))
        share_grads = contract(values, jnp.where(mine, upstream, jnp.zeros_like(upstream)), 1, 1)
        centre = jnp.sum(shares * share_grads, axis=0, keepdims=True)
        score_grads = (shares * (share_grads - centre)).astype(queries.dtype)
        query_grads = jnp.where(mine, contract(score_grads, key_rows, 0, 0), query_grads)
        key_grads = jnp.where(mine, contract(score_grads, queries, 1, 0), key_grads)
        value_grads = jnp.where(
            mine, contract(shares.astype(upstream.dtype), upstream, 1, 0), value_grads
        )
    outs[dq_at][block, dq_lane : dq_lane + width] = (query_grads * HD**-0.5).astype(
        outs[dq_at].dtype
    )

    @pl.when(step == 0)
    def _():
        key_sum[...] = key_grads
        value_sum[...] = value_grads

    @pl.when(step > 0)
    def _():
        key_sum[...] += key_grads
        value_sum[...] += value_grads

    @pl.when(step == pl.num_programs(0) - 1)
    def _():
        outs[dk_at][:, dk_lane : dk_lane + width] = key_sum[...].astype(outs[dk_at].dtype)
        outs[dv_at][:, dv_lane : dv_lane + width] = value_sum[...].astype(outs[dv_at].dtype)


def whole(array):
    return pl.BlockSpec(array.shape, lambda step: (0,) * len(array.shape))


def attend(prefix, arrays, places, width, causal):
    count = arrays[0].shape[0]
    rows = min(QUERY_ROWS, count)
    return pl.pallas_call(
        functools.partial(attend_kernel, places=places, width=width, causal=causal),
        grid=(count // rows,),
        in_specs=[pl.BlockSpec(memory_space=pltpu.SMEM)] + [whole(array) for array in arrays],
        out_specs=pl.BlockSpec((rows, width), lambda step: (step, 0)),
        out_shape=jax.ShapeDtypeStruct((count, width), jnp.bfloat16),
    )(prefix, *arrays)


def attend_back(prefix, arrays, upstream, places, spots, out_widths, width, causal):
    count = arrays[0].shape[0]
    rows = min(QUERY_ROWS, count)
    shapes = [jax.ShapeDtypeStruct((count, lanes), jnp.bfloat16) for lanes in out_widths]
    return pl.pallas_call(
        functools.partial(
            attend_back_kernel, places=places, spots=spots, width=width, causal=causal
        ),
        grid=(count // rows,),
        in_specs=[pl.BlockSpec(memory_space=pltpu.SMEM)]
        + [whole(array) for array in arrays]
        + [pl.BlockSpec((rows, width), lambda step: (step, 0))],
        out_specs=[whole(shape) for shape in shapes],
        out_shape=shapes,
        scratch_shapes=[pltpu.VMEM((count, width), jnp.float32)] * 2,
    )(prefix, *arrays, upstream)


def per_device(
    hidden_in,
    encoder_in,
    prefix_len,
    exit_flags,
    target_ids,
    out_cotangent,
    self_gain,
    self_query,
    self_key,
    self_value,
    self_output,
    cross_gain,
    cross_query,
    cross_key,
    cross_value,
    cross_output,
    feed_gain,
    feed_gate,
    feed_up,
    feed_down,
    exit_gain,
    embedding,
):
    seq_count, local_len, width = hidden_in.shape
    n_seq = lax.axis_size("seq")
    n_dp = lax.axis_size("dp")
    own = self_query.shape[1]
    own_feed = feed_gate.shape[1]
    own_rows = self_query.shape[0]
    vocab_rows = embedding.shape[0]
    low = jnp.bfloat16

    gains = jnp.stack([self_gain, cross_gain, feed_gain, exit_gain], axis=1)
    gains = jnp.pad(gains, ((0, 0), (0, GAIN_LANES - gains.shape[1])))
    self_pack = jnp.concatenate([self_query, self_key, self_value, self_output, gains], axis=1)
    self_full = lax.all_gather(self_pack, both, axis=0, tiled=True).reshape(n_seq, width, -1)
    cross_pack = jnp.concatenate([cross_query, cross_key, cross_value, cross_output], axis=1)
    cross_full = lax.all_gather(cross_pack, both, axis=0, tiled=True).reshape(n_seq, width, -1)
    feed_pack = jnp.concatenate([feed_gate, feed_up], axis=1)
    feed_full = lax.all_gather(feed_pack, both, axis=0, tiled=True).reshape(n_seq, width, -1)
    down_full = lax.all_gather(feed_down.T, both, axis=0, tiled=True).reshape(
        n_seq, n_dp, own, feed_down.shape[0]
    )
    table = lax.all_gather(embedding.T, "seq", axis=0, tiled=True)
    marks = lax.all_gather(jnp.concatenate([exit_flags, target_ids], axis=0), "dp", axis=0)

    self_qkv, self_out = self_full[:, :, : 3 * own], self_full[:, :, 3 * own : 4 * own]
    cross_q, cross_kv = cross_full[:, :, :own], cross_full[:, :, own : 3 * own]
    cross_out = cross_full[:, :, 3 * own :]
    gain_rows = self_full[0, :, 4 * own : 4 * own + 4].astype(jnp.float32).T
    gain_one, gain_two, gain_three, gain_exit = gain_rows

    residual_in = hidden_in.astype(jnp.float32).reshape(-1, width)
    token_count = residual_in.shape[0]
    normed_one = norm_rows(residual_in, gain_one).astype(low)
    qkv_one = swap(mix("td,zdn->ztn", normed_one, self_qkv).astype(low)).reshape(-1, 3 * own)
    self_places = ((0, 0), (0, own), (0, 2 * own))
    mixture_one = attend(prefix_len, [qkv_one], self_places, own, True)
    mixture_one = swap(mixture_one.reshape(n_seq, token_count, own))
    mixture_one = mixture_one.transpose(1, 0, 2).reshape(token_count, width)
    after_self = residual_in + mix("td,zdn->tzn", mixture_one, self_out).reshape(
        token_count, width
    )
    normed_two = norm_rows(after_self, gain_two).astype(low)
    states = encoder_in.reshape(-1, width)
    kv_two = swap(mix("td,zdn->ztn", states, cross_kv).astype(low)).reshape(-1, 2 * own)
    q_two = swap(mix("td,zdn->ztn", normed_two, cross_q).astype(low)).reshape(-1, own)
    cross_places = ((0, 0), (1, 0), (1, own))
    mixture_two = attend(prefix_len, [q_two, kv_two], cross_places, own, False)
    mixture_two = swap(mixture_two.reshape(n_seq, token_count, own))
    mixture_two = mixture_two.transpose(1, 0, 2).reshape(token_count, width)
    after_cross = after_self + mix("td,zdn->tzn", mixture_two, cross_out).reshape(
        token_count, width
    )
    normed_three = norm_rows(after_cross, gain_three).astype(low)
    gate_up = mix("td,zdn->ztn", normed_three, feed_full)
    gate_pre, up_pre = gate_up[:, :, :own_feed], gate_up[:, :, own_feed:]
    hidden_mid = gated_unit(gate_pre, up_pre).astype(low)
    hidden_rows = hidden_mid.transpose(1, 0, 2).reshape(token_count, n_dp, -1)
    after_feed = after_cross + mix("tkr,zknr->tzn", hidden_rows, down_full).reshape(
        token_count, width
    )
    block_output = after_feed.astype(low).reshape(hidden_in.shape)
    normed_exit = norm_rows(after_feed, gain_exit).astype(low)

    tokens = lax.all_gather(normed_exit, "dp", axis=0, tiled=True)
    flag_rows = marks[:, 0].reshape(-1, 1).astype(jnp.float32)
    target_rows = marks[:, 1].reshape(-1, 1) - lax.axis_index("dp") * vocab_rows
    logits = contract(tokens, table, 1, 0)
    row_max = jnp.max(logits, axis=1, keepdims=True)
    row_sum = jnp.sum(jnp.exp(logits - row_max), axis=1, keepdims=True)
    hits = jnp.arange(vocab_rows)[None, :] == target_rows
    picked = jnp.sum(jnp.where(hits, logits, 0.0), axis=1, keepdims=True)
    parts = lax.all_gather(jnp.stack([row_max[:, 0], row_sum[:, 0], picked[:, 0]]), "dp", axis=0)
    top = jnp.max(parts[:, 0], axis=0)
    log_total = top + jnp.log(jnp.sum(parts[:, 1] * jnp.exp(parts[:, 0] - top), axis=0))
    all_losses = flag_rows[:, 0] * (log_total - jnp.sum(parts[:, 2], axis=0))
    token_losses = lax.dynamic_slice(
        all_losses, (lax.axis_index("dp") * token_count,), (token_count,)
    ).reshape(exit_flags.shape)
    logit_grads = (
        flag_rows * (jnp.exp(logits - log_total[:, None]) - hits.astype(jnp.float32))
    ).astype(low)
    exit_in_grad = lax.psum_scatter(
        contract(logit_grads, table, 1, 1).astype(low), "dp", scatter_dimension=0, tiled=True
    ).astype(jnp.float32)
    embedding_grad = lax.psum_scatter(
        contract(tokens, logit_grads, 0, 0).astype(low), "seq", scatter_dimension=0, tiled=True
    ).astype(jnp.float32).T

    def scatter(full):
        return lax.psum_scatter(
            full.reshape(-1, full.shape[-1]).astype(low), both, scatter_dimension=0, tiled=True
        ).astype(jnp.float32)

    feed_grad, full_exit_gain = norm_back(after_feed, gain_exit, exit_in_grad)
    feed_grad = feed_grad + out_cotangent.reshape(token_count, width)
    branch_three = feed_grad.astype(low)
    branch_cols = branch_three.reshape(token_count, n_seq, own)
    down_grad = scatter(mix("tzn,tkr->zknr", branch_cols, hidden_rows)).T
    hidden_mid_grad = (
        mix("tzn,zknr->tkr", branch_cols, down_full)
        .reshape(token_count, n_seq, own_feed)
        .transpose(1, 0, 2)
    )
    unused, gated_pull = jax.vjp(gated_unit, gate_pre, up_pre)
    gate_grad, up_grad = gated_pull(hidden_mid_grad)
    gate_up_grad = jnp.concatenate([gate_grad.astype(low), up_grad.astype(low)], axis=2)
    feed_sums = scatter(mix("td,ztn->zdn", normed_three, gate_up_grad))
    normed_three_grad = mix("ztn,zdn->td", gate_up_grad, feed_full)
    cross_grad, full_feed_gain = norm_back(after_cross, gain_three, normed_three_grad)
    cross_grad = cross_grad + feed_grad
    branch_two = cross_grad.astype(low)
    branch_cols = branch_two.reshape(token_count, n_seq, own)
    mixture_two_grad = mix("twm,wdm->td", branch_cols, cross_out).astype(low)
    mixture_two_grad = swap(mixture_two_grad.reshape(token_count, n_seq, own).transpose(1, 0, 2))
    q_grad, kv_grad = attend_back(
        prefix_len,
        [q_two, kv_two],
        mixture_two_grad.reshape(-1, own),
        cross_places,
        cross_places,
        (own, 2 * own),
        own,
        False,
    )
    q_grad = swap(q_grad.reshape(n_seq, token_count, own))
    kv_grad = swap(kv_grad.reshape(n_seq, token_count, 2 * own))
    encoder_grad = mix("ztn,zdn->td", kv_grad, cross_kv).reshape(encoder_in.shape)
    cross_sums = scatter(
        jnp.concatenate(
            [
                mix("td,ztn->zdn", normed_two, q_grad).astype(low),
                mix("td,ztn->zdn", states, kv_grad).astype(low),
                mix("td,tzn->zdn", mixture_two, branch_cols).astype(low),
            ],
            axis=2,
        )
    )
    self_grad, full_cross_gain = norm_back(
        after_self, gain_two, mix("ztn,zdn->td", q_grad, cross_q)
    )
    self_grad = self_grad + cross_grad
    branch_one = self_grad.astype(low)
    branch_cols = branch_one.reshape(token_count, n_seq, own)
    mixture_one_grad = mix("twm,wdm->td", branch_cols, self_out).astype(low)
    mixture_one_grad = swap(mixture_one_grad.reshape(token_count, n_seq, own).transpose(1, 0, 2))
    (qkv_grad,) = attend_back(
        prefix_len,
        [qkv_one],
        mixture_one_grad.reshape(-1, own),
        self_places,
        self_places,
        (3 * own,),
        own,
        True,
    )
    qkv_grad = swap(qkv_grad.reshape(n_seq, token_count, 3 * own))
    normed_one_grad = mix("ztn,zdn->td", qkv_grad, self_qkv)
    input_grad, full_self_gain = norm_back(residual_in, gain_one, normed_one_grad)
    hidden_grad = (input_grad + self_grad).reshape(hidden_in.shape)
    gain_terms = jnp.stack(
        [full_self_gain, full_cross_gain, full_feed_gain, full_exit_gain], axis=1
    ).astype(low)
    gain_terms = jnp.pad(gain_terms, ((0, 0), (0, GAIN_LANES - gain_terms.shape[1])))
    self_sums = scatter(
        jnp.concatenate(
            [
                mix("td,ztn->zdn", normed_one, qkv_grad).astype(low),
                mix("td,tzn->zdn", mixture_one, branch_cols).astype(low),
                jnp.broadcast_to(gain_terms[None], (n_seq, width, GAIN_LANES)),
            ],
            axis=2,
        )
    )

    def piece(sums, at):
        return sums[:, at * own : (at + 1) * own]

    gain_sums = self_sums[:, 4 * own : 4 * own + 4].T
    return (
        block_output,
        token_losses,
        hidden_grad,
        encoder_grad,
        gain_sums[0],
        piece(self_sums, 0),
        piece(self_sums, 1),
        piece(self_sums, 2),
        piece(self_sums, 3),
        gain_sums[1],
        piece(cross_sums, 0),
        piece(cross_sums, 1),
        piece(cross_sums, 2),
        piece(cross_sums, 3),
        gain_sums[2],
        feed_sums[:, :own_feed],
        feed_sums[:, own_feed:],
        down_grad,
        gain_sums[3],
        embedding_grad,
    )


def solution(mesh):
    tokens = P("dp", "seq")
    rows = P("dp")
    matrix = P("dp", "seq")
    block = P("dp", "seq", None)
    attention = (rows,) + (matrix,) * 4
    return jax.shard_map(
        per_device,
        mesh=mesh,
        in_specs=(block, block, rows, tokens, tokens, block)
        + attention * 2
        + (rows, matrix, matrix, matrix, rows, matrix),
        out_specs=(block, tokens, block, block)
        + attention * 2
        + (rows, matrix, matrix, matrix, rows, matrix),
        check_vma=False,
    )
```

time: 3680 us -> 1210 us (0.33)
  waiting for transfers between devices: 2970 us -> 762 us
  matrix products: 358 us -> 135 us
  blocking collectives: 172 us -> 76.7 us
  Pallas kernels: 0 us -> 56.4 us
  local copies, waits for them, and re-layouts: 111 us -> 69.1 us
  starting transfers between devices: 2.13 us -> 41.9 us
    all_gather x17 -> x6, waiting for transfers between devices: 1250 us -> 285 us  [the longest x1 92.7 us: per_device(): table = lax.all_gather(embedding.T, 'seq', axis=0, tiled=True)]
    reduce_scatter x19 -> x6, waiting for transfers between devices: 1260 us -> 359 us  [the longest x4 313 us: scatter(): lax.psum_scatter(full.reshape(-1, full.shape[-1]).astype(low), both, scat...]
    unnamed x54 -> x12, waiting for transfers between devices: 464 us -> 1.38 us
    dot_general x48 -> x24, matrix products: 358 us -> 135 us  [the longest x3 69.5 us: contract(): lax.dot_general(first_op, second_op, (((first_dim,), (second_dim,)), ((),...]
    all_to_all x0 -> x7, waiting for transfers between devices: none -> 118 us  [swap(): return lax.all_to_all(pieces, 'seq', 0, 0, tiled=True)]
    all_gather x11 -> x2, blocking collectives: 123 us -> 18.5 us  [the longest x1 9.66 us: per_device(): lax.all_gather(jnp.stack([row_max[:, 0], row_sum[:, 0], picked[:, 0]]), '...]
    unnamed x156 -> x111, local copies, waits for them, and re-layouts: 79 us -> 14.6 us
    all_to_all x0 -> x3, blocking collectives: none -> 58.2 us  [swap(): return lax.all_to_all(pieces, 'seq', 0, 0, tiled=True)]
  transfers between devices with their start and end apart: 45 -> 19, of which waited for: 39 -> 15; matrix products, arithmetic and copies ran while one was open for 11% -> 14% of each run, Pallas kernels for 0% -> 5%
where the time goes in v1:
time: 1210 us; the launch traced here: 1200 us
  waiting for transfers between devices  762 us (63%)
  matrix products  135 us (11%)
  blocking collectives  76.7 us (6%)
  local copies, waits for them, and re-layouts  69.1 us (6%)
  Pallas kernels  56.4 us (5%)
  other arithmetic  42.6 us (4%)
  starting transfers between devices  41.9 us (3%)
  between operations  15.9 us (1%)
    reduce_scatter x4, waiting for transfers between devices, scatter(): lax.psum_scatter(full.reshape(-1, full.shape[-1]).astype(low), both, scat...  313 us
    all_to_all x7, waiting for transfers between devices, swap(): return lax.all_to_all(pieces, 'seq', 0, 0, tiled=True)  118 us
    all_gather x1, waiting for transfers between devices, per_device(): table = lax.all_gather(embedding.T, 'seq', axis=0, tiled=True)  92.7 us
    dot_general x3, matrix products, contract(): lax.dot_general(first_op, second_op, (((first_dim,), (second_dim,)), ((),...  69.5 us
    dot_general x21, matrix products, mix(): jnp.einsum(spec, first_op, second_op, preferred_element_type=jnp.float32)  65.3 us
    all_gather x1, waiting for transfers between devices, per_device(): lax.all_gather(self_pack, both, axis=0, tiled=True)  64.4 us
    all_gather x1, waiting for transfers between devices, per_device(): lax.all_gather(feed_pack, both, axis=0, tiled=True)  63.3 us
    all_to_all x3, blocking collectives, swap(): return lax.all_to_all(pieces, 'seq', 0, 0, tiled=True)  58.2 us
  transfers between devices with their start and end apart: 19, of which 15 were waited for; matrix products, arithmetic and copies ran while one was open for 14% of the time, Pallas kernels for 5%

profile of v1, /device:TPU:8, one launch (start us, length us, event | category | flops | bytes accessed | tf_op | source)
XLA Modules:
  0.0 1199.9 jit_solution(14463890722966521438)
XLA Ops:
  14.8 64.4 %all-gather.11.cloned.1.call-done = bf16[3072,896]{1,0:T(8,128)(2,1)} async-done(((bf16[96,896]{1,0:T(8,128)(2,1)}), bf16[3072,896]{1,0:T(8,128)(2,1)}) %all-gather.11.cloned.1.call-update) | async-done | bytes 5505040 | tf_op jit(solution)/shard_map/all_gather | solution.py:210
  81.0 4.5 fusion.21
  85.5 3.8 all-to-all-start
  89.9 28.5 %all-to-all-done = bf16[4,256,576]{1,2,0:T(8,128)(2,1)S(1)} async-done(((bf16[4,256,576]{1,2,0:T(8,128)(2,1)}), bf16[4,256,576]{1,2,0:T(8,128)(2,1)S(1)}, u32[]{:S(2)}, u32[]{:S(2)}) %all-to-all-start) | async-done | bytes 1179680 | tf_op jit(solution)/shard_map/all_to_all | solution.py:48
  119.8 10.0 shard_map.365
  131.8 6.8 all-to-all-start.1
  138.6 24.2 %all-gather.13.cloned.1.call-done = bf16[3072,768]{1,0:T(8,128)(2,1)} async-done(((bf16[96,768]{1,0:T(8,128)(2,1)}), bf16[3072,768]{1,0:T(8,128)(2,1)}) %all-gather.13.cloned.1.call-update) | async-done | bytes 4718608 | tf_op jit(solution)/shard_map/all_gather | solution.py:212
  162.7 4.3 fusion.39
  167.0 5.2 all-to-all-start.3
  181.3 10.6 all-to-all-done.3
  191.9 6.8 all-to-all-start.2
  201.0 9.3 all-to-all-done.2
  211.3 8.8 shard_map.366
  222.1 6.5 all-to-all-start.4
  228.9 4.5 all-gather.17.cloned.1.call-done
  233.3 3.9 copy.157
  242.9 63.3 %all-gather.15.cloned.1.call-done = bf16[3072,1024]{1,0:T(8,128)(2,1)} async-done(((bf16[96,1024]{1,0:T(8,128)(2,1)}), bf16[3072,1024]{1,0:T(8,128)(2,1)}) %all-gather.15.cloned.1.call-update) | async-done | bytes 6291472 | tf_op jit(solution)/shard_map/all_gather | solution.py:214
  306.2 4.8 convolution_bitcast_fusion
  316.9 8.9 all-gather.2
  325.8 92.7 %all-gather.21.cloned.1.call-done = bf16[768,4016]{1,0:T(8,128)(2,1)} async-done(((bf16[192,4016]{1,0:T(8,128)(2,1)}), bf16[768,4016]{1,0:T(8,128)(2,1)}) %all-gather.21.cloned.1.call-update) | async-done | bytes 6168592 | tf_op jit(solution)/shard_map/all_gather | solution.py:218
  418.5 35.7 %all-gather.19.cloned.1.call-done = bf16[2048,768]{1,0:T(8,128)(2,1)} async-done(((bf16[256,768]{1,0:T(8,128)(2,1)}), bf16[2048,768]{1,0:T(8,128)(2,1)}) %all-gather.19.cloned.1.call-update) | async-done | bytes 3145744 | tf_op jit(solution)/shard_map/all_gather | solution.py:260
  454.2 22.1 %fusion.111 = (f32[2048]{0:T(1024)S(1)}, f32[2048,4016]{0,1:T(8,128)}) fusion(bf16[2048,768]{1,0:T(8,128)(2,1)} %all-gather.19.cloned.1.call-done, bf16[768,4016]{1,0:T(8,128)(2,1)} %all-gather.21.cloned.1.call-done), kind=kOutput, calls=%fused_computation.170 | convolution fusion | flops 12641466368 | bytes 42221568 | tf_op jit(solution)/shard_map/dot_general | solution.py:20
  476.2 15.2 %exponential_reduce_fusion = (f32[2048]{0:T(1024)S(1)}, f32[2048]{0:T(1024)S(1)}) fusion(f32[2048,4016]{0,1:T(8,128)} %get-tuple-element.74, f32[2048]{0:T(1024)S(1)} %get-tuple-element.73, s32[2048]{0:T(1024)S(1)} %bitcast.277), kind=kLoop, calls=%fused_computation.3 | loop fusion | flops 41119744 | bytes 32931840 | tf_op jit(solution)/shard_map/reduce_sum | solution.py:265
  491.4 9.7 all-gather.3
  502.0 25.3 %convolution_convert_fusion.2 = bf16[2048,768]{1,0:T(8,128)(2,1)} fusion(bf16[768,4016]{1,0:T(8,128)(2,1)S(1)} %copy-done.52, f32[2048,4016]{0,1:T(8,128)} %get-tuple-element.74, f32[2048]{0:T(1024)S(1)} %log_add_fusion, f32[2048]{0:T(1024)S(1)} %bitcast.280, s32[2048]{0:T(1024)S(1)} %bitcast.278), kind=kOutput, calls=%fused_computation.13 | convolution fusion | flops 12684165120 | bytes 42237952 | tf_op jit(solution)/shard_map/dot_general | solution.py:20
  527.3 46.2 %reduce-scatter.7.cloned.1.call-done = bf16[256,768]{1,0:T(8,128)(2,1)} async-done(((bf16[2048,768]{1,0:T(8,128)(2,1)}), bf16[256,768]{1,0:T(8,128)(2,1)}) %reduce-scatter.7.cloned.1.call-update) | async-done | bytes 393232 | tf_op jit(solution)/shard_map/reduce_scatter | solution.py:278
  580.1 22.2 %convolution_convert_fusion = bf16[768,4016]{1,0:T(8,128)(2,1)} fusion(bf16[2048,768]{1,0:T(8,128)(2,1)} %all-gather.19.cloned.1.call-done, f32[2048,4016]{0,1:T(8,128)} %get-tuple-element.74, f32[2048]{0:T(1024)S(1)} %log_add_fusion, f32[2048]{0:T(1024)S(1)} %bitcast.281, s32[2048]{0:T(1024)S(1)} %bitcast.279), kind=kOutput, calls=%fused_computation.4 | convolution fusion | flops 12685676544 | bytes 42237952 | tf_op jit(solution)/shard_map/dot_general | solution.py:20
  607.6 6.3 dot_general.104
  614.0 7.9 fusion.12
  622.0 6.1 multiply_reduce_fusion
  632.5 18.2 %all_to_all.50 = bf16[4,256,192]{1,2,0:T(8,128)(2,1)S(1)} all-to-all(bf16[4,256,192]{1,2,0:T(8,128)(2,1)S(1)} %bitcast.254), channel_id=1, replica_groups=mesh['dp'=8,'seq'=4] {'seq'}, dimensions={0} | all-to-all | bytes 786432 | tf_op jit(solution)/shard_map/all_to_all | solution.py:48
  651.7 18.4 %shard_map.367 = (bf16[1024,192]{1,0:T(8,128)(2,1)}, bf16[1024,384]{1,0:T(8,128)(2,1)}) custom-call(s32[1]{0:T(128)S(6)} %copy.225.prefix_ref, bf16[1024,192]{1,0:T(8,128)(2,1)} %bitcast.239, bf16[1024,384]{1,0:T(8,128)(2,1)} %bitcast.232, bf16[1024,192]{1,0:T(8,128)(2,1)} %bitcast.247), custom_call_target="tpu_custom_call" | custom-call | tf_op jit(solution)/shard_map/pallas_call | solution.py:160
  671.3 15.5 %all_to_all.51 = bf16[4,256,192]{1,2,0:T(8,128)(2,1)S(1)} all-to-all(bf16[4,256,192]{1,2,0:T(8,128)(2,1)S(1)} %copy.168), channel_id=1, replica_groups=mesh['dp'=8,'seq'=4] {'seq'}, dimensions={0} | all-to-all | bytes 786432 | tf_op jit(solution)/shard_map/all_to_all | solution.py:48
  686.9 6.0 all-to-all-start.9
  694.9 36.6 %all-to-all-done.9 = bf16[4,256,384]{2,1,0:T(8,128)(2,1)} async-done(((bf16[4,256,384]{2,1,0:T(8,128)(2,1)}), bf16[4,256,384]{2,1,0:T(8,128)(2,1)}, u32[]{:S(2)}, u32[]{:S(2)}) %all-to-all-start.9) | async-done | bytes 786464 | tf_op jit(solution)/shard_map/all_to_all | solution.py:48
  735.9 6.6 copy.178
  743.8 5.8 convolution_convert_fusion.1
  756.9 24.4 %all_to_all.52 = bf16[4,256,192]{1,2,0:T(8,128)(2,1)S(1)} all-to-all(bf16[4,256,192]{1,2,0:T(8,128)(2,1)S(1)} %bitcast.255), channel_id=1, replica_groups=mesh['dp'=8,'seq'=4] {'seq'}, dimensions={0} | all-to-all | bytes 786432 | tf_op jit(solution)/shard_map/all_to_all | solution.py:48
  782.4 19.2 %shard_map.368 = bf16[1024,576]{1,0:T(8,128)(2,1)} custom-call(s32[1]{0:T(128)S(6)} %copy.225.prefix_ref, bf16[1024,576]{1,0:T(8,128)(2,1)} %bitcast.230, bf16[1024,192]{1,0:T(8,128)(2,1)} %bitcast.248), custom_call_target="tpu_custom_call" | custom-call | tf_op jit(solution)/shard_map/pallas_call | solution.py:160
  804.0 6.1 all-to-all-start.8
  811.7 32.6 %all-to-all-done.8 = bf16[4,256,576]{1,2,0:T(8,128)(2,1)S(1)} async-done(((bf16[4,256,576]{1,2,0:T(8,128)(2,1)}), bf16[4,256,576]{1,2,0:T(8,128)(2,1)S(1)}, u32[]{:S(2)}, u32[]{:S(2)}) %all-to-all-start.8) | async-done | bytes 1179680 | tf_op jit(solution)/shard_map/all_to_all | solution.py:48
  844.3 4.3 fusion.62
  852.9 8.5 copy.175
  863.0 4.1 fusion.36
  869.9 3.5 convert_bitcast_fusion.1
  873.3 81.3 %reduce-scatter.11.cloned.1.call-done = bf16[96,768]{1,0:T(8,128)(2,1)} async-done(((bf16[3072,768]{1,0:T(8,128)(2,1)}), bf16[96,768]{1,0:T(8,128)(2,1)}) %reduce-scatter.11.cloned.1.call-update) | async-done | bytes 147472 | tf_op jit(solution)/shard_map/reduce_scatter | solution.py:286
  956.4 118.0 %reduce-scatter.13.cloned.1.call-done = bf16[96,1024]{1,0:T(8,128)(2,1)} async-done(((bf16[3072,1024]{1,0:T(8,128)(2,1)}), bf16[96,1024]{1,0:T(8,128)(2,1)}) %reduce-scatter.13.cloned.1.call-update) | async-done | bytes 196624 | tf_op jit(solution)/shard_map/reduce_scatter | solution.py:286
  1076.1 113.3 %reduce-scatter.9.cloned.1.call-done = bf16[96,896]{1,0:T(8,128)(2,1)} async-done(((bf16[3072,896]{1,0:T(8,128)(2,1)}), bf16[96,896]{1,0:T(8,128)(2,1)}) %reduce-scatter.9.cloned.1.call-update) | async-done | bytes 172048 | tf_op jit(solution)/shard_map/reduce_scatter | solution.py:286
  (213 shorter events, 93.5 us)
Async XLA Ops:
  7.2 155.5 %copy-start = (bf16[1,256,768]{2,1,0:T(8,128)(2,1)S(1)}, bf16[1,256,768]{2,1,0:T(8,128)(2,1)}, u32[]{:S(2)}) copy-start(bf16[1,256,768]{2,1,0:T(8,128)(2,1)} %param.23) | copy-start | bytes 1179652
  7.2 7.4 copy-start.9
  7.2 72.0 %all-gather.11.cloned.1.call-start = ((), (), s32[]{:S(2)}) async-start(), calls=%async_computation.16 | async-start | bytes 5677056 | tf_op jit(solution)/shard_map/all_gather | solution.py:210
  9.9 152.8 %all-gather.13.cloned.1.call-start = ((), (), s32[]{:S(2)}) async-start(), calls=%async_computation.17 | async-start | bytes 4866048 | tf_op jit(solution)/shard_map/all_gather | solution.py:212
  11.6 221.7 %all-gather.17.cloned.1.call-start = ((), (), s32[]{:S(2)}) async-start(), calls=%async_computation.19 | async-start | bytes 3244032 | tf_op jit(solution)/shard_map/all_gather | solution.py:215
  12.3 293.8 %all-gather.15.cloned.1.call-start = ((), (), s32[]{:S(2)}) async-start(), calls=%async_computation.18 | async-start | bytes 6488064 | tf_op jit(solution)/shard_map/all_gather | solution.py:214
  14.1 404.5 %all-gather.21.cloned.1.call-start = ((), (), s32[]{:S(2)}) async-start(), calls=%async_computation.21 | async-start | bytes 7864320 | tf_op jit(solution)/shard_map/all_gather | solution.py:218
  14.8 70.6 %copy-start.42 = (f32[256]{0:T(256)}, f32[256]{0:T(256)S(1)}, u32[]{:S(2)}) copy-start(f32[256]{0:T(256)S(1)} %fusion.70) | copy-start | bytes 3076
  14.8 70.6 %copy-start.40 = (f32[256]{0:T(256)}, f32[256]{0:T(256)S(1)}, u32[]{:S(2)}) copy-start(f32[256]{0:T(256)S(1)} %fusion.94) | copy-start | bytes 3076
  85.5 32.9 %all-to-all-start = ((bf16[4,256,576]{1,2,0:T(8,128)(2,1)}), bf16[4,256,576]{1,2,0:T(8,128)(2,1)S(1)}, u32[]{:S(2)}, u32[]{:S(2)}) async-start(bf16[4,256,576]{1,2,0:T(8,128)(2,1)} %fusion.21), calls=%async_computation | async-start | bytes 2359296 | tf_op jit(solution)/shard_map/all_to_all | solution.py:48
  131.8 35.2 %all-to-all-start.1 = ((bf16[4,256,192]{1,2,0:T(8,128)(2,1)}), bf16[4,256,192]{1,2,0:T(8,128)(2,1)S(1)}, u32[]{:S(2)}, u32[]{:S(2)}) async-start(bf16[4,256,192]{1,2,0:T(8,128)(2,1)} %copy.148), calls=%async_computation.1 | async-start | bytes 786432 | tf_op jit(solution)/shard_map/all_to_all | solution.py:48
  167.0 9.2 copy-start.12
  167.0 24.9 %all-to-all-start.3 = ((bf16[4,256,384]{1,2,0:T(8,128)(2,1)}), bf16[4,256,384]{1,2,0:T(8,128)(2,1)}, u32[]{:S(2)}, u32[]{:S(2)}) async-start(bf16[4,256,384]{1,2,0:T(8,128)(2,1)} %fusion.39), calls=%async_computation.3 | async-start | bytes 1572864 | tf_op jit(solution)/shard_map/all_to_all | solution.py:48
  178.1 33.3 %copy-start.36 = (f32[256]{0:T(256)}, f32[256]{0:T(256)S(1)}, u32[]{:S(2)}) copy-start(f32[256]{0:T(256)S(1)} %get-tuple-element.67) | copy-start | bytes 3076
  178.1 62.7 %copy-start.5 = (f32[256,768]{1,0:T(8,128)}, f32[256,768]{1,0:T(8,128)S(1)}, u32[]{:S(2)}) copy-start(f32[256,768]{1,0:T(8,128)S(1)} %get-tuple-element.68) | copy-start | bytes 2359300
  178.1 13.8 %copy-start.46 = (f32[256]{0:T(256)}, f32[256]{0:T(256)S(1)}, u32[]{:S(2)}) copy-start(f32[256]{0:T(256)S(1)} %fusion.95) | copy-start | bytes 3076
  191.9 18.4 %all-to-all-start.2 = ((bf16[4,256,192]{1,2,0:T(8,128)(2,1)}), bf16[4,256,192]{1,2,0:T(8,128)(2,1)S(1)}, u32[]{:S(2)}, u32[]{:S(2)}) async-start(bf16[4,256,192]{1,2,0:T(8,128)(2,1)} %fusion.54), calls=%async_computation.2 | async-start | bytes 786432 | tf_op jit(solution)/shard_map/all_to_all | solution.py:48
  222.1 18.6 %all-to-all-start.4 = ((bf16[4,256,192]{1,2,0:T(8,128)(2,1)}), bf16[4,256,192]{1,2,0:T(8,128)(2,1)S(1)}, u32[]{:S(2)}, u32[]{:S(2)}) async-start(bf16[4,256,192]{1,2,0:T(8,128)(2,1)} %copy.154), calls=%async_computation.4 | async-start | bytes 786432 | tf_op jit(solution)/shard_map/all_to_all | solution.py:48
  228.7 225.5 %all-gather.19.cloned.1.call-start = ((), (), s32[]{:S(2)}) async-start(), calls=%async_computation.20 | async-start | bytes 3538944 | tf_op jit(solution)/shard_map/all_gather | solution.py:260
  240.8 65.4 %copy-start.15 = (bf16[4,256,192]{1,2,0:T(8,128)(2,1)}, bf16[4,256,192]{1,2,0:T(8,128)(2,1)S(1)}, u32[]{:S(2)}) copy-start(bf16[4,256,192]{1,2,0:T(8,128)(2,1)S(1)} %all-to-all-done.4) | copy-start | bytes 1179652
  242.8 68.2 %copy-start.44 = (f32[256]{0:T(256)}, f32[256]{0:T(256)S(1)}, u32[]{:S(2)}) copy-start(f32[256]{0:T(256)S(1)} %get-tuple-element.69) | copy-start | bytes 3076
  242.8 69.0 %copy-start.7 = (f32[256,768]{1,0:T(8,128)}, f32[256,768]{1,0:T(8,128)S(1)}, u32[]{:S(2)}) copy-start(f32[256,768]{1,0:T(8,128)S(1)} %get-tuple-element.70) | copy-start | bytes 2359300
  242.8 68.2 %copy-start.31 = (f32[256]{0:T(256)}, f32[256]{0:T(256)S(1)}, u32[]{:S(2)}) copy-start(f32[256]{0:T(256)S(1)} %fusion.96) | copy-start | bytes 3076
  315.8 259.6 %copy-start.3 = (f32[256,768]{1,0:T(8,128)}, f32[256,768]{1,0:T(8,128)S(1)}, u32[]{:S(2)}) copy-start(f32[256,768]{1,0:T(8,128)S(1)} %get-tuple-element.72) | copy-start | bytes 2359300
  316.8 256.7 %reduce-scatter.7.cloned.1.call-start = ((), (), s32[]{:S(2)}) async-start(), calls=%async_computation.22 | async-start | bytes 3538944 | tf_op jit(solution)/shard_map/reduce_scatter | solution.py:278
  325.8 254.3 %copy-start.35 = (f32[8,1,256]{2,1,0:T(1,128)}, f32[8,1,256]{2,1,0:T(1,128)S(1)}, u32[]{:S(2)}) copy-start(f32[8,1,256]{2,1,0:T(1,128)S(1)} %get-tuple-element.66) | copy-start | bytes 24580
  476.2 25.7 %copy-start.52 = (bf16[768,4016]{1,0:T(8,128)(2,1)S(1)}, bf16[768,4016]{1,0:T(8,128)(2,1)}, u32[]{:S(2)}) copy-start(bf16[768,4016]{1,0:T(8,128)(2,1)} %all-gather.21.cloned.1.call-done) | copy-start | bytes 18505732
  502.0 78.1 %copy-start.34 = (f32[2048]{0:T(1024)}, f32[2048]{0:T(1024)S(1)}, u32[]{:S(2)}) copy-start(f32[2048]{0:T(1024)S(1)} %log_add_fusion) | copy-start | bytes 24580
  527.3 48.1 %copy-start.18 = (f32[1,256,768]{2,1,0:T(8,128)S(1)}, f32[1,256,768]{2,1,0:T(8,128)}, u32[]{:S(2)}) copy-start(f32[1,256,768]{2,1,0:T(8,128)} %param.27) | copy-start | bytes 2359300
  527.3 341.0 %reduce-scatter.15.cloned.1.call-start = ((), (), s32[]{:S(2)}) async-start(), calls=%async_computation.26 | async-start | bytes 3244032 | tf_op jit(solution)/shard_map/reduce_scatter | solution.py:286
  579.8 290.1 %reduce-scatter.17.cloned.1.call-start = ((), (), s32[]{:S(2)}) async-start(), calls=%async_computation.27 | async-start | bytes 7864320 | tf_op jit(solution)/shard_map/reduce_scatter | solution.py:281
  607.6 6.3 copy-start.23
  613.9 7.9 copy-start.8
  613.9 7.9 copy-start.32
  650.7 42.1 %copy-start.16 = (bf16[4,256,192]{1,2,0:T(8,128)(2,1)S(1)}, bf16[4,256,192]{1,2,0:T(8,128)(2,1)}, u32[]{:S(2)}) copy-start(bf16[4,256,192]{1,2,0:T(8,128)(2,1)} %copy-done.15) | copy-start | bytes 1179652
  651.7 42.6 %copy-start.6 = (f32[256,768]{1,0:T(8,128)S(1)}, f32[256,768]{1,0:T(8,128)}, u32[]{:S(2)}) copy-start(f32[256,768]{1,0:T(8,128)} %copy-done.5) | copy-start | bytes 2359300
  651.7 42.6 %copy-start.47 = (f32[256]{0:T(256)S(1)}, f32[256]{0:T(256)}, u32[]{:S(2)}) copy-start(f32[256]{0:T(256)} %copy-done.46) | copy-start | bytes 3076
  686.9 44.6 %all-to-all-start.9 = ((bf16[4,256,384]{2,1,0:T(8,128)(2,1)}), bf16[4,256,384]{2,1,0:T(8,128)(2,1)}, u32[]{:S(2)}, u32[]{:S(2)}) async-start(bf16[4,256,384]{2,1,0:T(8,128)(2,1)} %bitcast.260), calls=%async_computation.10 | async-start | bytes 1572864 | tf_op jit(solution)/shard_map/all_to_all | solution.py:48
  692.8 261.8 %reduce-scatter.11.cloned.1.call-start = ((), (), s32[]{:S(2)}) async-start(), calls=%async_computation.24 | async-start | bytes 4866048 | tf_op jit(solution)/shard_map/reduce_scatter | solution.py:286
  742.5 331.9 %reduce-scatter.13.cloned.1.call-start = ((), (), s32[]{:S(2)}) async-start(), calls=%async_computation.25 | async-start | bytes 6488064 | tf_op jit(solution)/shard_map/reduce_scatter | solution.py:286
  801.5 8.6 copy-start.48
  801.5 8.6 copy-start.49
  801.5 8.7 copy-start.13
  801.5 42.8 %copy-start.10 = (bf16[1,256,768]{2,1,0:T(8,128)(2,1)S(1)}, bf16[1,256,768]{2,1,0:T(8,128)(2,1)}, u32[]{:S(2)}) copy-start(bf16[1,256,768]{2,1,0:T(8,128)(2,1)} %param.22) | copy-start | bytes 1179652
  801.5 42.8 %copy-start.30 = (f32[768]{0:T(1024)S(1)}, f32[768]{0:T(1024)}, u32[]{:S(2)}) copy-start(f32[768]{0:T(1024)} %copy-done.29) | copy-start | bytes 9220
  804.0 40.3 %all-to-all-start.8 = ((bf16[4,256,576]{1,2,0:T(8,128)(2,1)}), bf16[4,256,576]{1,2,0:T(8,128)(2,1)S(1)}, u32[]{:S(2)}, u32[]{:S(2)}) async-start(bf16[4,256,576]{1,2,0:T(8,128)(2,1)} %copy.172), calls=%async_computation.9 | async-start | bytes 2359296 | tf_op jit(solution)/shard_map/all_to_all | solution.py:48
  810.1 379.4 %reduce-scatter.9.cloned.1.call-start = ((), (), s32[]{:S(2)}) async-start(), calls=%async_computation.23 | async-start | bytes 5677056 | tf_op jit(solution)/shard_map/reduce_scatter | solution.py:286
  811.7 37.0 %copy-start.41 = (f32[256]{0:T(256)S(1)}, f32[256]{0:T(256)}, u32[]{:S(2)}) copy-start(f32[256]{0:T(256)} %copy-done.40) | copy-start | bytes 3076
  (24 other events, 95.2 us)
Sparse Core Ops, SparseCore 0:
  11.5 67.6 all-gather.10
  82.7 80.0 all-gather.12
  165.6 67.6 all-gather.16
  236.6 69.5 all-gather.14
  307.6 110.8 all-gather.20
  420.8 33.3 all-gather.18
  527.4 46.0 reduce-scatter.6
  579.9 104.6 reduce-scatter.14
  686.9 156.7 reduce-scatter.16
  849.1 105.4 reduce-scatter.10
  960.3 114.0 reduce-scatter.12
  1079.8 109.6 reduce-scatter.8

commit v2 on v1

--- a/solution.py
+++ b/solution.py
@@ -13,7 +13,6 @@
 
 norm_eps = 1e-06
 masked_score = -1000000000.0
-both = ("seq", "dp")
 
 
 def contract(first_op, second_op, first_dim, second_dim):
@@ -25,10 +24,6 @@
     )
 
 
-def mix(spec, first_op, second_op):
-    return jnp.einsum(spec, first_op, second_op, preferred_element_type=jnp.float32)
-
-
 def norm_rows(inputs, scaling):
     return (
         inputs * lax.rsqrt(jnp.mean(inputs * inputs, axis=-1, keepdims=True) + norm_eps) * scaling
@@ -46,6 +41,25 @@
 
 def swap(pieces):
     return lax.all_to_all(pieces, "seq", 0, 0, tiled=True)
+
+
+def spread(shard):
+    return swap(jnp.broadcast_to(shard[None], (lax.axis_size("seq"),) + shard.shape))
+
+
+def stacked(matrix, count):
+    rows, columns = matrix.shape
+    return matrix.astype(jnp.bfloat16).reshape(rows, count, columns // count).transpose(1, 0, 2)
+
+
+def side_by_side(pieces):
+    count, rows, columns = pieces.shape
+    return pieces.transpose(1, 0, 2).reshape(rows, count * columns)
+
+
+def cut(array, sizes, axis):
+    edges = [sum(sizes[:at]) for at in range(1, len(sizes))]
+    return jnp.split(array, edges, axis=axis)
 
 
 def head_lanes(width, head):
@@ -206,54 +220,76 @@
 
     gains = jnp.stack([self_gain, cross_gain, feed_gain, exit_gain], axis=1)
     gains = jnp.pad(gains, ((0, 0), (0, GAIN_LANES - gains.shape[1])))
-    self_pack = jnp.concatenate([self_query, self_key, self_value, self_output, gains], axis=1)
-    self_full = lax.all_gather(self_pack, both, axis=0, tiled=True).reshape(n_seq, width, -1)
-    cross_pack = jnp.concatenate([cross_query, cross_key, cross_value, cross_output], axis=1)
-    cross_full = lax.all_gather(cross_pack, both, axis=0, tiled=True).reshape(n_seq, width, -1)
-    feed_pack = jnp.concatenate([feed_gate, feed_up], axis=1)
-    feed_full = lax.all_gather(feed_pack, both, axis=0, tiled=True).reshape(n_seq, width, -1)
-    down_full = lax.all_gather(feed_down.T, both, axis=0, tiled=True).reshape(
-        n_seq, n_dp, own, feed_down.shape[0]
+    down_folds = -(-feed_down.shape[0] // own_rows)
+    down_pad = down_folds * own_rows - feed_down.shape[0]
+    self_parts = spread(
+        jnp.concatenate([self_query, self_key, self_value, self_output], axis=1)
+    )
+    self_full = lax.all_gather(
+        jnp.concatenate(
+            [
+                side_by_side(self_parts[:, :, : 3 * own]),
+                side_by_side(self_parts[:, :, 3 * own :]),
+                gains,
+            ],
+            axis=1,
+        ),
+        "dp",
+        axis=0,
+        tiled=True,
+    )
+    rest_sizes = (own, 2 * own, own, own_feed, own_feed) + (own,) * down_folds
+    rest_parts = spread(
+        jnp.concatenate(
+            [cross_query, cross_key, cross_value, cross_output, feed_gate, feed_up]
+            + list(
+                jnp.pad(feed_down, ((0, down_pad), (0, 0))).reshape(down_folds, own_rows, own)
+            ),
+            axis=1,
+        )
+    )
+    rest_full = lax.all_gather(
+        jnp.concatenate(
+            [side_by_side(part) for part in cut(rest_parts, rest_sizes, 2)], axis=1
+        ),
+        "dp",
+        axis=0,
+        tiled=True,
     )
     table = lax.all_gather(embedding.T, "seq", axis=0, tiled=True)
     marks = lax.all_gather(jnp.concatenate([exit_flags, target_ids], axis=0), "dp", axis=0)
 
-    self_qkv, self_out = self_full[:, :, : 3 * own], self_full[:, :, 3 * own : 4 * own]
-    cross_q, cross_kv = cross_full[:, :, :own], cross_full[:, :, own : 3 * own]
-    cross_out = cross_full[:, :, 3 * own :]
-    gain_rows = self_full[0, :, 4 * own : 4 * own + 4].astype(jnp.float32).T
+    full_sizes = tuple(n_seq * size for size in rest_sizes)
+    self_qkv, self_out = self_full[:, : 3 * width], self_full[:, 3 * width : 4 * width]
+    cross_q, cross_kv, cross_out, gate_full, up_full, *down_parts = cut(rest_full, full_sizes, 1)
+    down_full = jnp.stack(
+        [part.reshape(n_dp, own_rows, width) for part in down_parts], axis=1
+    ).reshape(n_dp, -1, width)[:, : feed_down.shape[0]]
+    down_full = down_full.reshape(-1, width)
+    gain_rows = self_full[:, 4 * width : 4 * width + 4].astype(jnp.float32).T
     gain_one, gain_two, gain_three, gain_exit = gain_rows
 
     residual_in = hidden_in.astype(jnp.float32).reshape(-1, width)
     token_count = residual_in.shape[0]
     normed_one = norm_rows(residual_in, gain_one).astype(low)
-    qkv_one = swap(mix("td,zdn->ztn", normed_one, self_qkv).astype(low)).reshape(-1, 3 * own)
+    qkv_one = swap(stacked(contract(normed_one, self_qkv, 1, 0), n_seq)).reshape(-1, 3 * own)
     self_places = ((0, 0), (0, own), (0, 2 * own))
     mixture_one = attend(prefix_len, [qkv_one], self_places, own, True)
-    mixture_one = swap(mixture_one.reshape(n_seq, token_count, own))
-    mixture_one = mixture_one.transpose(1, 0, 2).reshape(token_count, width)
-    after_self = residual_in + mix("td,zdn->tzn", mixture_one, self_out).reshape(
-        token_count, width
-    )
+    mixture_one = side_by_side(swap(mixture_one.reshape(n_seq, token_count, own)))
+    after_self = residual_in + contract(mixture_one, self_out, 1, 0)
     normed_two = norm_rows(after_self, gain_two).astype(low)
     states = encoder_in.reshape(-1, width)
-    kv_two = swap(mix("td,zdn->ztn", states, cross_kv).astype(low)).reshape(-1, 2 * own)
-    q_two = swap(mix("td,zdn->ztn", normed_two, cross_q).astype(low)).reshape(-1, own)
+    kv_two = swap(stacked(contract(states, cross_kv, 1, 0), n_seq)).reshape(-1, 2 * own)
+    q_two = swap(stacked(contract(normed_two, cross_q, 1, 0), n_seq)).reshape(-1, own)
     cross_places = ((0, 0), (1, 0), (1, own))
     mixture_two = attend(prefix_len, [q_two, kv_two], cross_places, own, False)
-    mixture_two = swap(mixture_two.reshape(n_seq, token_count, own))
-    mixture_two = mixture_two.transpose(1, 0, 2).reshape(token_count, width)
-    after_cross = after_self + mix("td,zdn->tzn", mixture_two, cross_out).reshape(
-        token_count, width
-    )
+    mixture_two = side_by_side(swap(mixture_two.reshape(n_seq, token_count, own)))
+    after_cross = after_self + contract(mixture_two, cross_out, 1, 0)
     normed_three = norm_rows(after_cross, gain_three).astype(low)
-    gate_up = mix("td,zdn->ztn", normed_three, feed_full)
-    gate_pre, up_pre = gate_up[:, :, :own_feed], gate_up[:, :, own_feed:]
+    gate_pre = contract(normed_three, gate_full, 1, 0)
+    up_pre = contract(normed_three, up_full, 1, 0)
     hidden_mid = gated_unit(gate_pre, up_pre).astype(low)
-    hidden_rows = hidden_mid.transpose(1, 0, 2).reshape(token_count, n_dp, -1)
-    after_feed = after_cross + mix("tkr,zknr->tzn", hidden_rows, down_full).reshape(
-        token_count, width
-    )
+    after_feed = after_cross + contract(hidden_mid, down_full, 1, 0)
     block_output = after_feed.astype(low).reshape(hidden_in.shape)
     normed_exit = norm_rows(after_feed, gain_exit).astype(low)
 
@@ -277,37 +313,25 @@
     ).astype(low)
     exit_in_grad = lax.psum_scatter(
         contract(logit_grads, table, 1, 1).astype(low), "dp", scatter_dimension=0, tiled=True
-    ).astype(jnp.float32)
-    embedding_grad = lax.psum_scatter(
-        contract(tokens, logit_grads, 0, 0).astype(low), "seq", scatter_dimension=0, tiled=True
-    ).astype(jnp.float32).T
-
-    def scatter(full):
-        return lax.psum_scatter(
-            full.reshape(-1, full.shape[-1]).astype(low), both, scatter_dimension=0, tiled=True
-        ).astype(jnp.float32)
+    )
+    table_terms = contract(tokens, logit_grads, 0, 0).astype(low)
+    exit_in_grad, table_terms = lax.optimization_barrier((exit_in_grad, table_terms))
+    exit_in_grad = exit_in_grad.astype(jnp.float32)
+    embedding_grad = lax.psum_scatter(table_terms, "seq", scatter_dimension=0, tiled=True)
+    embedding_grad = embedding_grad.astype(jnp.float32).T
 
     feed_grad, full_exit_gain = norm_back(after_feed, gain_exit, exit_in_grad)
     feed_grad = feed_grad + out_cotangent.reshape(token_count, width)
     branch_three = feed_grad.astype(low)
-    branch_cols = branch_three.reshape(token_count, n_seq, own)
-    down_grad = scatter(mix("tzn,tkr->zknr", branch_cols, hidden_rows)).T
-    hidden_mid_grad = (
-        mix("tzn,zknr->tkr", branch_cols, down_full)
-        .reshape(token_count, n_seq, own_feed)
-        .transpose(1, 0, 2)
-    )
+    hidden_mid_grad = contract(branch_three, down_full, 1, 1)
     unused, gated_pull = jax.vjp(gated_unit, gate_pre, up_pre)
     gate_grad, up_grad = gated_pull(hidden_mid_grad)
-    gate_up_grad = jnp.concatenate([gate_grad.astype(low), up_grad.astype(low)], axis=2)
-    feed_sums = scatter(mix("td,ztn->zdn", normed_three, gate_up_grad))
-    normed_three_grad = mix("ztn,zdn->td", gate_up_grad, feed_full)
+    gate_grad, up_grad = gate_grad.astype(low), up_grad.astype(low)
+    normed_three_grad = contract(gate_grad, gate_full, 1, 1) + contract(up_grad, up_full, 1, 1)
     cross_grad, full_feed_gain = norm_back(after_cross, gain_three, normed_three_grad)
     cross_grad = cross_grad + feed_grad
     branch_two = cross_grad.astype(low)
-    branch_cols = branch_two.reshape(token_count, n_seq, own)
-    mixture_two_grad = mix("twm,wdm->td", branch_cols, cross_out).astype(low)
-    mixture_two_grad = swap(mixture_two_grad.reshape(token_count, n_seq, own).transpose(1, 0, 2))
+    mixture_two_grad = swap(stacked(contract(branch_two, cross_out, 1, 1), n_seq))
     q_grad, kv_grad = attend_back(
         prefix_len,
         [q_two, kv_two],
@@ -318,27 +342,43 @@
         own,
         False,
     )
-    q_grad = swap(q_grad.reshape(n_seq, token_count, own))
-    kv_grad = swap(kv_grad.reshape(n_seq, token_count, 2 * own))
-    encoder_grad = mix("ztn,zdn->td", kv_grad, cross_kv).reshape(encoder_in.shape)
-    cross_sums = scatter(
+    q_grad = side_by_side(swap(q_grad.reshape(n_seq, token_count, own)))
+    kv_grad = side_by_side(swap(kv_grad.reshape(n_seq, token_count, 2 * own)))
+    encoder_grad = contract(kv_grad, cross_kv, 1, 1).reshape(encoder_in.shape)
+    down_terms = contract(hidden_mid, branch_three, 0, 0).astype(low)
+    down_terms = jnp.pad(
+        down_terms.reshape(n_dp, -1, width), ((0, 0), (0, down_pad), (0, 0))
+    ).reshape(n_dp, down_folds, own_rows, width)
+    rest_terms = lax.psum_scatter(
         jnp.concatenate(
             [
-                mix("td,ztn->zdn", normed_two, q_grad).astype(low),
-                mix("td,ztn->zdn", states, kv_grad).astype(low),
-                mix("td,tzn->zdn", mixture_two, branch_cols).astype(low),
-            ],
-            axis=2,
+                contract(normed_two, q_grad, 0, 0).astype(low),
+                contract(states, kv_grad, 0, 0).astype(low),
+                contract(mixture_two, branch_two, 0, 0).astype(low),
+                contract(normed_three, gate_grad, 0, 0).astype(low),
+                contract(normed_three, up_grad, 0, 0).astype(low),
+            ]
+            + [down_terms[:, fold].reshape(width, width) for fold in range(down_folds)],
+            axis=1,
+        ),
+        "dp",
+        scatter_dimension=0,
+        tiled=True,
+    )
+    rest_sums = swap(
+        jnp.concatenate(
+            [stacked(part, n_seq) for part in cut(rest_terms, full_sizes, 1)], axis=2
         )
     )
-    self_grad, full_cross_gain = norm_back(
-        after_self, gain_two, mix("ztn,zdn->td", q_grad, cross_q)
-    )
+    rest_sums = jnp.sum(rest_sums.astype(jnp.float32), axis=0)
+    cross_q_sum, cross_kv_sum, cross_out_sum, gate_sum, up_sum, *down_sums = cut(
+        rest_sums, rest_sizes, 1
+    )
+    down_grad = jnp.concatenate(down_sums, axis=0)[: feed_down.shape[0]]
+    self_grad, full_cross_gain = norm_back(after_self, gain_two, contract(q_grad, cross_q, 1, 1))
     self_grad = self_grad + cross_grad
     branch_one = self_grad.astype(low)
-    branch_cols = branch_one.reshape(token_count, n_seq, own)
-    mixture_one_grad = mix("twm,wdm->td", branch_cols, self_out).astype(low)
-    mixture_one_grad = swap(mixture_one_grad.reshape(token_count, n_seq, own).transpose(1, 0, 2))
+    mixture_one_grad = swap(stacked(contract(branch_one, self_out, 1, 1), n_seq))
     (qkv_grad,) = attend_back(
         prefix_len,
         [qkv_one],
@@ -349,24 +389,38 @@
         own,
         True,
     )
-    qkv_grad = swap(qkv_grad.reshape(n_seq, token_count, 3 * own))
-    normed_one_grad = mix("ztn,zdn->td", qkv_grad, self_qkv)
+    qkv_grad = side_by_side(swap(qkv_grad.reshape(n_seq, token_count, 3 * own)))
+    normed_one_grad = contract(qkv_grad, self_qkv, 1, 1)
     input_grad, full_self_gain = norm_back(residual_in, gain_one, normed_one_grad)
     hidden_grad = (input_grad + self_grad).reshape(hidden_in.shape)
     gain_terms = jnp.stack(
         [full_self_gain, full_cross_gain, full_feed_gain, full_exit_gain], axis=1
     ).astype(low)
     gain_terms = jnp.pad(gain_terms, ((0, 0), (0, GAIN_LANES - gain_terms.shape[1])))
-    self_sums = scatter(
+    self_terms = lax.psum_scatter(
         jnp.concatenate(
             [
-                mix("td,ztn->zdn", normed_one, qkv_grad).astype(low),
-                mix("td,tzn->zdn", mixture_one, branch_cols).astype(low),
-                jnp.broadcast_to(gain_terms[None], (n_seq, width, GAIN_LANES)),
+                contract(normed_one, qkv_grad, 0, 0).astype(low),
+                contract(mixture_one, branch_one, 0, 0).astype(low),
+                gain_terms,
+            ],
+            axis=1,
+        ),
+        "dp",
+        scatter_dimension=0,
+        tiled=True,
+    )
+    self_sums = swap(
+        jnp.concatenate(
+            [
+                stacked(self_terms[:, : 3 * width], n_seq),
+                stacked(self_terms[:, 3 * width : 4 * width], n_seq),
+                jnp.broadcast_to(self_terms[None, :, 4 * width :], (n_seq, own_rows, GAIN_LANES)),
             ],
             axis=2,
         )
     )
+    self_sums = jnp.sum(self_sums.astype(jnp.float32), axis=0)
 
     def piece(sums, at):
         return sums[:, at * own : (at + 1) * own]
@@ -383,13 +437,13 @@
         piece(self_sums, 2),
         piece(self_sums, 3),
         gain_sums[1],
-        piece(cross_sums, 0),
-        piece(cross_sums, 1),
-        piece(cross_sums, 2),
-        piece(cross_sums, 3),
+        cross_q_sum,
+        piece(cross_kv_sum, 0),
+        piece(cross_kv_sum, 1),
+        cross_out_sum,
         gain_sums[2],
-        feed_sums[:, :own_feed],
-        feed_sums[:, own_feed:],
+        gate_sum,
+        up_sum,
         down_grad,
         gain_sums[3],
         embedding_grad,

time: 1210 us -> 977 us (0.81)
  waiting for transfers between devices: 762 us -> 436 us
  blocking collectives: 76.7 us -> 123 us
  local copies, waits for them, and re-layouts: 69.1 us -> 95.5 us
    reduce_scatter x5 -> x2, waiting for transfers between devices: 313 us -> 102 us  [the longest x1 99.4 us: per_device(): lax.psum_scatter(jnp.concatenate([contract(normed_two, q_grad, 0, 0).asty...]
    all_gather x4 -> x2, waiting for transfers between devices: 156 us -> 13.5 us  [the longest x1 13.5 us: per_device(): lax.all_gather(jnp.concatenate([side_by_side(part) for part in cut(rest_p...]
    unnamed x12 -> x9, waiting for transfers between devices: 1.38 us -> 132 us
    all_gather x1, waiting for transfers between devices: 92.7 us -> 12.9 us  [per_device(): table = lax.all_gather(embedding.T, 'seq', axis=0, tiled=True)]
    dot_general x3 -> x27, matrix products: 69.5 us -> 144 us  [contract(): lax.dot_general(first_op, second_op, (((first_dim,), (second_dim,)), ((),...]
    dot_general x21 -> x0, matrix products: 65.3 us -> none  [mix(): jnp.einsum(spec, first_op, second_op, preferred_element_type=jnp.float32)]
    all_to_all x3 -> x5, blocking collectives: 58.2 us -> 105 us  [swap(): return lax.all_to_all(pieces, 'seq', 0, 0, tiled=True)]
    reduce_scatter x1, waiting for transfers between devices: 46.2 us -> 18.5 us  [per_device(): lax.psum_scatter(contract(logit_grads, table, 1, 1).astype(low), 'dp', sc...]
  transfers between devices with their start and end apart: 19 -> 17, of which waited for: 15 -> 14; matrix products, arithmetic and copies ran while one was open for 14% -> 16% of each run, Pallas kernels for 5% -> 2%
where the time goes in v2:
time: 977 us; the launch traced here: 965 us
  waiting for transfers between devices  436 us (45%)
  matrix products  144 us (15%)
  blocking collectives  123 us (13%)
  local copies, waits for them, and re-layouts  95.5 us (10%)
  Pallas kernels  56.6 us (6%)
  starting transfers between devices  53.3 us (5%)
  other arithmetic  39.5 us (4%)
  between operations  16.4 us (2%)
    dot_general x27, matrix products, contract(): lax.dot_general(first_op, second_op, (((first_dim,), (second_dim,)), ((),...  144 us
    unnamed x9, waiting for transfers between devices  132 us
    all_to_all x9, waiting for transfers between devices, swap(): return lax.all_to_all(pieces, 'seq', 0, 0, tiled=True)  122 us
    all_to_all x5, blocking collectives, swap(): return lax.all_to_all(pieces, 'seq', 0, 0, tiled=True)  105 us
    reduce_scatter x1, waiting for transfers between devices, per_device(): lax.psum_scatter(jnp.concatenate([contract(normed_two, q_grad, 0, 0).asty...  99.4 us
    all_to_all x9, starting transfers between devices, swap(): return lax.all_to_all(pieces, 'seq', 0, 0, tiled=True)  53.1 us
    pallas_call x2, Pallas kernels, attend_back(): pl.pallas_call(functools.partial(attend_back_kernel, places=places, spots...  37.3 us
    all_gather x1, waiting for transfers between devices, per_device(): tokens = lax.all_gather(normed_exit, 'dp', axis=0, tiled=True)  35.7 us
  transfers between devices with their start and end apart: 17, of which 14 were waited for; matrix products, arithmetic and copies ran while one was open for 16% of the time, Pallas kernels for 2%

profile of v2, /device:TPU:8, one launch (start us, length us, event | category | flops | bytes accessed | tf_op | source)
XLA Modules:
  0.0 965.2 jit_solution(6736136653727037011)
XLA Ops:
  9.1 5.3 all-to-all-start
  15.4 11.7 %all-to-all-done = bf16[4,96,768]{2,1,0:T(8,128)(2,1)S(1)} async-done(((bf16[4,96,768]{2,1,0:T(8,128)(2,1)}), bf16[4,96,768]{2,1,0:T(8,128)(2,1)S(1)}, u32[]{:S(2)}, u32[]{:S(2)}) %all-to-all-start) | async-done | bytes 589856 | tf_op jit(solution)/shard_map/all_to_all | solution.py:43
  30.0 47.0 %all_to_all.70 = bf16[4,96,2368]{2,1,0:T(8,128)(2,1)S(1)} all-to-all(bf16[4,96,2368]{2,1,0:T(8,128)(2,1)S(1)} %broadcast_in_dim.19), channel_id=1, replica_groups=mesh['dp'=8,'seq'=4] {'seq'}, dimensions={0} | all-to-all | bytes 3637248 | tf_op jit(solution)/shard_map/all_to_all | solution.py:43
  97.6 5.1 all-to-all-start.1
  103.4 23.6 %all-to-all-done.1 = bf16[4,256,576]{1,2,0:T(8,128)(2,1)S(1)} async-done(((bf16[4,256,576]{1,2,0:T(8,128)(2,1)}), bf16[4,256,576]{1,2,0:T(8,128)(2,1)S(1)}, u32[]{:S(2)}, u32[]{:S(2)}) %all-to-all-start.1) | async-done | bytes 1179680 | tf_op jit(solution)/shard_map/all_to_all | solution.py:43
  128.4 10.4 %shard_map.365 = bf16[1024,192]{1,0:T(8,128)(2,1)} custom-call(s32[1]{0:T(128)S(6)} %copy.213.prefix_ref, bf16[1024,576]{1,0:T(8,128)(2,1)} %bitcast.229), custom_call_target="tpu_custom_call" | custom-call | tf_op jit(solution)/shard_map/pallas_call | solution.py:161
  140.0 14.7 %all_to_all.71 = bf16[4,256,192]{1,2,0:T(8,128)(2,1)S(1)} all-to-all(bf16[4,256,192]{1,2,0:T(8,128)(2,1)S(1)} %copy.108), channel_id=1, replica_groups=mesh['dp'=8,'seq'=4] {'seq'}, dimensions={0} | all-to-all | bytes 786432 | tf_op jit(solution)/shard_map/all_to_all | solution.py:43
  156.8 13.5 %all-gather.11.cloned.1.call-done = bf16[768,9472]{1,0:T(8,128)(2,1)} async-done(((bf16[96,9472]{1,0:T(8,128)(2,1)}), bf16[768,9472]{1,0:T(8,128)(2,1)}) %all-gather.11.cloned.1.call-update) | async-done | bytes 14549008 | tf_op jit(solution)/shard_map/all_gather | solution.py:251
  173.0 5.1 all-to-all-start.4
  182.0 16.7 %all-to-all-done.4 = bf16[4,256,192]{1,2,0:T(8,128)(2,1)S(1)} async-done(((bf16[4,256,192]{1,2,0:T(8,128)(2,1)}), bf16[4,256,192]{1,2,0:T(8,128)(2,1)S(1)}, u32[]{:S(2)}, u32[]{:S(2)}) %all-to-all-start.4) | async-done | bytes 393248 | tf_op jit(solution)/shard_map/all_to_all | solution.py:43
  198.7 7.0 all-to-all-start.5
  206.7 37.4 %all-to-all-done.5 = bf16[4,256,384]{2,1,0:T(8,128)(2,1)S(1)} async-done(((bf16[4,256,384]{2,1,0:T(8,128)(2,1)}), bf16[4,256,384]{2,1,0:T(8,128)(2,1)S(1)}, u32[]{:S(2)}, u32[]{:S(2)}) %all-to-all-start.5) | async-done | bytes 786464 | tf_op jit(solution)/shard_map/all_to_all | solution.py:43
  244.9 8.8 shard_map.366
  255.8 6.4 all-to-all-start.6
  266.7 10.7 %all-to-all-done.6 = bf16[4,256,192]{1,2,0:T(8,128)(2,1)S(1)} async-done(((bf16[4,256,192]{1,2,0:T(8,128)(2,1)}), bf16[4,256,192]{1,2,0:T(8,128)(2,1)S(1)}, u32[]{:S(2)}, u32[]{:S(2)}) %all-to-all-start.6) | async-done | bytes 393248 | tf_op jit(solution)/shard_map/all_to_all | solution.py:43
  283.2 5.3 multiply_convert_fusion.2
  291.6 9.1 all-gather.2
  300.7 12.9 %all-gather.15.cloned.1.call-done = bf16[768,4016]{1,0:T(8,128)(2,1)} async-done(((bf16[192,4016]{1,0:T(8,128)(2,1)}), bf16[768,4016]{1,0:T(8,128)(2,1)}) %all-gather.15.cloned.1.call-update) | async-done | bytes 6168592 | tf_op jit(solution)/shard_map/all_gather | solution.py:259
  313.6 35.7 %all-gather.13.cloned.1.call-done = bf16[2048,768]{1,0:T(8,128)(2,1)} async-done(((bf16[256,768]{1,0:T(8,128)(2,1)}), bf16[2048,768]{1,0:T(8,128)(2,1)}) %all-gather.13.cloned.1.call-update) | async-done | bytes 3145744 | tf_op jit(solution)/shard_map/all_gather | solution.py:296
  349.3 22.2 %fusion.94 = (f32[2048]{0:T(1024)S(1)}, f32[2048,4016]{0,1:T(8,128)}) fusion(bf16[2048,768]{1,0:T(8,128)(2,1)} %all-gather.13.cloned.1.call-done, bf16[768,4016]{1,0:T(8,128)(2,1)} %all-gather.15.cloned.1.call-done), kind=kOutput, calls=%fused_computation.209 | convolution fusion | flops 12641466368 | bytes 42221568 | tf_op jit(solution)/shard_map/dot_general | solution.py:19
  371.5 15.2 %exponential_reduce_fusion = (f32[2048]{0:T(1024)S(1)}, f32[2048]{0:T(1024)S(1)}) fusion(f32[2048,4016]{0,1:T(8,128)} %get-tuple-element.163, f32[2048]{0:T(1024)S(1)} %get-tuple-element.162, s32[2048]{0:T(1024)S(1)} %bitcast.273), kind=kLoop, calls=%fused_computation.3 | loop fusion | flops 41119744 | bytes 32931840 | tf_op jit(solution)/shard_map/reduce_sum | solution.py:301
  386.7 9.5 all-gather.3
  397.1 25.3 %convolution_convert_fusion.7 = bf16[2048,768]{1,0:T(8,128)(2,1)} fusion(bf16[768,4016]{1,0:T(8,128)(2,1)S(1)} %copy-done.56, f32[2048,4016]{0,1:T(8,128)} %get-tuple-element.163, f32[2048]{0:T(1024)S(1)} %log_add_fusion, f32[2048]{0:T(1024)S(1)} %bitcast.276, s32[2048]{0:T(1024)S(1)} %bitcast.274), kind=kOutput, calls=%fused_computation.19 | convolution fusion | flops 12684165120 | bytes 42237952 | tf_op jit(solution)/shard_map/dot_general | solution.py:19
  422.4 27.7 %convolution_convert_fusion = bf16[768,4016]{0,1:T(8,128)(2,1)} fusion(bf16[2048,768]{1,0:T(8,128)(2,1)} %all-gather.13.cloned.1.call-done, f32[2048,4016]{0,1:T(8,128)} %get-tuple-element.163, f32[2048]{0:T(1024)S(1)} %log_add_fusion, f32[2048]{0:T(1024)S(1)} %bitcast.277, s32[2048]{0:T(1024)S(1)} %bitcast.275), kind=kOutput, calls=%fused_computation.6 | convolution fusion | flops 12685676544 | bytes 42237952 | tf_op jit(solution)/shard_map/dot_general | solution.py:19
  450.1 18.5 %reduce-scatter.7.cloned.1.call-done = bf16[256,768]{1,0:T(8,128)(2,1)} async-done(((bf16[2048,768]{1,0:T(8,128)(2,1)}), bf16[256,768]{1,0:T(8,128)(2,1)}) %reduce-scatter.7.cloned.1.call-update) | async-done | bytes 393232 | tf_op jit(solution)/shard_map/reduce_scatter | solution.py:314
  472.9 4.0 fusion.22
  476.9 3.7 fusion.8
  480.6 3.7 multiply_reduce_fusion
  486.5 14.6 %all_to_all.72 = bf16[4,256,192]{1,2,0:T(8,128)(2,1)S(1)} all-to-all(bf16[4,256,192]{1,2,0:T(8,128)(2,1)S(1)} %bitcast.257), channel_id=1, replica_groups=mesh['dp'=8,'seq'=4] {'seq'}, dimensions={0} | all-to-all | bytes 786432 | tf_op jit(solution)/shard_map/all_to_all | solution.py:43
  502.2 18.2 %shard_map.367 = (bf16[1024,192]{1,0:T(8,128)(2,1)}, bf16[1024,384]{1,0:T(8,128)(2,1)}) custom-call(s32[1]{0:T(128)S(6)} %copy.213.prefix_ref, bf16[1024,192]{1,0:T(8,128)(2,1)} %bitcast.241, bf16[1024,384]{1,0:T(8,128)(2,1)} %bitcast.232, bf16[1024,192]{1,0:T(8,128)(2,1)} %bitcast.246), custom_call_target="tpu_custom_call" | custom-call | tf_op jit(solution)/shard_map/pallas_call | solution.py:174
  521.6 13.8 %all_to_all.73 = bf16[4,256,192]{1,2,0:T(8,128)(2,1)S(1)} all-to-all(bf16[4,256,192]{1,2,0:T(8,128)(2,1)S(1)} %copy.130), channel_id=1, replica_groups=mesh['dp'=8,'seq'=4] {'seq'}, dimensions={0} | all-to-all | bytes 786432 | tf_op jit(solution)/shard_map/all_to_all | solution.py:43
  542.7 14.7 %all_to_all.74 = bf16[4,256,192]{1,2,0:T(8,128)(2,1)} all-to-all(bf16[4,256,192]{1,2,0:T(8,128)(2,1)} %bitcast.258), channel_id=1, replica_groups=mesh['dp'=8,'seq'=4] {'seq'}, dimensions={0} | all-to-all | bytes 786432 | tf_op jit(solution)/shard_map/all_to_all | solution.py:43
  559.5 19.1 %shard_map.368 = bf16[1024,576]{1,0:T(8,128)(2,1)} custom-call(s32[1]{0:T(128)S(6)} %copy.213.prefix_ref, bf16[1024,576]{1,0:T(8,128)(2,1)} %bitcast.230, bf16[1024,192]{1,0:T(8,128)(2,1)} %bitcast.247), custom_call_target="tpu_custom_call" | custom-call | tf_op jit(solution)/shard_map/pallas_call | solution.py:174
  581.0 6.1 all-to-all-start.10
  592.7 17.6 %all-to-all-done.10 = bf16[4,256,576]{1,2,0:T(8,128)(2,1)} async-done(((bf16[4,256,576]{1,2,0:T(8,128)(2,1)}), bf16[4,256,576]{1,2,0:T(8,128)(2,1)}, u32[]{:S(2)}, u32[]{:S(2)}) %all-to-all-start.10) | async-done | bytes 1179680 | tf_op jit(solution)/shard_map/all_to_all | solution.py:43
  610.3 4.5 convolution_convert_fusion.1
  614.8 5.0 fusion.50
  620.7 5.6 fusion.1
  628.7 7.5 all-to-all-start.11
  648.4 4.3 all-to-all-done.11
  670.9 8.8 copy.154
  685.3 5.1 all-to-all-start.12
  690.4 99.4 %reduce-scatter.11.cloned.1.call-done = bf16[96,9472]{1,0:T(8,128)(2,1)} async-done(((bf16[768,9472]{1,0:T(8,128)(2,1)}), bf16[96,9472]{1,0:T(8,128)(2,1)}) %reduce-scatter.11.cloned.1.call-update) | async-done | bytes 1818640 | tf_op jit(solution)/shard_map/reduce_scatter | solution.py:352
  795.0 3.7 concatenate.38
  798.7 5.4 all-to-all-start.13
  805.7 3.6 fusion.26
  812.1 130.8 %reduce-scatter.13.cloned.1.call-done = bf16[192,4016]{1,0:T(8,128)(2,1)} async-done(((bf16[768,4016]{1,0:T(8,128)(2,1)}), bf16[192,4016]{1,0:T(8,128)(2,1)}) %reduce-scatter.13.cloned.1.call-update) | async-done | bytes 1542160
  948.3 5.2 copy.152
  (297 shorter events, 139.3 us)
Async XLA Ops:
  7.2 170.9 %copy-start = (bf16[1,256,768]{2,1,0:T(8,128)(2,1)S(1)}, bf16[1,256,768]{2,1,0:T(8,128)(2,1)}, u32[]{:S(2)}) copy-start(bf16[1,256,768]{2,1,0:T(8,128)(2,1)} %param.23) | copy-start | bytes 1179652
  9.1 17.9 %all-to-all-start = ((bf16[4,96,768]{2,1,0:T(8,128)(2,1)}), bf16[4,96,768]{2,1,0:T(8,128)(2,1)S(1)}, u32[]{:S(2)}, u32[]{:S(2)}) async-start(bf16[4,96,768]{2,1,0:T(8,128)(2,1)} %broadcast_in_dim.18), calls=%async_computation | async-start | bytes 1179648 | tf_op jit(solution)/shard_map/all_to_all | solution.py:43
  14.4 14.8 %copy-start.24 = (bf16[256,192]{0,1:T(8,128)(2,1)S(1)}, bf16[256,192]{0,1:T(8,128)(2,1)}, u32[]{:S(2)}) copy-start(bf16[256,192]{0,1:T(8,128)(2,1)} %param.41) | copy-start | bytes 294916
  14.4 76.2 %all-gather.9.cloned.1.call-start = ((), (), s32[]{:S(2)}) async-start(), calls=%async_computation.18 | async-start | bytes 5529600 | tf_op jit(solution)/shard_map/all_gather | solution.py:228
  15.3 14.3 %copy-start.27 = (bf16[96,512]{1,0:T(8,128)(2,1)S(1)}, bf16[96,512]{1,0:T(8,128)(2,1)}, u32[]{:S(2)}) copy-start(bf16[96,512]{1,0:T(8,128)(2,1)} %param.39) | copy-start | bytes 294916
  15.3 14.3 %copy-start.28 = (bf16[96,512]{1,0:T(8,128)(2,1)S(1)}, bf16[96,512]{1,0:T(8,128)(2,1)}, u32[]{:S(2)}) copy-start(bf16[96,512]{1,0:T(8,128)(2,1)} %param.40) | copy-start | bytes 294916
  15.3 14.3 %copy-start.29 = (bf16[96,192]{1,0:T(8,128)(2,1)S(1)}, bf16[96,192]{1,0:T(8,128)(2,1)}, u32[]{:S(2)}) copy-start(bf16[96,192]{1,0:T(8,128)(2,1)} %param.34) | copy-start | bytes 110596
  15.3 14.3 %copy-start.30 = (bf16[96,192]{1,0:T(8,128)(2,1)S(1)}, bf16[96,192]{1,0:T(8,128)(2,1)}, u32[]{:S(2)}) copy-start(bf16[96,192]{1,0:T(8,128)(2,1)} %param.35) | copy-start | bytes 110596
  15.3 14.3 %copy-start.31 = (bf16[96,192]{1,0:T(8,128)(2,1)S(1)}, bf16[96,192]{1,0:T(8,128)(2,1)}, u32[]{:S(2)}) copy-start(bf16[96,192]{1,0:T(8,128)(2,1)} %param.36) | copy-start | bytes 110596
  15.3 14.3 %copy-start.32 = (bf16[96,192]{1,0:T(8,128)(2,1)S(1)}, bf16[96,192]{1,0:T(8,128)(2,1)}, u32[]{:S(2)}) copy-start(bf16[96,192]{1,0:T(8,128)(2,1)} %param.37) | copy-start | bytes 110596
  29.1 141.1 %all-gather.11.cloned.1.call-start = ((), (), s32[]{:S(2)}) async-start(), calls=%async_computation.19 | async-start | bytes 16367616 | tf_op jit(solution)/shard_map/all_gather | solution.py:251
  79.2 6.0 copy-start.19
  79.3 8.0 copy-start.17
  89.7 223.9 %all-gather.15.cloned.1.call-start = ((), (), s32[]{:S(2)}) async-start(), calls=%async_computation.21 | async-start | bytes 7864320 | tf_op jit(solution)/shard_map/all_gather | solution.py:259
  90.6 5.5 copy-start.33
  97.6 29.3 %all-to-all-start.1 = ((bf16[4,256,576]{1,2,0:T(8,128)(2,1)}), bf16[4,256,576]{1,2,0:T(8,128)(2,1)S(1)}, u32[]{:S(2)}, u32[]{:S(2)}) async-start(bf16[4,256,576]{1,2,0:T(8,128)(2,1)} %bitcast.9), calls=%async_computation.1 | async-start | bytes 2359296 | tf_op jit(solution)/shard_map/all_to_all | solution.py:43
  154.7 18.2 %copy-start.14 = (bf16[4,256,192]{1,2,0:T(8,128)(2,1)}, bf16[4,256,192]{1,2,0:T(8,128)(2,1)S(1)}, u32[]{:S(2)}) copy-start(bf16[4,256,192]{1,2,0:T(8,128)(2,1)S(1)} %all_to_all.71) | copy-start | bytes 1179652
  156.7 16.2 %copy-start.51 = (f32[256]{0:T(256)}, f32[256]{0:T(256)S(1)}, u32[]{:S(2)}) copy-start(f32[256]{0:T(256)S(1)} %get-tuple-element.154) | copy-start | bytes 3076
  156.8 16.2 %copy-start.41 = (f32[256]{0:T(256)}, f32[256]{0:T(256)S(1)}, u32[]{:S(2)}) copy-start(f32[256]{0:T(256)S(1)} %fusion.83) | copy-start | bytes 3076
  173.0 25.7 %all-to-all-start.4 = ((bf16[4,256,192]{1,2,0:T(8,128)(2,1)}), bf16[4,256,192]{1,2,0:T(8,128)(2,1)S(1)}, u32[]{:S(2)}, u32[]{:S(2)}) async-start(bf16[4,256,192]{1,2,0:T(8,128)(2,1)} %bitcast.23), calls=%async_computation.4 | async-start | bytes 786432 | tf_op jit(solution)/shard_map/all_to_all | solution.py:43
  198.7 45.4 %all-to-all-start.5 = ((bf16[4,256,384]{2,1,0:T(8,128)(2,1)}), bf16[4,256,384]{2,1,0:T(8,128)(2,1)S(1)}, u32[]{:S(2)}, u32[]{:S(2)}) async-start(bf16[4,256,384]{2,1,0:T(8,128)(2,1)} %bitcast.28), calls=%async_computation.5 | async-start | bytes 1572864 | tf_op jit(solution)/shard_map/all_to_all | solution.py:43
  255.8 21.7 %all-to-all-start.6 = ((bf16[4,256,192]{1,2,0:T(8,128)(2,1)}), bf16[4,256,192]{1,2,0:T(8,128)(2,1)S(1)}, u32[]{:S(2)}, u32[]{:S(2)}) async-start(bf16[4,256,192]{1,2,0:T(8,128)(2,1)} %copy.123), calls=%async_computation.6 | async-start | bytes 786432 | tf_op jit(solution)/shard_map/all_to_all | solution.py:43
  262.2 87.1 %all-gather.13.cloned.1.call-start = ((), (), s32[]{:S(2)}) async-start(), calls=%async_computation.20 | async-start | bytes 3538944 | tf_op jit(solution)/shard_map/all_gather | solution.py:296
  277.5 5.7 copy-start.10
  280.2 8.3 copy-start.22
  283.2 5.3 copy-start.57
  283.2 6.3 copy-start.11
  291.5 177.1 %reduce-scatter.7.cloned.1.call-start = ((), (), s32[]{:S(2)}) async-start(), calls=%async_computation.22 | async-start | bytes 3538944 | tf_op jit(solution)/shard_map/reduce_scatter | solution.py:314
  300.7 121.7 %copy-start.40 = (f32[8,1,256]{2,1,0:T(1,128)}, f32[8,1,256]{2,1,0:T(1,128)S(1)}, u32[]{:S(2)}) copy-start(f32[8,1,256]{2,1,0:T(1,128)S(1)} %get-tuple-element.153) | copy-start | bytes 24580
  371.5 25.6 %copy-start.56 = (bf16[768,4016]{1,0:T(8,128)(2,1)S(1)}, bf16[768,4016]{1,0:T(8,128)(2,1)}, u32[]{:S(2)}) copy-start(bf16[768,4016]{1,0:T(8,128)(2,1)} %all-gather.15.cloned.1.call-done) | copy-start | bytes 18505732
  397.1 25.4 %copy-start.39 = (f32[2048]{0:T(1024)}, f32[2048]{0:T(1024)S(1)}, u32[]{:S(2)}) copy-start(f32[2048]{0:T(1024)S(1)} %log_add_fusion) | copy-start | bytes 24580
  486.4 49.1 %copy-start.42 = (f32[256]{0:T(256)S(1)}, f32[256]{0:T(256)}, u32[]{:S(2)}) copy-start(f32[256]{0:T(256)} %copy-done.41) | copy-start | bytes 3076
  502.2 35.8 %copy-start.52 = (f32[256]{0:T(256)S(1)}, f32[256]{0:T(256)}, u32[]{:S(2)}) copy-start(f32[256]{0:T(256)} %copy-done.51) | copy-start | bytes 3076
  578.6 8.5 copy-start.50
  578.6 31.7 %copy-start.26 = (f32[768]{0:T(1024)S(1)}, f32[768]{0:T(1024)}, u32[]{:S(2)}) copy-start(f32[768]{0:T(1024)} %copy-done.25) | copy-start | bytes 9220
  578.6 31.7 %copy-start.34 = (f32[256]{0:T(256)S(1)}, f32[256]{0:T(256)}, u32[]{:S(2)}) copy-start(f32[256]{0:T(256)} %copy-done.33) | copy-start | bytes 3076
  581.0 29.2 %all-to-all-start.10 = ((bf16[4,256,576]{1,2,0:T(8,128)(2,1)}), bf16[4,256,576]{1,2,0:T(8,128)(2,1)}, u32[]{:S(2)}, u32[]{:S(2)}) async-start(bf16[4,256,576]{1,2,0:T(8,128)(2,1)} %copy.133), calls=%async_computation.11 | async-start | bytes 2359296 | tf_op jit(solution)/shard_map/all_to_all | solution.py:43
  587.1 95.2 %reduce-scatter.9.cloned.1.call-start = ((), (), s32[]{:S(2)}) async-start(), calls=%async_computation.23 | async-start | bytes 5529600 | tf_op jit(solution)/shard_map/reduce_scatter | solution.py:400
  628.7 24.0 %all-to-all-start.11 = ((bf16[4,256,384]{1,2,0:T(8,128)(2,1)}), bf16[4,256,384]{1,2,0:T(8,128)(2,1)}, u32[]{:S(2)}, u32[]{:S(2)}) async-start(bf16[4,256,384]{1,2,0:T(8,128)(2,1)} %copy.134), calls=%async_computation.12 | async-start | bytes 1572864 | tf_op jit(solution)/shard_map/all_to_all | solution.py:43
  636.2 153.6 %reduce-scatter.11.cloned.1.call-start = ((), (), s32[]{:S(2)}) async-start(), calls=%async_computation.24 | async-start | bytes 16367616 | tf_op jit(solution)/shard_map/reduce_scatter | solution.py:352
  670.8 272.1 %reduce-scatter.13.cloned.1.call-start = ((), (), s32[]{:S(2)}) async-start(), calls=%async_computation.25 | async-start | bytes 7864320
  685.3 113.5 %all-to-all-start.12 = ((bf16[4,96,896]{2,1,0:T(8,128)(2,1)}), bf16[4,96,896]{2,1,0:T(8,128)(2,1)S(1)}, u32[]{:S(2)}, u32[]{:S(2)}) async-start(bf16[4,96,896]{2,1,0:T(8,128)(2,1)} %pad_maximum_fusion.1), calls=%async_computation.14 | async-start | bytes 1376256 | tf_op jit(solution)/shard_map/all_to_all | solution.py:43
  798.7 154.8 %all-to-all-start.13 = ((bf16[4,96,2368]{2,1,0:T(8,128)(2,1)}), bf16[4,96,2368]{2,1,0:T(8,128)(2,1)}, u32[]{:S(2)}, u32[]{:S(2)}) async-start(bf16[4,96,2368]{2,1,0:T(8,128)(2,1)} %concatenate.38), calls=%async_computation.16 | async-start | bytes 3735552 | tf_op jit(solution)/shard_map/all_to_all | solution.py:43
  804.2 5.1 copy-start.45
  804.2 5.1 copy-start.53
  804.2 5.1 copy-start.4
  804.2 5.1 copy-start.18
  804.2 5.1 copy-start.35
  (34 other events, 92.0 us)
Sparse Core Ops, SparseCore 0:
  29.2 41.4 all-gather.8
  89.8 80.4 all-gather.10
  171.8 141.7 all-gather.14
  315.9 33.3 all-gather.12
  422.5 46.0 reduce-scatter.6
  626.5 55.7 reduce-scatter.8
  685.9 103.8 reduce-scatter.10
  792.1 150.8 reduce-scatter.12

commit v3 on v1

v3 whole, which is shorter than its diff:
```python
import functools

import jax
import jax.numpy as jnp
from jax import lax
from jax.experimental import pallas as pl
from jax.experimental.layout import Layout, with_layout_constraint
from jax.experimental.pallas import tpu as pltpu
from jax.sharding import PartitionSpec as P

HD = 64
GAIN_LANES = 128
TOKEN_ROWS = 256
LANES = 128

norm_eps = 1e-06
masked_score = -1000000000.0


def contract(first_op, second_op, first_dim, second_dim):
    return lax.dot_general(
        first_op,
        second_op,
        (((first_dim,), (second_dim,)), ((), ())),
        preferred_element_type=jnp.float32,
    )


def rows_first(array):
    return with_layout_constraint(array, Layout(major_to_minor=tuple(range(array.ndim))))


def norm_columns(inputs, scaling):
    return (
        inputs
        * lax.rsqrt(jnp.mean(inputs * inputs, axis=0, keepdims=True) + norm_eps)
        * scaling[:, None]
    )


def norm_back(inputs, scaling, upstream):
    unused, pullback = jax.vjp(norm_columns, inputs, scaling)
    return pullback(upstream)


def gated_unit(gate_in, upward):
    return jax.nn.gelu(gate_in, approximate=True) * upward


def swap(pieces):
    return lax.all_to_all(pieces, "seq", 0, 0, tiled=True)


def move_kernel(*refs, moves, count):
    for source, taken, target, put in moves:
        refs[count + target][put] = refs[source][taken]


def move(arrays, shapes, moves):
    return pl.pallas_call(
        functools.partial(move_kernel, moves=moves, count=len(arrays)),
        out_shape=[jax.ShapeDtypeStruct(shape, jnp.bfloat16) for shape in shapes],
    )(*arrays)


def sum_kernel(terms_ref, *refs, pieces):
    for ref, low, high in zip(refs, pieces[:-1], pieces[1:]):
        total = terms_ref[0, :, low:high].astype(jnp.float32)
        for block in range(1, terms_ref.shape[0]):
            total += terms_ref[block, :, low:high].astype(jnp.float32)
        ref[...] = total


def edges(sizes):
    return [sum(sizes[:at]) for at in range(len(sizes) + 1)]


every = slice(None)


def fetch(shards, extra):
    n_seq = lax.axis_size("seq")
    rows = shards[0].shape[0]
    sizes = [shard.shape[1] for shard in shards]
    starts = edges(sizes)
    moves = [
        (at, (every, every), 0, (block, every, slice(starts[at], starts[at + 1])))
        for at in range(len(shards))
        for block in range(n_seq)
    ]
    (copies,) = move(shards, [(n_seq, rows, starts[-1])], moves)
    parts = swap(copies)
    moves = [
        (
            0,
            (block, every, slice(starts[at], starts[at + 1])),
            0,
            (every, slice(low, low + sizes[at])),
        )
        for at in range(len(shards))
        for block in range(n_seq)
        for low in [n_seq * starts[at] + block * sizes[at]]
    ]
    width = n_seq * starts[-1]
    if extra is not None:
        moves.append((1, (every, every), 0, (every, slice(width, width + extra.shape[1]))))
        width += extra.shape[1]
    (full,) = move([parts] if extra is None else [parts, extra], [(rows, width)], moves)
    return lax.all_gather(full, "dp", axis=0, tiled=True)


def deliver(terms, sizes, extra, out_sizes):
    n_seq = lax.axis_size("seq")
    rows = terms.shape[0]
    starts = edges(sizes)
    moves = [
        (
            0,
            (every, slice(low, low + sizes[at])),
            0,
            (block, every, slice(starts[at], starts[at + 1])),
        )
        for at in range(len(sizes))
        for block in range(n_seq)
        for low in [n_seq * starts[at] + block * sizes[at]]
    ]
    width = starts[-1]
    if extra:
        low = n_seq * width
        moves += [
            (0, (every, slice(low, low + extra)), 0, (block, every, slice(width, width + extra)))
            for block in range(n_seq)
        ]
    (parts,) = move([terms], [(n_seq, rows, width + extra)], moves)
    return pl.pallas_call(
        functools.partial(sum_kernel, pieces=edges(out_sizes)),
        out_shape=[jax.ShapeDtypeStruct((rows, size), jnp.float32) for size in out_sizes],
    )(swap(parts))


def cut(array, sizes):
    return jnp.split(array, edges(sizes)[1:-1], axis=1)


def head_rows(row, head):
    return slice(row + head * HD, row + (head + 1) * HD)


def score_columns(key_ref, key_row, queries, head, allowed):
    scores = jnp.concatenate(
        [
            contract(key_ref[block, head_rows(key_row, head), :], queries, 0, 0)
            for block in range(key_ref.shape[0])
        ],
        axis=0,
    )
    if allowed is not None:
        scores = jnp.where(allowed, scores, masked_score)
    exponent = jnp.exp(scores - jnp.max(scores, axis=0, keepdims=True))
    return exponent * (1.0 / jnp.sum(exponent, axis=0, keepdims=True))


def allowed_columns(prefix_ref, step, blocks, rows):
    key_pos = lax.broadcasted_iota(jnp.int32, (blocks * rows, rows), 0)
    query_pos = step * rows + lax.broadcasted_iota(jnp.int32, (blocks * rows, rows), 1)
    return (key_pos <= query_pos) | (key_pos < prefix_ref[0])


def attend_kernel(prefix_ref, *refs, places, causal):
    out_ref = refs[-1]
    step = pl.program_id(0)
    (q_at, q_row), (k_at, k_row), (v_at, v_row) = places
    blocks, unused, rows = refs[k_at].shape
    allowed = allowed_columns(prefix_ref, step, blocks, rows) if causal else None
    for head in range(out_ref.shape[1] // HD):
        queries = refs[q_at][step, head_rows(q_row, head), :]
        queries = queries * jnp.asarray(HD**-0.5, queries.dtype)
        shares = score_columns(refs[k_at], k_row, queries, head, allowed).astype(queries.dtype)
        total = jnp.zeros(queries.shape, jnp.float32)
        for block in range(blocks):
            values = refs[v_at][block, head_rows(v_row, head), :]
            total += contract(values, shares[block * rows : (block + 1) * rows], 1, 0)
        out_ref[0, head_rows(0, head), :] = total.astype(out_ref.dtype)


def attend_back_kernel(prefix_ref, *refs, places, count, causal):
    upstream_ref = refs[count]
    outs = refs[count + 1 : -2]
    key_sum, value_sum = refs[-2:]
    step = pl.program_id(0)
    (q_at, q_row), (k_at, k_row), (v_at, v_row) = places
    blocks, unused, rows = refs[k_at].shape
    allowed = allowed_columns(prefix_ref, step, blocks, rows) if causal else None

    @pl.when(step == 0)
    def _():
        key_sum[...] = jnp.zeros_like(key_sum)
        value_sum[...] = jnp.zeros_like(value_sum)

    for head in range(upstream_ref.shape[1] // HD):
        mine = head_rows(0, head)
        queries = refs[q_at][step, head_rows(q_row, head), :]
        queries = queries * jnp.asarray(HD**-0.5, queries.dtype)
        upstream = upstream_ref[0, mine, :]
        shares = score_columns(refs[k_at], k_row, queries, head, allowed)
        share_grads = jnp.concatenate(
            [
                contract(refs[v_at][block, head_rows(v_row, head), :], upstream, 0, 0)
                for block in range(blocks)
            ],
            axis=0,
        )
        centre = jnp.sum(shares * share_grads, axis=0, keepdims=True)
        score_grads = (shares * (share_grads - centre)).astype(queries.dtype)
        shares = shares.astype(queries.dtype)
        total = jnp.zeros(queries.shape, jnp.float32)
        for block in range(blocks):
            part = slice(block * rows, (block + 1) * rows)
            key_rows = refs[k_at][block, head_rows(k_row, head), :]
            total += contract(key_rows, score_grads[part], 1, 0)
            key_sum[block, mine, :] += contract(queries, score_grads[part], 1, 1)
            value_sum[block, mine, :] += contract(upstream, shares[part], 1, 1)
        outs[q_at][step, head_rows(q_row, head), :] = (total * HD**-0.5).astype(outs[q_at].dtype)

    @pl.when(step == pl.num_programs(0) - 1)
    def _():
        width = key_sum.shape[1]
        outs[k_at][:, k_row : k_row + width, :] = key_sum[...].astype(outs[k_at].dtype)
        outs[v_at][:, v_row : v_row + width, :] = value_sum[...].astype(outs[v_at].dtype)


def exit_kernel(token_ref, table_ref, shifted_ref, product_ref, part_ref, logit_ref, *, rows):
    lanes = table_ref.shape[1]
    chunk = next(size for size in (1024, 512, 256, 128) if lanes % size == 0)
    tokens = token_ref[...]
    row_max = jnp.full((tokens.shape[0], 1), -jnp.inf, jnp.float32)
    for low in range(0, lanes, chunk):
        logits = contract(tokens, table_ref[:, low : low + chunk], 1, 0)
        if low + chunk > rows:
            lane = low + lax.broadcasted_iota(jnp.int32, (1, chunk), 1)
            logits = jnp.where(lane < rows, logits, -jnp.inf)
        logit_ref[:, low : low + chunk] = logits
        row_max = jnp.maximum(row_max, jnp.max(logits, axis=1, keepdims=True))
    row_sum = jnp.zeros_like(row_max)
    product = jnp.zeros(product_ref.shape, jnp.float32)
    for low in range(0, lanes, chunk):
        shifted = jnp.exp(logit_ref[:, low : low + chunk] - row_max)
        row_sum += jnp.sum(shifted, axis=1, keepdims=True)
        shifted = shifted.astype(shifted_ref.dtype)
        shifted_ref[:, low : low + chunk] = shifted
        product += contract(shifted, table_ref[:, low : low + chunk], 1, 1)
    product_ref[...] = product
    lane = lax.broadcasted_iota(jnp.int32, part_ref.shape, 1)
    part_ref[...] = jnp.where(lane == 0, row_max, row_sum)


def exit_rows(tokens, table, rows):
    count, width = tokens.shape
    lanes = table.shape[1]
    step_rows = min(TOKEN_ROWS, count)
    return pl.pallas_call(
        functools.partial(exit_kernel, rows=rows),
        grid=(count // step_rows,),
        in_specs=[pl.BlockSpec((step_rows, width), lambda step: (step, 0)), whole(table)],
        out_specs=[
            pl.BlockSpec((step_rows, lanes), lambda step: (step, 0)),
            pl.BlockSpec((step_rows, width), lambda step: (step, 0)),
            pl.BlockSpec((step_rows, LANES), lambda step: (step, 0)),
        ],
        out_shape=[
            jax.ShapeDtypeStruct((count, lanes), jnp.bfloat16),
            jax.ShapeDtypeStruct((count, width), jnp.float32),
            jax.ShapeDtypeStruct((count, LANES), jnp.float32),
        ],
        scratch_shapes=[pltpu.VMEM((step_rows, lanes), jnp.float32)],
    )(tokens, table)


def whole(array):
    return pl.BlockSpec(array.shape, lambda step: (0,) * len(array.shape))


def attend(prefix, arrays, places, width, causal):
    blocks, unused, rows = arrays[0].shape
    return pl.pallas_call(
        functools.partial(attend_kernel, places=places, causal=causal),
        grid=(blocks,),
        in_specs=[pl.BlockSpec(memory_space=pltpu.SMEM)] + [whole(array) for array in arrays],
        out_specs=pl.BlockSpec((1, width, rows), lambda step: (step, 0, 0)),
        out_shape=jax.ShapeDtypeStruct((blocks, width, rows), jnp.bfloat16),
    )(prefix, *arrays)


def attend_back(prefix, arrays, upstream, places, causal):
    blocks, width, rows = upstream.shape
    return pl.pallas_call(
        functools.partial(attend_back_kernel, places=places, count=len(arrays), causal=causal),
        grid=(blocks,),
        in_specs=[pl.BlockSpec(memory_space=pltpu.SMEM)]
        + [whole(array) for array in arrays]
        + [pl.BlockSpec((1, width, rows), lambda step: (step, 0, 0))],
        out_specs=[whole(array) for array in arrays],
        out_shape=[jax.ShapeDtypeStruct(array.shape, array.dtype) for array in arrays],
        scratch_shapes=[pltpu.VMEM((blocks, width, rows), jnp.float32)] * 2,
    )(prefix, *arrays, upstream)


def per_device(
    hidden_in,
    encoder_in,
    prefix_len,
    exit_flags,
    target_ids,
    out_cotangent,
    self_gain,
    self_query,
    self_key,
    self_value,
    self_output,
    cross_gain,
    cross_query,
    cross_key,
    cross_value,
    cross_output,
    feed_gain,
    feed_gate,
    feed_up,
    feed_down,
    exit_gain,
    embedding,
):
    width = hidden_in.shape[2]
    n_seq = lax.axis_size("seq")
    n_dp = lax.axis_size("dp")
    own_rows, own = self_query.shape
    own_feed = feed_gate.shape[1]
    fold_rows = feed_down.shape[0]
    folds = -(-fold_rows // own_rows)
    vocab_rows = embedding.shape[0]
    vocab_lanes = -(-vocab_rows // LANES) * LANES
    low = jnp.bfloat16

    gains = jnp.stack([self_gain, cross_gain, feed_gain, exit_gain], axis=1)
    gains = jnp.pad(gains, ((0, 0), (0, GAIN_LANES - gains.shape[1])))
    near = fetch(
        [
            jnp.concatenate([self_query, self_key, self_value], axis=1),
            self_output,
            cross_query,
            jnp.concatenate([cross_key, cross_value], axis=1),
            cross_output,
        ],
        gains,
    )
    near_sizes = (3 * own, own, own, 2 * own, own)
    self_qkv, self_out, cross_q, cross_kv, cross_out, gain_columns = cut(
        near, tuple(n_seq * size for size in near_sizes) + (GAIN_LANES,)
    )
    folded = jnp.pad(feed_down, ((0, folds * own_rows - fold_rows), (0, 0)))
    feed = fetch(
        [feed_gate, feed_up]
        + [folded[fold * own_rows : (fold + 1) * own_rows] for fold in range(folds)],
        None,
    )
    feed_sizes = (own_feed, own_feed) + (own,) * folds
    gate_full, up_full, *downs = cut(feed, tuple(n_seq * size for size in feed_sizes))
    table = lax.all_gather(
        jnp.pad(embedding.T, ((0, 0), (0, vocab_lanes - vocab_rows))), "seq", axis=0, tiled=True
    )
    marks = lax.all_gather(jnp.concatenate([exit_flags, target_ids], axis=0), "dp", axis=0)
    gain_one, gain_two, gain_three, gain_exit = gain_columns[:, :4].astype(jnp.float32).T

    def blocks(rows):
        return rows.astype(low).reshape(n_seq, -1, rows.shape[1])

    def fold_up(rows):
        rows = rows.reshape(n_dp, fold_rows, -1)
        rows = jnp.pad(rows, ((0, 0), (0, folds * own_rows - fold_rows), (0, 0)))
        return [
            rows[:, fold * own_rows : (fold + 1) * own_rows].reshape(width, -1)
            for fold in range(folds)
        ]

    def unfold(parts):
        parts = [part.reshape(n_dp, own_rows, -1) for part in parts]
        rows = jnp.concatenate(parts, axis=1)[:, :fold_rows]
        return rows.reshape(n_dp * fold_rows, -1)

    residual_in = hidden_in.reshape(-1, width).T.astype(jnp.float32)
    token_count = residual_in.shape[1]
    states = encoder_in.reshape(-1, width).T
    cotangent = out_cotangent.reshape(-1, width).T
    residual_in, states, cotangent, marks = lax.optimization_barrier(
        (residual_in, states, cotangent, marks)
    )
    residual_in, states = rows_first(residual_in), rows_first(states)
    cotangent = rows_first(cotangent)
    normed_one = norm_columns(residual_in, gain_one).astype(low)
    qkv_one = swap(blocks(contract(self_qkv, normed_one, 0, 0)))
    kv_two = swap(blocks(contract(cross_kv, states, 0, 0)))
    self_places = ((0, 0), (0, own), (0, 2 * own))
    mixture_one = swap(attend(prefix_len, [qkv_one], self_places, own, True))
    mixture_one = mixture_one.reshape(width, token_count)
    after_self = residual_in + contract(self_out, mixture_one, 0, 0)
    normed_two = norm_columns(after_self, gain_two).astype(low)
    q_two = swap(blocks(contract(cross_q, normed_two, 0, 0)))
    cross_places = ((0, 0), (1, 0), (1, own))
    mixture_two = swap(attend(prefix_len, [q_two, kv_two], cross_places, own, False))
    mixture_two = mixture_two.reshape(width, token_count)
    after_cross = after_self + contract(cross_out, mixture_two, 0, 0)
    normed_three = norm_columns(after_cross, gain_three).astype(low)
    gate_pre = contract(gate_full, normed_three, 0, 0)
    up_pre = contract(up_full, normed_three, 0, 0)
    hidden_mid = gated_unit(gate_pre, up_pre).astype(low)
    hidden_folds = fold_up(hidden_mid)
    after_feed = after_cross
    for down, hidden in zip(downs, hidden_folds):
        after_feed = after_feed + contract(down, hidden, 0, 0)
    block_output = after_feed.T.astype(low).reshape(hidden_in.shape)
    normed_exit = rows_first(norm_columns(after_feed, gain_exit).astype(low).T)
    normed_exit, table = lax.optimization_barrier((normed_exit, table))

    tokens = lax.all_gather(normed_exit, "dp", axis=0, tiled=True)
    flag_rows = marks[:, 0].reshape(-1, 1).astype(jnp.float32)
    target_rows = marks[:, 1].reshape(-1, 1) - lax.axis_index("dp") * vocab_rows
    hits = jnp.arange(vocab_lanes)[None, :] == target_rows
    hits = hits & (target_rows < vocab_rows)
    target_terms = contract(hits.astype(low), table, 1, 1).astype(low)
    tokens, target_terms = lax.optimization_barrier((tokens, target_terms))
    shifted, products, parts = exit_rows(tokens, table, vocab_rows)
    picked = jnp.sum(tokens.astype(jnp.float32) * target_terms.astype(jnp.float32), axis=1)
    row_max = parts[:, 0]
    parts = lax.all_gather(jnp.stack([row_max, parts[:, 1], picked]), "dp", axis=0)
    top = jnp.max(parts[:, 0], axis=0)
    log_total = top + jnp.log(jnp.sum(parts[:, 1] * jnp.exp(parts[:, 0] - top), axis=0))
    all_losses = flag_rows[:, 0] * (log_total - jnp.sum(parts[:, 2], axis=0))
    token_losses = lax.dynamic_slice(
        all_losses, (lax.axis_index("dp") * token_count,), (token_count,)
    ).reshape(exit_flags.shape)
    factor = flag_rows * jnp.exp(row_max - log_total)[:, None]
    exit_in_grad = lax.psum_scatter(
        rows_first((factor * products - flag_rows * target_terms.astype(jnp.float32)).astype(low)),
        "dp",
        scatter_dimension=0,
        tiled=True,
    )
    logit_grads = jnp.where(hits, factor * shifted - flag_rows, factor * shifted).astype(low)
    table_terms = contract(tokens, logit_grads, 0, 0).astype(low)
    exit_in_grad, table_terms = lax.optimization_barrier((rows_first(exit_in_grad), table_terms))
    exit_in_grad = rows_first(exit_in_grad.T).astype(jnp.float32)
    table_sums = lax.psum_scatter(table_terms, "seq", scatter_dimension=0, tiled=True)

    feed_grad, full_exit_gain = norm_back(after_feed, gain_exit, exit_in_grad)
    feed_grad = feed_grad + cotangent
    branch_three = feed_grad.astype(low)
    hidden_mid_grad = unfold([contract(down, branch_three, 1, 0) for down in downs])
    unused, gated_pull = jax.vjp(gated_unit, gate_pre, up_pre)
    gate_grad, up_grad = gated_pull(hidden_mid_grad)
    gate_grad, up_grad = gate_grad.astype(low), up_grad.astype(low)
    normed_three_grad = contract(gate_full, gate_grad, 1, 0) + contract(up_full, up_grad, 1, 0)
    cross_grad, full_feed_gain = norm_back(after_cross, gain_three, normed_three_grad)
    cross_grad = cross_grad + feed_grad
    branch_two = cross_grad.astype(low)
    mixture_two_grad = swap(blocks(contract(cross_out, branch_two, 1, 0)))
    q_grad, kv_grad = attend_back(
        prefix_len, [q_two, kv_two], mixture_two_grad, cross_places, False
    )
    q_grad = swap(q_grad).reshape(-1, token_count)
    kv_grad = swap(kv_grad).reshape(-1, token_count)
    encoder_grad = contract(kv_grad, cross_kv, 0, 1).reshape(encoder_in.shape)
    rest_terms = jnp.concatenate(
        [
            contract(normed_two, q_grad, 1, 1).astype(low),
            contract(states, kv_grad, 1, 1).astype(low),
            contract(mixture_two, branch_two, 1, 1).astype(low),
            contract(normed_three, gate_grad, 1, 1).astype(low),
            contract(normed_three, up_grad, 1, 1).astype(low),
        ]
        + [contract(hidden, branch_three, 1, 1).astype(low) for hidden in hidden_folds],
        axis=1,
    )
    self_grad, full_cross_gain = norm_back(after_self, gain_two, contract(cross_q, q_grad, 1, 0))
    self_grad = self_grad + cross_grad
    branch_one = self_grad.astype(low)
    mixture_one_grad = blocks(contract(self_out, branch_one, 1, 0))
    mixture_one_grad, rest_terms = lax.optimization_barrier((mixture_one_grad, rest_terms))
    rest_terms, table_sums = lax.optimization_barrier((rest_terms, table_sums))
    embedding_grad = table_sums[:, :vocab_rows].astype(jnp.float32).T
    rest_terms = lax.psum_scatter(rest_terms, "dp", scatter_dimension=0, tiled=True)
    (qkv_grad,) = attend_back(prefix_len, [qkv_one], swap(mixture_one_grad), self_places, True)
    qkv_grad = swap(qkv_grad).reshape(-1, token_count)
    normed_one_grad = contract(self_qkv, qkv_grad, 1, 0)
    input_grad, full_self_gain = norm_back(residual_in, gain_one, normed_one_grad)
    hidden_grad = (input_grad + self_grad).T.reshape(hidden_in.shape)
    gain_terms = jnp.stack(
        [full_self_gain, full_cross_gain, full_feed_gain, full_exit_gain], axis=1
    ).astype(low)
    gain_terms = jnp.pad(gain_terms, ((0, 0), (0, GAIN_LANES - gain_terms.shape[1])))
    self_terms = jnp.concatenate(
        [
            contract(normed_one, qkv_grad, 1, 1).astype(low),
            contract(mixture_one, branch_one, 1, 1).astype(low),
            gain_terms,
        ],
        axis=1,
    )
    self_terms, rest_terms = lax.optimization_barrier((self_terms, rest_terms))
    self_terms = lax.psum_scatter(self_terms, "dp", scatter_dimension=0, tiled=True)
    (
        cross_query_grad,
        cross_key_grad,
        cross_value_grad,
        cross_output_grad,
        feed_gate_grad,
        feed_up_grad,
        *down_sums,
    ) = deliver(rest_terms, near_sizes[2:] + feed_sizes, 0, (own,) * 4 + feed_sizes)
    down_grad = jnp.concatenate(down_sums, axis=0)[:fold_rows]
    self_query_grad, self_key_grad, self_value_grad, self_output_grad, gain_sums = deliver(
        self_terms, near_sizes[:2], GAIN_LANES, (own,) * 4 + (GAIN_LANES,)
    )
    gain_sums = gain_sums[:, :4].T
    return (
        block_output,
        token_losses,
        hidden_grad,
        encoder_grad,
        gain_sums[0],
        self_query_grad,
        self_key_grad,
        self_value_grad,
        self_output_grad,
        gain_sums[1],
        cross_query_grad,
        cross_key_grad,
        cross_value_grad,
        cross_output_grad,
        gain_sums[2],
        feed_gate_grad,
        feed_up_grad,
        down_grad,
        gain_sums[3],
        embedding_grad,
    )


def solution(mesh):
    tokens = P("dp", "seq")
    rows = P("dp")
    matrix = P("dp", "seq")
    block = P("dp", "seq", None)
    attention = (rows,) + (matrix,) * 4
    return jax.shard_map(
        per_device,
        mesh=mesh,
        in_specs=(block, block, rows, tokens, tokens, block)
        + attention * 2
        + (rows, matrix, matrix, matrix, rows, matrix),
        out_specs=(block, tokens, block, block)
        + attention * 2
        + (rows, matrix, matrix, matrix, rows, matrix),
        check_vma=False,
    )
```

time: 1210 us -> 838 us (0.69)
  waiting for transfers between devices: 762 us -> 289 us
  blocking collectives: 76.7 us -> 172 us
  Pallas kernels: 56.4 us -> 133 us
  local copies, waits for them, and re-layouts: 69.1 us -> 27.8 us
  matrix products: 135 us -> 115 us
    reduce_scatter x6 -> x4, waiting for transfers between devices: 359 us -> 96.2 us  [the longest x1 39.3 us: per_device(): lax.psum_scatter(self_terms, 'dp', scatter_dimension=0, tiled=True)]
    all_gather x5 -> x3, waiting for transfers between devices: 249 us -> 35.6 us  [the longest x1 28.1 us: per_device(): lax.all_gather(jnp.pad(embedding.T, ((0, 0), (0, vocab_lanes - vocab_rows...]
    all_to_all x3 -> x6, blocking collectives: 58.2 us -> 153 us  [swap(): return lax.all_to_all(pieces, 'seq', 0, 0, tiled=True)]
    pallas_call x4 -> x13, Pallas kernels: 56.4 us -> 133 us  [the longest x1 57.2 us: exit_rows(): pl.pallas_call(functools.partial(exit_kernel, rows=rows), grid=(count //...]
    dot_general x21 -> x0, matrix products: 65.3 us -> none  [mix(): jnp.einsum(spec, first_op, second_op, preferred_element_type=jnp.float32)]
    dot_general x3 -> x32, matrix products: 69.5 us -> 115 us  [contract(): lax.dot_general(first_op, second_op, (((first_dim,), (second_dim,)), ((),...]
    all_to_all x7 -> x8, waiting for transfers between devices: 118 us -> 142 us  [swap(): return lax.all_to_all(pieces, 'seq', 0, 0, tiled=True)]
    all_gather x1, waiting for transfers between devices: 35.7 us -> 14.6 us  [per_device(): tokens = lax.all_gather(normed_exit, 'dp', axis=0, tiled=True)]
  transfers between devices with their start and end apart: 19 -> 16, of which waited for: 15 -> 13; matrix products, arithmetic and copies ran while one was open for 14% -> 18% of each run, Pallas kernels for 5% -> 8%
where the time goes in v3:
time: 838 us; the launch traced here: 829 us
  waiting for transfers between devices  289 us (34%)
  blocking collectives  172 us (21%)
  Pallas kernels  133 us (16%)
  matrix products  115 us (14%)
  starting transfers between devices  45.1 us (5%)
  other arithmetic  32 us (4%)
  local copies, waits for them, and re-layouts  27.8 us (3%)
  between operations  16 us (2%)
    all_to_all x6, blocking collectives, swap(): return lax.all_to_all(pieces, 'seq', 0, 0, tiled=True)  153 us
    all_to_all x8, waiting for transfers between devices, swap(): return lax.all_to_all(pieces, 'seq', 0, 0, tiled=True)  142 us
    dot_general x32, matrix products, contract(): lax.dot_general(first_op, second_op, (((first_dim,), (second_dim,)), ((),...  115 us
    pallas_call x1, Pallas kernels, exit_rows(): pl.pallas_call(functools.partial(exit_kernel, rows=rows), grid=(count //...  57.2 us
    all_to_all x8, starting transfers between devices, swap(): return lax.all_to_all(pieces, 'seq', 0, 0, tiled=True)  44.9 us
    reduce_scatter x1, waiting for transfers between devices, per_device(): lax.psum_scatter(self_terms, 'dp', scatter_dimension=0, tiled=True)  39.3 us
    reduce_scatter x1, waiting for transfers between devices, per_device(): lax.psum_scatter(rest_terms, 'dp', scatter_dimension=0, tiled=True)  39 us
    pallas_call x2, Pallas kernels, attend_back(): pl.pallas_call(functools.partial(attend_back_kernel, places=places, count...  35.9 us
  transfers between devices with their start and end apart: 16, of which 13 were waited for; matrix products, arithmetic and copies ran while one was open for 18% of the time, Pallas kernels for 8%

profile of v3, /device:TPU:8, one launch (start us, length us, event | category | flops | bytes accessed | tf_op | source)
XLA Modules:
  0.0 829.1 jit_solution(40404594134088017)
XLA Ops:
  12.6 5.4 all-to-all-start
  18.9 24.5 %all-to-all-done.refs_0_ = bf16[4,96,1536]{2,1,0:T(8,128)(2,1)S(1)} async-done(((bf16[4,96,1536]{2,1,0:T(8,128)(2,1)}), bf16[4,96,1536]{2,1,0:T(8,128)(2,1)S(1)}, u32[]{:S(2)}, u32[]{:S(2)}) %all-to-all-start) | async-done | bytes 1179680 | tf_op jit(solution)/shard_map/all_to_all | solution.py:51
  50.0 36.2 %all_to_all.70.refs_0_ = bf16[4,96,1600]{2,1,0:T(8,128)(2,1)} all-to-all(bf16[4,96,1600]{2,1,0:T(8,128)(2,1)} %shard_map.369), channel_id=1, replica_groups=mesh['dp'=8,'seq'=4] {'seq'}, dimensions={0} | all-to-all | bytes 2457600 | tf_op jit(solution)/shard_map/all_to_all | solution.py:51
  91.8 9.2 %all-gather.2 = s32[8,2,256]{2,1,0:T(2,128)S(1)} all-gather(s32[1,2,256]{2,1,0:T(2,128)S(1)} %add_bitcast_fusion), channel_id=2, replica_groups=mesh['dp'=8,'seq'=4] {'dp'}, dimensions={0}, use_global_device_ids=true | all-gather | bytes 18432 | tf_op jit(solution)/shard_map/all_gather | solution.py:370
  101.2 7.4 all-gather.9.cloned.1.call-done
  110.4 4.3 convolution_convert_fusion.1
  114.7 5.1 all-to-all-start.1
  120.5 25.0 %all-to-all-done.1.refs_0_ = bf16[4,576,256]{2,1,0:T(8,128)(2,1)S(1)} async-done(((bf16[4,576,256]{2,1,0:T(8,128)(2,1)}), bf16[4,576,256]{2,1,0:T(8,128)(2,1)S(1)}, u32[]{:S(2)}, u32[]{:S(2)}) %all-to-all-start.1) | async-done | bytes 1179680 | tf_op jit(solution)/shard_map/all_to_all | solution.py:51
  146.6 10.6 %shard_map.367 = bf16[4,192,256]{2,1,0:T(8,128)(2,1)} custom-call(s32[1]{0:T(128)S(6)} %copy.162.prefix_ref, bf16[4,576,256]{2,1,0:T(8,128)(2,1)} %copy-done.1), custom_call_target="tpu_custom_call" | custom-call | tf_op jit(solution)/shard_map/pallas_call | solution.py:285
  157.2 6.6 all-to-all-start.2
  163.8 3.4 convolution_convert_fusion.5
  167.2 5.4 all-to-all-done.2
  172.6 5.9 all-to-all-start.4
  182.8 31.4 %all-to-all-done.4.refs_1_ = bf16[4,384,256]{2,1,0:T(8,128)(2,1)S(1)} async-done(((bf16[4,384,256]{2,1,0:T(8,128)(2,1)}), bf16[4,384,256]{2,1,0:T(8,128)(2,1)S(1)}, u32[]{:S(2)}, u32[]{:S(2)}) %all-to-all-start.4) | async-done | bytes 786464 | tf_op jit(solution)/shard_map/all_to_all | solution.py:51
  214.2 24.5 %all_to_all.71.refs_0_ = bf16[4,192,256]{2,1,0:T(8,128)(2,1)} all-to-all(bf16[4,192,256]{2,1,0:T(8,128)(2,1)S(1)} %bitcast.150), channel_id=1, replica_groups=mesh['dp'=8,'seq'=4] {'seq'}, dimensions={0} | all-to-all | bytes 786432 | tf_op jit(solution)/shard_map/all_to_all | solution.py:51
  238.7 10.1 %shard_map.368 = bf16[4,192,256]{2,1,0:T(8,128)(2,1)} custom-call(s32[1]{0:T(128)S(6)} %copy.162.prefix_ref, bf16[4,192,256]{2,1,0:T(8,128)(2,1)} %all_to_all.71.refs_0_, bf16[4,384,256]{2,1,0:T(8,128)(2,1)} %copy-done.4), custom_call_target="tpu_custom_call" | custom-call | tf_op jit(solution)/shard_map/pallas_call | solution.py:285
  248.8 23.6 %all_to_all.72 = bf16[4,192,256]{2,1,0:T(8,128)(2,1)S(1)} all-to-all(bf16[4,192,256]{2,1,0:T(8,128)(2,1)} %shard_map.368), channel_id=1, replica_groups=mesh['dp'=8,'seq'=4] {'seq'}, dimensions={0} | all-to-all | bytes 786432 | tf_op jit(solution)/shard_map/all_to_all | solution.py:51
  274.6 3.1 fusion.35
  284.9 28.1 %all-gather.13.cloned.1.call-done.table_ref = bf16[768,4096]{1,0:T(8,128)(2,1)} async-done(((bf16[192,4096]{1,0:T(8,128)(2,1)}), bf16[768,4096]{1,0:T(8,128)(2,1)}) %all-gather.13.cloned.1.call-update) | async-done | bytes 6291472 | tf_op jit(solution)/shard_map/all_gather | solution.py:367
  314.6 19.6 %fusion.23 = bf16[2048,768]{1,0:T(8,128)(2,1)} fusion(bf16[768,4096]{1,0:T(8,128)(2,1)} %all-gather.13.cloned.1.call-done.table_ref, s32[2048]{0:T(1024)S(1)} %bitcast.161, pred[2048]{0:T(1024)(128)(4,1)S(1)} %broadcast_compare_fusion), kind=kOutput, calls=%fused_computation.29 | convolution fusion | flops 12903251968 | bytes 9447424 | tf_op jit(solution)/shard_map/dot_general | solution.py:21
  334.3 14.6 %all-gather.15.cloned.1.call-done.token_ref = bf16[2048,768]{1,0:T(8,128)(2,1)} async-done(((bf16[256,768]{1,0:T(8,128)(2,1)}), bf16[2048,768]{1,0:T(8,128)(2,1)}) %all-gather.15.cloned.1.call-update) | async-done | bytes 3145744 | tf_op jit(solution)/shard_map/all_gather | solution.py:423
  348.8 57.2 %shard_map.371 = (bf16[2048,4096]{1,0:T(8,128)(2,1)}, f32[2048,768]{1,0:T(8,128)}, f32[2048,128]{1,0:T(8,128)}) custom-call(bf16[2048,768]{1,0:T(8,128)(2,1)} %all-gather.15.cloned.1.call-done.token_ref, bf16[768,4096]{1,0:T(8,128)(2,1)} %all-gather.13.cloned.1.call-done.table_ref), custom_call_target="tpu_custom_call" | custom-call | tf_op jit(solution)/shard_map/pallas_call | solution.py:261
  406.0 3.8 fusion.16
  410.8 9.3 %all-gather.3 = f32[8,3,2048]{2,1,0:T(4,128)S(1)} all-gather(f32[1,3,2048]{2,1,0:T(4,128)S(1)} %maximum_bitcast_fusion), channel_id=3, replica_groups=mesh['dp'=8,'seq'=4] {'dp'}, dimensions={0}, use_global_device_ids=true | all-gather | bytes 221184 | tf_op jit(solution)/shard_map/all_gather | solution.py:433
  424.8 4.5 fusion.18
  430.0 27.6 %fusion.13 = bf16[768,4096]{1,0:T(8,128)(2,1)} fusion(bf16[2048,768]{1,0:T(8,128)(2,1)} %all-gather.15.cloned.1.call-done.token_ref, bf16[2048,4096]{1,0:T(8,128)(2,1)} %get-tuple-element.64, f32[2048]{0:T(1024)S(1)} %bitcast.154, f32[2048]{0:T(1024)S(1)} %multiply_reduce_fusion, s32[2048]{0:T(1024)S(1)} %bitcast.162, pred[2048]{0:T(1024)(128)(4,1)S(1)} %copy-done.69), kind=kOutput, calls=%fused_computation.16 | convolution fusion | flops 12946767872 | bytes 26241024 | tf_op jit(solution)/shard_map/dot_general | solution.py:21
  457.6 18.0 %reduce-scatter.5.cloned.1.call-done = bf16[256,768]{1,0:T(8,128)(2,1)} async-done(((bf16[2048,768]{1,0:T(8,128)(2,1)}), bf16[256,768]{1,0:T(8,128)(2,1)}) %reduce-scatter.5.cloned.1.call-update) | async-done | bytes 393232 | tf_op jit(solution)/shard_map/reduce_scatter | solution.py:441
  488.8 3.6 fusion.29
  498.2 27.0 %all_to_all.73.refs_2_ = bf16[4,192,256]{2,1,0:T(8,128)(2,1)} all-to-all(bf16[4,192,256]{2,1,0:T(8,128)(2,1)S(1)} %bitcast.151), channel_id=1, replica_groups=mesh['dp'=8,'seq'=4] {'seq'}, dimensions={0} | all-to-all | bytes 786432 | tf_op jit(solution)/shard_map/all_to_all | solution.py:51
  525.2 17.6 %shard_map.372 = (bf16[4,192,256]{2,1,0:T(8,128)(2,1)}, bf16[4,384,256]{2,1,0:T(8,128)(2,1)}) custom-call(s32[1]{0:T(128)S(6)} %copy.162.prefix_ref, bf16[4,192,256]{2,1,0:T(8,128)(2,1)} %all_to_all.71.refs_0_, bf16[4,384,256]{2,1,0:T(8,128)(2,1)} %copy-done.4, bf16[4,192,256]{2,1,0:T(8,128)(2,1)} %all_to_all.73.refs_2_), custom_call_target="tpu_custom_call" | custom-call | tf_op jit(solution)/shard_map/pallas_call | solution.py:296
  542.8 28.4 %all_to_all.74 = bf16[4,192,256]{2,1,0:T(8,128)(2,1)S(1)} all-to-all(bf16[4,192,256]{2,1,0:T(8,128)(2,1)} %get-tuple-element.67), channel_id=1, replica_groups=mesh['dp'=8,'seq'=4] {'seq'}, dimensions={0} | all-to-all | bytes 786432 | tf_op jit(solution)/shard_map/all_to_all | solution.py:51
  571.1 6.2 all-to-all-start.9
  584.3 30.3 %all-to-all-done.9 = bf16[4,384,256]{2,1,0:T(8,128)(2,1)S(1)} async-done(((bf16[4,384,256]{2,1,0:T(8,128)(2,1)}), bf16[4,384,256]{2,1,0:T(8,128)(2,1)S(1)}, u32[]{:S(2)}, u32[]{:S(2)}) %all-to-all-start.9) | async-done | bytes 786464 | tf_op jit(solution)/shard_map/all_to_all | solution.py:51
  615.5 3.2 fusion.22
  624.2 2.8 fusion.20
  632.9 13.5 %all_to_all.75.refs_1_ = bf16[4,192,256]{2,1,0:T(8,128)(2,1)} all-to-all(bf16[4,192,256]{2,1,0:T(8,128)(2,1)S(1)} %bitcast.147), channel_id=1, replica_groups=mesh['dp'=8,'seq'=4] {'seq'}, dimensions={0} | all-to-all | bytes 786432 | tf_op jit(solution)/shard_map/all_to_all | solution.py:51
  646.5 18.4 %shard_map.373 = bf16[4,576,256]{2,1,0:T(8,128)(2,1)} custom-call(s32[1]{0:T(128)S(6)} %copy.162.prefix_ref, bf16[4,576,256]{2,1,0:T(8,128)(2,1)} %copy-done.1, bf16[4,192,256]{2,1,0:T(8,128)(2,1)} %all_to_all.75.refs_1_), custom_call_target="tpu_custom_call" | custom-call | tf_op jit(solution)/shard_map/pallas_call | solution.py:296
  664.8 5.3 all-to-all-start.11
  671.7 18.9 %all-to-all-done.11 = bf16[4,576,256]{2,1,0:T(8,128)(2,1)S(1)} async-done(((bf16[4,576,256]{2,1,0:T(8,128)(2,1)}), bf16[4,576,256]{2,1,0:T(8,128)(2,1)S(1)}, u32[]{:S(2)}, u32[]{:S(2)}) %all-to-all-start.11) | async-done | bytes 1179680 | tf_op jit(solution)/shard_map/all_to_all | solution.py:51
  690.6 4.0 multiply_reduce_fusion.3
  698.6 39.0 %reduce-scatter.9.cloned.1.call-done.refs_0_ = bf16[96,9472]{1,0:T(8,128)(2,1)} async-done(((bf16[768,9472]{1,0:T(8,128)(2,1)}), bf16[96,9472]{1,0:T(8,128)(2,1)}) %reduce-scatter.9.cloned.1.call-update) | async-done | bytes 1818640 | tf_op jit(solution)/shard_map/reduce_scatter | solution.py:489
  737.6 3.0 shard_map.376
  740.7 5.1 all-to-all-start.13
  749.1 4.1 fusion.53
  756.6 39.3 %reduce-scatter.11.cloned.1.call-done.refs_0_ = bf16[96,3200]{1,0:T(8,128)(2,1)} async-done(((bf16[768,3200]{1,0:T(8,128)(2,1)}), bf16[96,3200]{1,0:T(8,128)(2,1)}) %reduce-scatter.11.cloned.1.call-update) | async-done | bytes 614416 | tf_op jit(solution)/shard_map/reduce_scatter | solution.py:508
  798.0 5.1 all-to-all-start.12
  803.1 3.4 convert_bitcast_fusion
  810.9 6.7 all-to-all-done.12.terms_ref
  (273 shorter events, 103.8 us)
Async XLA Ops:
  7.2 10.9 %copy-start.74 = (bf16[96]{0:T(256)(128)(2,1)S(1)}, bf16[96]{0:T(256)(128)(2,1)}, u32[]{:S(2)}) copy-start(bf16[96]{0:T(256)(128)(2,1)} %param.42) | copy-start | bytes 580
  7.2 10.9 %copy-start.75 = (bf16[96]{0:T(256)(128)(2,1)S(1)}, bf16[96]{0:T(256)(128)(2,1)}, u32[]{:S(2)}) copy-start(bf16[96]{0:T(256)(128)(2,1)} %param.38) | copy-start | bytes 580
  7.2 10.9 %copy-start.76 = (bf16[96]{0:T(256)(128)(2,1)S(1)}, bf16[96]{0:T(256)(128)(2,1)}, u32[]{:S(2)}) copy-start(bf16[96]{0:T(256)(128)(2,1)} %param.33) | copy-start | bytes 580
  7.2 10.9 %copy-start.77 = (bf16[96]{0:T(256)(128)(2,1)S(1)}, bf16[96]{0:T(256)(128)(2,1)}, u32[]{:S(2)}) copy-start(bf16[96]{0:T(256)(128)(2,1)} %param.28) | copy-start | bytes 580
  12.6 34.4 %copy-start.44 = (bf16[256,192]{0,1:T(8,128)(2,1)S(1)}, bf16[256,192]{0,1:T(8,128)(2,1)}, u32[]{:S(2)}) copy-start(bf16[256,192]{0,1:T(8,128)(2,1)} %param.41) | copy-start | bytes 294916
  12.6 30.7 %all-to-all-start = ((bf16[4,96,1536]{2,1,0:T(8,128)(2,1)}), bf16[4,96,1536]{2,1,0:T(8,128)(2,1)S(1)}, u32[]{:S(2)}, u32[]{:S(2)}) async-start(bf16[4,96,1536]{2,1,0:T(8,128)(2,1)} %shard_map.365), calls=%async_computation | async-start | bytes 2359296 | tf_op jit(solution)/shard_map/all_to_all | solution.py:51
  18.1 90.5 %all-gather.9.cloned.1.call-start = ((), (), s32[]{:S(2)}) async-start(), calls=%async_computation.18 | async-start | bytes 10838016 | tf_op jit(solution)/shard_map/all_gather | solution.py:109
  47.0 227.5 %all-gather.11.cloned.1.call-start = ((), (), s32[]{:S(2)}) async-start(), calls=%async_computation.19 | async-start | bytes 11059200 | tf_op jit(solution)/shard_map/all_gather | solution.py:109
  50.0 38.8 %copy-start.27 = (bf16[4016,192]{0,1:T(8,128)(2,1)S(1)}, bf16[4016,192]{0,1:T(8,128)(2,1)}, u32[]{:S(2)}) copy-start(bf16[4016,192]{0,1:T(8,128)(2,1)} %param.43) | copy-start | bytes 4626436
  88.7 224.3 %all-gather.13.cloned.1.call-start = ((), (), s32[]{:S(2)}) async-start(), calls=%async_computation.20 | async-start | bytes 7864320 | tf_op jit(solution)/shard_map/all_gather | solution.py:367
  90.7 73.1 %copy-start.25 = (bf16[1,256,768]{1,2,0:T(8,128)(2,1)}, bf16[1,256,768]{1,2,0:T(8,128)(2,1)S(1)}, u32[]{:S(2)}) copy-start(bf16[1,256,768]{1,2,0:T(8,128)(2,1)S(1)} %copy.115) | copy-start | bytes 1179652
  101.2 7.4 copy-start.56
  101.2 13.5 %copy-start.54 = (f32[256]{0:T(256)}, f32[256]{0:T(256)S(1)}, u32[]{:S(2)}) copy-start(f32[256]{0:T(256)S(1)} %fusion.93) | copy-start | bytes 3076
  110.4 70.1 %copy-start.52 = (f32[768]{0:T(1024)}, f32[768]{0:T(1024)S(1)}, u32[]{:S(2)}) copy-start(f32[768]{0:T(1024)S(1)} %get-tuple-element.182) | copy-start | bytes 9220
  110.4 163.9 %copy-start.46 = (f32[768]{0:T(1024)}, f32[768]{0:T(1024)S(1)}, u32[]{:S(2)}) copy-start(f32[768]{0:T(1024)S(1)} %get-tuple-element.181) | copy-start | bytes 9220
  114.7 30.8 %all-to-all-start.1 = ((bf16[4,576,256]{2,1,0:T(8,128)(2,1)}), bf16[4,576,256]{2,1,0:T(8,128)(2,1)S(1)}, u32[]{:S(2)}, u32[]{:S(2)}) async-start(bf16[4,576,256]{2,1,0:T(8,128)(2,1)} %bitcast.12), calls=%async_computation.1 | async-start | bytes 2359296 | tf_op jit(solution)/shard_map/all_to_all | solution.py:51
  157.2 15.4 %all-to-all-start.2 = ((bf16[4,192,256]{2,1,0:T(8,128)(2,1)}), bf16[4,192,256]{2,1,0:T(8,128)(2,1)S(1)}, u32[]{:S(2)}, u32[]{:S(2)}) async-start(bf16[4,192,256]{2,1,0:T(8,128)(2,1)} %shard_map.367), calls=%async_computation.2 | async-start | bytes 786432 | tf_op jit(solution)/shard_map/all_to_all | solution.py:51
  172.6 10.2 %copy-start.23 = (bf16[4,192,256]{2,1,0:T(8,128)(2,1)}, bf16[4,192,256]{2,1,0:T(8,128)(2,1)S(1)}, u32[]{:S(2)}) copy-start(bf16[4,192,256]{2,1,0:T(8,128)(2,1)S(1)} %all-to-all-done.2) | copy-start | bytes 1179652
  172.6 41.6 %all-to-all-start.4 = ((bf16[4,384,256]{2,1,0:T(8,128)(2,1)}), bf16[4,384,256]{2,1,0:T(8,128)(2,1)S(1)}, u32[]{:S(2)}, u32[]{:S(2)}) async-start(bf16[4,384,256]{2,1,0:T(8,128)(2,1)} %bitcast.15), calls=%async_computation.4 | async-start | bytes 1572864 | tf_op jit(solution)/shard_map/all_to_all | solution.py:51
  178.6 170.3 %all-gather.15.cloned.1.call-start = ((), (), s32[]{:S(2)}) async-start(), calls=%async_computation.21 | async-start | bytes 3538944 | tf_op jit(solution)/shard_map/all_gather | solution.py:423
  180.4 91.9 %copy-start.63 = (f32[256]{0:T(256)}, f32[256]{0:T(256)S(1)}, u32[]{:S(2)}) copy-start(f32[256]{0:T(256)S(1)} %get-tuple-element.206) | copy-start | bytes 3076
  180.4 91.9 %copy-start.35 = (f32[768,256]{1,0:T(8,128)}, f32[768,256]{1,0:T(8,128)S(1)}, u32[]{:S(2)}) copy-start(f32[768,256]{1,0:T(8,128)S(1)} %get-tuple-element.207) | copy-start | bytes 2359300
  180.4 91.9 %copy-start.61 = (f32[256]{0:T(256)}, f32[256]{0:T(256)S(1)}, u32[]{:S(2)}) copy-start(f32[256]{0:T(256)S(1)} %fusion.94) | copy-start | bytes 3076
  214.2 24.5 %copy-start.4 = (bf16[4,384,256]{2,1,0:T(8,128)(2,1)}, bf16[4,384,256]{2,1,0:T(8,128)(2,1)S(1)}, u32[]{:S(2)}) copy-start(bf16[4,384,256]{2,1,0:T(8,128)(2,1)S(1)} %all-to-all-done.4.refs_1_) | copy-start | bytes 2359300
  283.8 29.4 %copy-start.67 = (f32[256]{0:T(256)}, f32[256]{0:T(256)S(1)}, u32[]{:S(2)}) copy-start(f32[256]{0:T(256)S(1)} %get-tuple-element.212) | copy-start | bytes 3076
  283.8 29.3 %copy-start.50 = (f32[256]{0:T(256)}, f32[256]{0:T(256)S(1)}, u32[]{:S(2)}) copy-start(f32[256]{0:T(256)S(1)} %fusion.96) | copy-start | bytes 3076
  313.1 162.5 %reduce-scatter.5.cloned.1.call-start = ((), (), s32[]{:S(2)}) async-start(), calls=%async_computation.22 | async-start | bytes 3538944 | tf_op jit(solution)/shard_map/reduce_scatter | solution.py:441
  313.2 21.1 %copy-start.48 = (s32[8,1,256]{2,1,0:T(1,128)}, s32[8,1,256]{2,1,0:T(1,128)S(1)}, u32[]{:S(2)}) copy-start(s32[8,1,256]{2,1,0:T(1,128)S(1)} %get-tuple-element.204) | copy-start | bytes 24580
  314.6 19.6 %copy-start.68 = (pred[2048]{0:T(1024)(128)(4,1)}, pred[2048]{0:T(1024)(128)(4,1)S(1)}, u32[]{:S(2)}) copy-start(pred[2048]{0:T(1024)(128)(4,1)S(1)} %broadcast_compare_fusion) | copy-start | bytes 6148
  420.9 8.5 %copy-start.45 = (f32[2048]{0:T(1024)}, f32[2048]{0:T(1024)S(1)}, u32[]{:S(2)}) copy-start(f32[2048]{0:T(1024)S(1)} %log_add_fusion) | copy-start | bytes 24580
  429.4 202.6 %reduce-scatter.7.cloned.1.call-start = ((), (), s32[]{:S(2)}) async-start(), calls=%async_computation.23 | async-start | bytes 7864320 | tf_op jit(solution)/shard_map/reduce_scatter | solution.py:451
  457.6 21.5 %copy-start.5 = (f32[1,256,768]{1,2,0:T(8,128)S(1)}, f32[1,256,768]{1,2,0:T(8,128)}, u32[]{:S(2)}) copy-start(f32[1,256,768]{1,2,0:T(8,128)} %copy.116) | copy-start | bytes 2359300
  496.4 81.0 %copy-start.36 = (f32[768,256]{1,0:T(8,128)S(1)}, f32[768,256]{1,0:T(8,128)}, u32[]{:S(2)}) copy-start(f32[768,256]{1,0:T(8,128)} %copy-done.35) | copy-start | bytes 2359300
  496.4 81.0 %copy-start.53 = (f32[768]{0:T(1024)S(1)}, f32[768]{0:T(1024)}, u32[]{:S(2)}) copy-start(f32[768]{0:T(1024)} %copy-done.52) | copy-start | bytes 9220
  542.8 37.1 %copy-start.7 = (f32[768,256]{1,0:T(8,128)S(1)}, f32[768,256]{1,0:T(8,128)}, u32[]{:S(2)}) copy-start(f32[768,256]{1,0:T(8,128)} %copy-done.6) | copy-start | bytes 2359300
  571.1 8.8 %copy-start.42 = (bf16[4,192,256]{2,1,0:T(8,128)(2,1)}, bf16[4,192,256]{2,1,0:T(8,128)(2,1)S(1)}, u32[]{:S(2)}) copy-start(bf16[4,192,256]{2,1,0:T(8,128)(2,1)S(1)} %all_to_all.74) | copy-start | bytes 1179652
  571.1 43.4 %all-to-all-start.9 = ((bf16[4,384,256]{2,1,0:T(8,128)(2,1)}), bf16[4,384,256]{2,1,0:T(8,128)(2,1)S(1)}, u32[]{:S(2)}, u32[]{:S(2)}) async-start(bf16[4,384,256]{2,1,0:T(8,128)(2,1)} %get-tuple-element.68), calls=%async_computation.10 | async-start | bytes 1572864 | tf_op jit(solution)/shard_map/all_to_all | solution.py:51
  577.3 160.3 %reduce-scatter.9.cloned.1.call-start = ((), (), s32[]{:S(2)}) async-start(), calls=%async_computation.24 | async-start | bytes 16367616 | tf_op jit(solution)/shard_map/reduce_scatter | solution.py:489
  632.9 37.2 %copy-start.60 = (bf16[768]{0:T(1024)(128)(2,1)S(1)}, bf16[768]{0:T(1024)(128)(2,1)}, u32[]{:S(2)}) copy-start(bf16[768]{0:T(1024)(128)(2,1)} %get-tuple-element.176) | copy-start | bytes 4612
  632.9 37.2 %copy-start.70 = (bf16[768]{0:T(1024)(128)(2,1)S(1)}, bf16[768]{0:T(1024)(128)(2,1)}, u32[]{:S(2)}) copy-start(bf16[768]{0:T(1024)(128)(2,1)} %get-tuple-element.174) | copy-start | bytes 4612
  632.9 37.2 %copy-start.71 = (bf16[768]{0:T(1024)(128)(2,1)S(1)}, bf16[768]{0:T(1024)(128)(2,1)}, u32[]{:S(2)}) copy-start(bf16[768]{0:T(1024)(128)(2,1)} %get-tuple-element.172) | copy-start | bytes 4612
  632.9 37.2 %copy-start.24 = (bf16[4,192,256]{2,1,0:T(8,128)(2,1)S(1)}, bf16[4,192,256]{2,1,0:T(8,128)(2,1)}, u32[]{:S(2)}) copy-start(bf16[4,192,256]{2,1,0:T(8,128)(2,1)} %copy-done.23) | copy-start | bytes 1179652
  646.5 44.1 %copy-start.55 = (f32[256]{0:T(256)S(1)}, f32[256]{0:T(256)}, u32[]{:S(2)}) copy-start(f32[256]{0:T(256)} %copy-done.54) | copy-start | bytes 3076
  664.8 25.8 %all-to-all-start.11 = ((bf16[4,576,256]{2,1,0:T(8,128)(2,1)}), bf16[4,576,256]{2,1,0:T(8,128)(2,1)S(1)}, u32[]{:S(2)}, u32[]{:S(2)}) async-start(bf16[4,576,256]{2,1,0:T(8,128)(2,1)} %shard_map.373), calls=%async_computation.12 | async-start | bytes 2359296 | tf_op jit(solution)/shard_map/all_to_all | solution.py:51
  670.1 125.8 %reduce-scatter.11.cloned.1.call-start = ((), (), s32[]{:S(2)}) async-start(), calls=%async_computation.25 | async-start | bytes 5529600 | tf_op jit(solution)/shard_map/reduce_scatter | solution.py:508
  740.7 57.3 %all-to-all-start.13 = ((bf16[4,96,2368]{2,1,0:T(8,128)(2,1)}), bf16[4,96,2368]{2,1,0:T(8,128)(2,1)S(1)}, u32[]{:S(2)}, u32[]{:S(2)}) async-start(bf16[4,96,2368]{2,1,0:T(8,128)(2,1)} %shard_map.376), calls=%async_computation.17 | async-start | bytes 3735552 | tf_op jit(solution)/shard_map/all_to_all | solution.py:51
  798.0 8.6 %copy-start.3 = (bf16[4,96,2368]{2,1,0:T(8,128)(2,1)}, bf16[4,96,2368]{2,1,0:T(8,128)(2,1)S(1)}, u32[]{:S(2)}) copy-start(bf16[4,96,2368]{2,1,0:T(8,128)(2,1)S(1)} %all-to-all-done.13.terms_ref) | copy-start | bytes 5455876
  798.0 19.7 %all-to-all-start.12 = ((bf16[4,96,896]{2,1,0:T(8,128)(2,1)}), bf16[4,96,896]{2,1,0:T(8,128)(2,1)S(1)}, u32[]{:S(2)}, u32[]{:S(2)}) async-start(bf16[4,96,896]{2,1,0:T(8,128)(2,1)} %shard_map.374), calls=%async_computation.16 | async-start | bytes 1376256 | tf_op jit(solution)/shard_map/all_to_all | solution.py:51
  (50 other events, 148.9 us)
Sparse Core Ops, SparseCore 0:
  47.1 61.4 all-gather.8
  110.5 60.3 all-gather.10
  173.0 139.9 all-gather.12
  315.4 33.3 all-gather.14
  429.5 46.0 reduce-scatter.4
  477.7 144.4 reduce-scatter.6
  632.1 105.4 reduce-scatter.8
  741.1 54.7 reduce-scatter.10

commit v4 on v3

--- a/solution.py
+++ b/solution.py
@@ -6,6 +6,7 @@
 from jax.experimental import pallas as pl
 from jax.experimental.layout import Layout, with_layout_constraint
 from jax.experimental.pallas import tpu as pltpu
+from jax.sharding import Mesh
 from jax.sharding import PartitionSpec as P
 
 HD = 64
@@ -15,6 +16,7 @@
 
 norm_eps = 1e-06
 masked_score = -1000000000.0
+dp = ("group", "part")
 
 
 def contract(first_op, second_op, first_dim, second_dim):
@@ -47,8 +49,30 @@
     return jax.nn.gelu(gate_in, approximate=True) * upward
 
 
-def swap(pieces):
-    return lax.all_to_all(pieces, "seq", 0, 0, tiled=True)
+def swap(pieces, axis):
+    return lax.all_to_all(pieces, axis, 0, 0, tiled=True)
+
+
+def relocate(block):
+    size = lax.axis_size("seq")
+    pairs = [
+        ((group * size + part) * size + at, (group * size + at) * size + part)
+        for group in range(lax.axis_size("group"))
+        for part in range(size)
+        for at in range(size)
+    ]
+    return lax.ppermute(block, ("group", "part", "seq"), pairs)
+
+
+def shift(block, by):
+    size = lax.axis_size("seq")
+    return lax.ppermute(block, "seq", [(at, (at + by) % size) for at in range(size)])
+
+
+def spot(by):
+    size = lax.axis_size("seq")
+    at = lax.axis_index("seq") + by % size
+    return jnp.where(at >= size, at - size, at)
 
 
 def move_kernel(*refs, moves, count):
@@ -89,7 +113,7 @@
         for block in range(n_seq)
     ]
     (copies,) = move(shards, [(n_seq, rows, starts[-1])], moves)
-    parts = swap(copies)
+    parts = swap(copies, "seq")
     moves = [
         (
             0,
@@ -106,7 +130,7 @@
         moves.append((1, (every, every), 0, (every, slice(width, width + extra.shape[1]))))
         width += extra.shape[1]
     (full,) = move([parts] if extra is None else [parts, extra], [(rows, width)], moves)
-    return lax.all_gather(full, "dp", axis=0, tiled=True)
+    return lax.all_gather(full, dp, axis=0, tiled=True)
 
 
 def deliver(terms, sizes, extra, out_sizes):
@@ -135,7 +159,7 @@
     return pl.pallas_call(
         functools.partial(sum_kernel, pieces=edges(out_sizes)),
         out_shape=[jax.ShapeDtypeStruct((rows, size), jnp.float32) for size in out_sizes],
-    )(swap(parts))
+    )(swap(parts, "seq"))
 
 
 def cut(array, sizes):
@@ -183,10 +207,9 @@
         out_ref[0, head_rows(0, head), :] = total.astype(out_ref.dtype)
 
 
-def attend_back_kernel(prefix_ref, *refs, places, count, causal):
+def attend_back_kernel(prefix_ref, *refs, places, spots, count, causal):
     upstream_ref = refs[count]
-    outs = refs[count + 1 : -2]
-    key_sum, value_sum = refs[-2:]
+    out_ref, key_sum, value_sum = refs[count + 1 :]
     step = pl.program_id(0)
     (q_at, q_row), (k_at, k_row), (v_at, v_row) = places
     blocks, unused, rows = refs[k_at].shape
@@ -220,13 +243,13 @@
             total += contract(key_rows, score_grads[part], 1, 0)
             key_sum[block, mine, :] += contract(queries, score_grads[part], 1, 1)
             value_sum[block, mine, :] += contract(upstream, shares[part], 1, 1)
-        outs[q_at][step, head_rows(q_row, head), :] = (total * HD**-0.5).astype(outs[q_at].dtype)
+        out_ref[step, head_rows(spots[0], head), :] = (total * HD**-0.5).astype(out_ref.dtype)
 
     @pl.when(step == pl.num_programs(0) - 1)
     def _():
         width = key_sum.shape[1]
-        outs[k_at][:, k_row : k_row + width, :] = key_sum[...].astype(outs[k_at].dtype)
-        outs[v_at][:, v_row : v_row + width, :] = value_sum[...].astype(outs[v_at].dtype)
+        out_ref[:, spots[1] : spots[1] + width, :] = key_sum[...].astype(out_ref.dtype)
+        out_ref[:, spots[2] : spots[2] + width, :] = value_sum[...].astype(out_ref.dtype)
 
 
 def exit_kernel(token_ref, table_ref, shifted_ref, product_ref, part_ref, logit_ref, *, rows):
@@ -293,14 +316,21 @@
 
 def attend_back(prefix, arrays, upstream, places, causal):
     blocks, width, rows = upstream.shape
+    shape = jax.ShapeDtypeStruct((blocks, 3 * width, rows), jnp.bfloat16)
     return pl.pallas_call(
-        functools.partial(attend_back_kernel, places=places, count=len(arrays), causal=causal),
+        functools.partial(
+            attend_back_kernel,
+            places=places,
+            spots=(0, width, 2 * width),
+            count=len(arrays),
+            causal=causal,
+        ),
         grid=(blocks,),
         in_specs=[pl.BlockSpec(memory_space=pltpu.SMEM)]
         + [whole(array) for array in arrays]
         + [pl.BlockSpec((1, width, rows), lambda step: (step, 0, 0))],
-        out_specs=[whole(array) for array in arrays],
-        out_shape=[jax.ShapeDtypeStruct(array.shape, array.dtype) for array in arrays],
+        out_specs=whole(shape),
+        out_shape=shape,
         scratch_shapes=[pltpu.VMEM((blocks, width, rows), jnp.float32)] * 2,
     )(prefix, *arrays, upstream)
 
@@ -331,7 +361,7 @@
 ):
     width = hidden_in.shape[2]
     n_seq = lax.axis_size("seq")
-    n_dp = lax.axis_size("dp")
+    n_dp = lax.axis_size(dp)
     own_rows, own = self_query.shape
     own_feed = feed_gate.shape[1]
     fold_rows = feed_down.shape[0]
@@ -364,10 +394,21 @@
     )
     feed_sizes = (own_feed, own_feed) + (own,) * folds
     gate_full, up_full, *downs = cut(feed, tuple(n_seq * size for size in feed_sizes))
-    table = lax.all_gather(
-        jnp.pad(embedding.T, ((0, 0), (0, vocab_lanes - vocab_rows))), "seq", axis=0, tiled=True
-    )
-    marks = lax.all_gather(jnp.concatenate([exit_flags, target_ids], axis=0), "dp", axis=0)
+    shard = jnp.pad(embedding.T, ((0, 0), (0, vocab_lanes - vocab_rows)))
+    shards = [shard] + [shift(shard, by) for by in range(1, n_seq)]
+    table = jnp.zeros((width, vocab_lanes), low)
+    for by in range(n_seq):
+        table = lax.dynamic_update_slice(table, shards[by], (spot(-by) * own, 0))
+
+    marks = jnp.concatenate(
+        [exit_flags, target_ids, jnp.broadcast_to(prefix_len[:, None], exit_flags.shape)], axis=0
+    )
+    marks = relocate(marks)
+    prefix_len = marks[2, :1]
+    marks = lax.all_gather(marks[:2], dp, axis=0)
+    hidden = relocate(hidden_in.reshape(-1, width))
+    states = relocate(encoder_in.reshape(-1, width))
+    cotangent = relocate(out_cotangent.reshape(-1, width))
     gain_one, gain_two, gain_three, gain_exit = gain_columns[:, :4].astype(jnp.float32).T
 
     def blocks(rows):
@@ -386,26 +427,30 @@
         rows = jnp.concatenate(parts, axis=1)[:, :fold_rows]
         return rows.reshape(n_dp * fold_rows, -1)
 
-    residual_in = hidden_in.reshape(-1, width).T.astype(jnp.float32)
+    residual_in = hidden.T.astype(jnp.float32)
     token_count = residual_in.shape[1]
-    states = encoder_in.reshape(-1, width).T
-    cotangent = out_cotangent.reshape(-1, width).T
-    residual_in, states, cotangent, marks = lax.optimization_barrier(
-        (residual_in, states, cotangent, marks)
-    )
+    residual_in, states, marks = lax.optimization_barrier((residual_in, states.T, marks))
     residual_in, states = rows_first(residual_in), rows_first(states)
-    cotangent = rows_first(cotangent)
+    cotangent = rows_first(cotangent.T)
     normed_one = norm_columns(residual_in, gain_one).astype(low)
-    qkv_one = swap(blocks(contract(self_qkv, normed_one, 0, 0)))
-    kv_two = swap(blocks(contract(cross_kv, states, 0, 0)))
+    attended = swap(
+        jnp.concatenate(
+            [
+                blocks(contract(self_qkv, normed_one, 0, 0)),
+                blocks(contract(cross_kv, states, 0, 0)),
+            ],
+            axis=1,
+        ),
+        "part",
+    )
     self_places = ((0, 0), (0, own), (0, 2 * own))
-    mixture_one = swap(attend(prefix_len, [qkv_one], self_places, own, True))
+    mixture_one = swap(attend(prefix_len, [attended], self_places, own, True), "part")
     mixture_one = mixture_one.reshape(width, token_count)
     after_self = residual_in + contract(self_out, mixture_one, 0, 0)
     normed_two = norm_columns(after_self, gain_two).astype(low)
-    q_two = swap(blocks(contract(cross_q, normed_two, 0, 0)))
-    cross_places = ((0, 0), (1, 0), (1, own))
-    mixture_two = swap(attend(prefix_len, [q_two, kv_two], cross_places, own, False))
+    q_two = swap(blocks(contract(cross_q, normed_two, 0, 0)), "part")
+    cross_places = ((0, 0), (1, 3 * own), (1, 4 * own))
+    mixture_two = swap(attend(prefix_len, [q_two, attended], cross_places, own, False), "part")
     mixture_two = mixture_two.reshape(width, token_count)
     after_cross = after_self + contract(cross_out, mixture_two, 0, 0)
     normed_three = norm_columns(after_cross, gain_three).astype(low)
@@ -416,13 +461,13 @@
     after_feed = after_cross
     for down, hidden in zip(downs, hidden_folds):
         after_feed = after_feed + contract(down, hidden, 0, 0)
-    block_output = after_feed.T.astype(low).reshape(hidden_in.shape)
+    block_output = relocate(after_feed.T.astype(low)).reshape(hidden_in.shape)
     normed_exit = rows_first(norm_columns(after_feed, gain_exit).astype(low).T)
     normed_exit, table = lax.optimization_barrier((normed_exit, table))
 
-    tokens = lax.all_gather(normed_exit, "dp", axis=0, tiled=True)
+    tokens = lax.all_gather(normed_exit, dp, axis=0, tiled=True)
     flag_rows = marks[:, 0].reshape(-1, 1).astype(jnp.float32)
-    target_rows = marks[:, 1].reshape(-1, 1) - lax.axis_index("dp") * vocab_rows
+    target_rows = marks[:, 1].reshape(-1, 1) - lax.axis_index(dp) * vocab_rows
     hits = jnp.arange(vocab_lanes)[None, :] == target_rows
     hits = hits & (target_rows < vocab_rows)
     target_terms = contract(hits.astype(low), table, 1, 1).astype(low)
@@ -430,25 +475,33 @@
     shifted, products, parts = exit_rows(tokens, table, vocab_rows)
     picked = jnp.sum(tokens.astype(jnp.float32) * target_terms.astype(jnp.float32), axis=1)
     row_max = parts[:, 0]
-    parts = lax.all_gather(jnp.stack([row_max, parts[:, 1], picked]), "dp", axis=0)
+    parts = lax.all_gather(jnp.stack([row_max, parts[:, 1], picked]), dp, axis=0)
     top = jnp.max(parts[:, 0], axis=0)
     log_total = top + jnp.log(jnp.sum(parts[:, 1] * jnp.exp(parts[:, 0] - top), axis=0))
     all_losses = flag_rows[:, 0] * (log_total - jnp.sum(parts[:, 2], axis=0))
     token_losses = lax.dynamic_slice(
-        all_losses, (lax.axis_index("dp") * token_count,), (token_count,)
-    ).reshape(exit_flags.shape)
+        all_losses, (lax.axis_index(dp) * token_count,), (token_count,)
+    )
+    token_losses = relocate(token_losses.reshape(exit_flags.shape))
     factor = flag_rows * jnp.exp(row_max - log_total)[:, None]
     exit_in_grad = lax.psum_scatter(
         rows_first((factor * products - flag_rows * target_terms.astype(jnp.float32)).astype(low)),
-        "dp",
+        dp,
         scatter_dimension=0,
         tiled=True,
     )
     logit_grads = jnp.where(hits, factor * shifted - flag_rows, factor * shifted).astype(low)
     table_terms = contract(tokens, logit_grads, 0, 0).astype(low)
-    exit_in_grad, table_terms = lax.optimization_barrier((rows_first(exit_in_grad), table_terms))
+    exit_in_grad, table_terms, block_output, token_losses = lax.optimization_barrier(
+        (rows_first(exit_in_grad), table_terms, block_output, token_losses)
+    )
     exit_in_grad = rows_first(exit_in_grad.T).astype(jnp.float32)
-    table_sums = lax.psum_scatter(table_terms, "seq", scatter_dimension=0, tiled=True)
+
+    def table_block(by):
+        return lax.dynamic_slice(table_terms, (spot(by) * own, 0), (own, vocab_lanes))
+
+    table_parts = [shift(table_block(by), by) for by in range(1, n_seq)]
+    table_sums = table_block(0).astype(jnp.float32)
 
     feed_grad, full_exit_gain = norm_back(after_feed, gain_exit, exit_in_grad)
     feed_grad = feed_grad + cotangent
@@ -461,37 +514,51 @@
     cross_grad, full_feed_gain = norm_back(after_cross, gain_three, normed_three_grad)
     cross_grad = cross_grad + feed_grad
     branch_two = cross_grad.astype(low)
-    mixture_two_grad = swap(blocks(contract(cross_out, branch_two, 1, 0)))
-    q_grad, kv_grad = attend_back(
-        prefix_len, [q_two, kv_two], mixture_two_grad, cross_places, False
-    )
-    q_grad = swap(q_grad).reshape(-1, token_count)
-    kv_grad = swap(kv_grad).reshape(-1, token_count)
-    encoder_grad = contract(kv_grad, cross_kv, 0, 1).reshape(encoder_in.shape)
-    rest_terms = jnp.concatenate(
+    mixture_two_grad = blocks(contract(cross_out, branch_two, 1, 0))
+    feed_terms = jnp.concatenate(
         [
-            contract(normed_two, q_grad, 1, 1).astype(low),
-            contract(states, kv_grad, 1, 1).astype(low),
-            contract(mixture_two, branch_two, 1, 1).astype(low),
             contract(normed_three, gate_grad, 1, 1).astype(low),
             contract(normed_three, up_grad, 1, 1).astype(low),
         ]
         + [contract(hidden, branch_three, 1, 1).astype(low) for hidden in hidden_folds],
         axis=1,
     )
+    mixture_two_grad, feed_terms = lax.optimization_barrier((mixture_two_grad, feed_terms))
+    feed_terms = lax.psum_scatter(feed_terms, dp, scatter_dimension=0, tiled=True)
+    cross_grads = attend_back(
+        prefix_len, [q_two, attended], swap(mixture_two_grad, "part"), cross_places, False
+    )
+    cross_grads, table_parts[0] = lax.optimization_barrier((cross_grads, table_parts[0]))
+    cross_grads = swap(cross_grads, "part")
+    q_grad = cross_grads[:, :own].reshape(-1, token_count)
+    kv_grad = cross_grads[:, own:].reshape(-1, token_count)
+    encoder_grad = relocate(contract(kv_grad, cross_kv, 0, 1)).reshape(encoder_in.shape)
+    cross_terms = jnp.concatenate(
+        [
+            contract(normed_two, q_grad, 1, 1).astype(low),
+            contract(states, kv_grad, 1, 1).astype(low),
+            contract(mixture_two, branch_two, 1, 1).astype(low),
+        ],
+        axis=1,
+    )
     self_grad, full_cross_gain = norm_back(after_self, gain_two, contract(cross_q, q_grad, 1, 0))
     self_grad = self_grad + cross_grad
     branch_one = self_grad.astype(low)
     mixture_one_grad = blocks(contract(self_out, branch_one, 1, 0))
-    mixture_one_grad, rest_terms = lax.optimization_barrier((mixture_one_grad, rest_terms))
-    rest_terms, table_sums = lax.optimization_barrier((rest_terms, table_sums))
-    embedding_grad = table_sums[:, :vocab_rows].astype(jnp.float32).T
-    rest_terms = lax.psum_scatter(rest_terms, "dp", scatter_dimension=0, tiled=True)
-    (qkv_grad,) = attend_back(prefix_len, [qkv_one], swap(mixture_one_grad), self_places, True)
-    qkv_grad = swap(qkv_grad).reshape(-1, token_count)
+    mixture_one_grad, cross_terms, table_parts[1] = lax.optimization_barrier(
+        (mixture_one_grad, cross_terms, table_parts[1])
+    )
+    qkv_grad = attend_back(
+        prefix_len, [attended], swap(mixture_one_grad, "part"), self_places, True
+    )
+    qkv_grad, table_parts[2:], encoder_grad, feed_terms, cross_terms = lax.optimization_barrier(
+        (qkv_grad, table_parts[2:], encoder_grad, feed_terms, cross_terms)
+    )
+    cross_terms = lax.psum_scatter(cross_terms, dp, scatter_dimension=0, tiled=True)
+    qkv_grad = swap(qkv_grad, "part").reshape(-1, token_count)
     normed_one_grad = contract(self_qkv, qkv_grad, 1, 0)
     input_grad, full_self_gain = norm_back(residual_in, gain_one, normed_one_grad)
-    hidden_grad = (input_grad + self_grad).T.reshape(hidden_in.shape)
+    hidden_grad = relocate((input_grad + self_grad).T).reshape(hidden_in.shape)
     gain_terms = jnp.stack(
         [full_self_gain, full_cross_gain, full_feed_gain, full_exit_gain], axis=1
     ).astype(low)
@@ -504,17 +571,15 @@
         ],
         axis=1,
     )
-    self_terms, rest_terms = lax.optimization_barrier((self_terms, rest_terms))
-    self_terms = lax.psum_scatter(self_terms, "dp", scatter_dimension=0, tiled=True)
-    (
-        cross_query_grad,
-        cross_key_grad,
-        cross_value_grad,
-        cross_output_grad,
-        feed_gate_grad,
-        feed_up_grad,
-        *down_sums,
-    ) = deliver(rest_terms, near_sizes[2:] + feed_sizes, 0, (own,) * 4 + feed_sizes)
+    self_terms, cross_terms = lax.optimization_barrier((self_terms, cross_terms))
+    self_terms = lax.psum_scatter(self_terms, dp, scatter_dimension=0, tiled=True)
+    for part in table_parts:
+        table_sums = table_sums + part.astype(jnp.float32)
+    embedding_grad = table_sums[:, :vocab_rows].T
+    cross_query_grad, cross_key_grad, cross_value_grad, cross_output_grad = deliver(
+        cross_terms, near_sizes[2:], 0, (own,) * 4
+    )
+    feed_gate_grad, feed_up_grad, *down_sums = deliver(feed_terms, feed_sizes, 0, feed_sizes)
     down_grad = jnp.concatenate(down_sums, axis=0)[:fold_rows]
     self_query_grad, self_key_grad, self_value_grad, self_output_grad, gain_sums = deliver(
         self_terms, near_sizes[:2], GAIN_LANES, (own,) * 4 + (GAIN_LANES,)
@@ -545,14 +610,16 @@
 
 
 def solution(mesh):
-    tokens = P("dp", "seq")
-    rows = P("dp")
-    matrix = P("dp", "seq")
-    block = P("dp", "seq", None)
+    size = mesh.shape["seq"]
+    planes = Mesh(mesh.devices.reshape(-1, size, size), dp + ("seq",))
+    tokens = P(dp, "seq")
+    rows = P(dp)
+    matrix = P(dp, "seq")
+    block = P(dp, "seq", None)
     attention = (rows,) + (matrix,) * 4
     return jax.shard_map(
         per_device,
-        mesh=mesh,
+        mesh=planes,
         in_specs=(block, block, rows, tokens, tokens, block)
         + attention * 2
         + (rows, matrix, matrix, matrix, rows, matrix),

time: 838 us -> 912 us (1.088)
  starting transfers between devices: 45.1 us -> 84.4 us
  waiting for transfers between devices: 289 us -> 320 us
  blocking collectives: 172 us -> 148 us
  local copies, waits for them, and re-layouts: 27.8 us -> 49.3 us
  matrix products: 115 us -> 102 us
    ppermute x0 -> x14, waiting for transfers between devices: none -> 117 us  [the longest x6 117 us: shift(): lax.ppermute(block, 'seq', [(at, (at + by) % size) for at in range(size)])]
    all_to_all x6 -> x3, blocking collectives: 153 us -> 76 us  [swap(): return lax.all_to_all(pieces, axis, 0, 0, tiled=True)]
    all_gather x2, blocking collectives: 18.5 us -> 71.7 us  [the longest x1 62.5 us: per_device(): marks = lax.all_gather(marks[:2], dp, axis=0)]
    all_gather x4 -> x3, waiting for transfers between devices: 50.1 us -> 12.1 us  [the longest x1 12 us: per_device(): tokens = lax.all_gather(normed_exit, dp, axis=0, tiled=True)]
    reduce_scatter x3, waiting for transfers between devices: 78.3 us -> 40.8 us  [the longest x1 29.1 us: per_device(): lax.psum_scatter(cross_terms, dp, scatter_dimension=0, tiled=True)]
    ppermute x0 -> x14, starting transfers between devices: none -> 36 us  [the longest x8 19.6 us: relocate(): return lax.ppermute(block, ('group', 'part', 'seq'), pairs)]
    dot_general x32, matrix products: 115 us -> 102 us  [contract(): lax.dot_general(first_op, second_op, (((first_dim,), (second_dim,)), ((),...]
    all_to_all x8 -> x10, waiting for transfers between devices: 142 us -> 133 us  [swap(): return lax.all_to_all(pieces, axis, 0, 0, tiled=True)]
  transfers between devices with their start and end apart: 16 -> 31, of which waited for: 13 -> 16; matrix products, arithmetic and copies ran while one was open for 18% -> 14% of each run, Pallas kernels for 8% -> 8%
where the time goes in v4:
time: 912 us; the launch traced here: 900 us
  waiting for transfers between devices  320 us (35%)
  blocking collectives  148 us (16%)
  Pallas kernels  140 us (15%)
  matrix products  102 us (11%)
  starting transfers between devices  84.4 us (9%)
  local copies, waits for them, and re-layouts  49.3 us (5%)
  other arithmetic  39.9 us (4%)
  between operations  16.3 us (2%)
    all_to_all x10, waiting for transfers between devices, swap(): return lax.all_to_all(pieces, axis, 0, 0, tiled=True)  133 us
    ppermute x6, waiting for transfers between devices, shift(): lax.ppermute(block, 'seq', [(at, (at + by) % size) for at in range(size)])  117 us
    dot_general x32, matrix products, contract(): lax.dot_general(first_op, second_op, (((first_dim,), (second_dim,)), ((),...  102 us
    all_to_all x3, blocking collectives, swap(): return lax.all_to_all(pieces, axis, 0, 0, tiled=True)  76 us
    all_gather x1, blocking collectives, per_device(): marks = lax.all_gather(marks[:2], dp, axis=0)  62.5 us
    pallas_call x1, Pallas kernels, exit_rows(): pl.pallas_call(functools.partial(exit_kernel, rows=rows), grid=(count //...  57.5 us
    all_to_all x10, starting transfers between devices, swap(): return lax.all_to_all(pieces, axis, 0, 0, tiled=True)  48.2 us
    pallas_call x2, Pallas kernels, attend_back(): pl.pallas_call(functools.partial(attend_back_kernel, places=places, spots...  37.9 us
  transfers between devices with their start and end apart: 31, of which 16 were waited for; matrix products, arithmetic and copies ran while one was open for 14% of the time, Pallas kernels for 8%

profile of v4, /device:TPU:8, one launch (start us, length us, event | category | flops | bytes accessed | tf_op | source)
XLA Modules:
  0.0 899.9 jit_solution(14176473476040320623)
XLA Ops:
  12.6 5.4 all-to-all-start
  18.9 24.5 %all-to-all-done.refs_0_ = bf16[4,96,1536]{2,1,0:T(8,128)(2,1)S(1)} async-done(((bf16[4,96,1536]{2,1,0:T(8,128)(2,1)}), bf16[4,96,1536]{2,1,0:T(8,128)(2,1)S(1)}, u32[]{:S(2)}, u32[]{:S(2)}) %all-to-all-start) | async-done | bytes 1179680 | tf_op jit(solution)/shard_map/all_to_all | solution.py:53
  49.9 36.2 %all_to_all.65.refs_0_ = bf16[4,96,1600]{2,1,0:T(8,128)(2,1)} all-to-all(bf16[4,96,1600]{2,1,0:T(8,128)(2,1)} %shard_map.369), channel_id=1, replica_groups=mesh['group'=2,'part'=4,'seq'=4] {'seq'}, dimensions={0} | all-to-all | bytes 2457600 | tf_op jit(solution)/shard_map/all_to_all | solution.py:53
  91.2 3.5 collective-permute-start.1
  103.1 6.1 collective-permute-start.3
  109.1 62.5 %all-gather.2 = s32[8,2,256]{2,1,0:T(2,128)} all-gather(s32[1,2,256]{2,1,0:T(2,128)S(1)} %slice_bitcast_fusion.1), channel_id=2, replica_groups=mesh['group'=2,'part'=4,'seq'=4] {'group','part'}, dimensions={0}, use_global_device_ids=true | all-gather | bytes 18432 | tf_op jit(solution)/shard_map/all_gather | solution.py:408
  181.0 3.6 all-to-all-start.1
  186.9 21.9 %all-to-all-done.1.refs_0_.refs_1_ = bf16[4,960,256]{2,1,0:T(8,128)(2,1)S(1)} async-done(((bf16[4,960,256]{2,1,0:T(8,128)(2,1)}), bf16[4,960,256]{2,1,0:T(8,128)(2,1)S(1)}, u32[]{:S(2)}, u32[]{:S(2)}) %all-to-all-start.1) | async-done | bytes 1966112 | tf_op jit(solution)/shard_map/all_to_all | solution.py:53
  210.1 11.5 %shard_map.367 = bf16[4,192,256]{2,1,0:T(8,128)(2,1)} custom-call(s32[1]{0:T(128)} %bitcast.11.prefix_ref, bf16[4,960,256]{2,1,0:T(8,128)(2,1)} %copy-done), custom_call_target="tpu_custom_call" | custom-call | tf_op jit(solution)/shard_map/pallas_call | solution.py:308
  221.6 3.5 all-to-all-start.2
  227.8 4.7 all-to-all-done.2
  237.4 3.5 all-to-all-start.3
  240.9 46.0 %collective-permute-done.4 = bf16[192,4096]{1,0:T(8,128)(2,1)} collective-permute-done((bf16[192,4096]{1,0:T(8,128)(2,1)}, bf16[192,4096]{1,0:T(8,128)(2,1)}, u32[]{:S(2)}, u32[]{:S(2)}) %collective-permute-start.4) | collective-permute-done | bytes 1572896 | tf_op jit(solution)/shard_map/ppermute | solution.py:69
  290.3 11.2 %shard_map.368 = bf16[4,192,256]{2,1,0:T(8,128)(2,1)} custom-call(s32[1]{0:T(128)} %bitcast.11.prefix_ref, bf16[4,192,256]{2,1,0:T(8,128)(2,1)} %copy-done.6, bf16[4,960,256]{2,1,0:T(8,128)(2,1)} %copy-done), custom_call_target="tpu_custom_call" | custom-call | tf_op jit(solution)/shard_map/pallas_call | solution.py:308
  301.5 3.7 all-to-all-start.4
  308.0 4.6 all-to-all-done.4
  327.4 19.6 %fusion.22 = bf16[2048,768]{1,0:T(8,128)(2,1)} fusion(bf16[768,4096]{1,0:T(8,128)(2,1)} %constant_dynamic-update-slice_fusion.table_ref, s32[2048]{0:T(1024)S(1)} %bitcast.165, pred[2048]{0:T(1024)(128)(4,1)S(1)} %broadcast_compare_fusion), kind=kOutput, calls=%fused_computation.29 | convolution fusion | flops 12903251968 | bytes 9447424 | tf_op jit(solution)/shard_map/dot_general | solution.py:23
  347.0 12.0 %all-gather.12.cloned.1.call-done.token_ref = bf16[2048,768]{1,0:T(8,128)(2,1)} async-done(((bf16[256,768]{1,0:T(8,128)(2,1)}), bf16[2048,768]{1,0:T(8,128)(2,1)}) %all-gather.12.cloned.1.call-update) | async-done | bytes 3145744 | tf_op jit(solution)/shard_map/all_gather | solution.py:468
  359.1 57.5 %shard_map.371 = (bf16[2048,4096]{1,0:T(8,128)(2,1)}, f32[2048,768]{1,0:T(8,128)}, f32[2048,128]{1,0:T(8,128)}) custom-call(bf16[2048,768]{1,0:T(8,128)(2,1)} %all-gather.12.cloned.1.call-done.token_ref, bf16[768,4096]{1,0:T(8,128)(2,1)} %constant_dynamic-update-slice_fusion.table_ref), custom_call_target="tpu_custom_call" | custom-call | tf_op jit(solution)/shard_map/pallas_call | solution.py:284
  416.6 3.8 fusion.16
  421.3 9.3 %all-gather.3 = f32[8,3,2048]{2,1,0:T(4,128)S(1)} all-gather(f32[1,3,2048]{2,1,0:T(4,128)S(1)} %maximum_bitcast_fusion), channel_id=3, replica_groups=mesh['group'=2,'part'=4,'seq'=4] {'group','part'}, dimensions={0}, use_global_device_ids=true | all-gather | bytes 221184 | tf_op jit(solution)/shard_map/all_gather | solution.py:478
  435.5 4.5 fusion.18
  451.1 27.5 %fusion.13 = bf16[768,4096]{1,0:T(8,128)(2,1)} fusion(bf16[2048,768]{1,0:T(8,128)(2,1)} %all-gather.12.cloned.1.call-done.token_ref, bf16[2048,4096]{1,0:T(8,128)(2,1)} %get-tuple-element.71, f32[2048]{0:T(1024)S(1)} %bitcast.159, f32[2048]{0:T(1024)} %copy-done.41, s32[2048]{0:T(1024)} %bitcast.166, pred[2048]{0:T(1024)(128)(4,1)} %copy-done.63), kind=kOutput, calls=%fused_computation.16 | convolution fusion | flops 12946767872 | bytes 26241024 | tf_op jit(solution)/shard_map/dot_general | solution.py:23
  478.7 17.5 %reduce-scatter.5.cloned.1.call-done = bf16[256,768]{1,0:T(8,128)(2,1)} async-done(((bf16[2048,768]{1,0:T(8,128)(2,1)}), bf16[256,768]{1,0:T(8,128)(2,1)}) %reduce-scatter.5.cloned.1.call-update) | async-done | bytes 393232 | tf_op jit(solution)/shard_map/reduce_scatter | solution.py:487
  525.8 4.7 constant_dynamic-slice_fusion
  530.6 4.5 collective-permute-start.9
  535.1 10.5 %all_to_all.66.refs_2_ = bf16[4,192,256]{2,1,0:T(8,128)(2,1)} all-to-all(bf16[4,192,256]{2,1,0:T(8,128)(2,1)S(1)} %bitcast.154), channel_id=1, replica_groups=mesh['group'=2,'part'=4,'seq'=4] {'part'}, dimensions={0} | all-to-all | bytes 786432 | tf_op jit(solution)/shard_map/all_to_all | solution.py:53
  545.6 18.8 %shard_map.372 = bf16[4,576,256]{2,1,0:T(8,128)(2,1)} custom-call(s32[1]{0:T(128)} %bitcast.11.prefix_ref, bf16[4,192,256]{2,1,0:T(8,128)(2,1)} %copy-done.6, bf16[4,960,256]{2,1,0:T(8,128)(2,1)} %copy-done, bf16[4,192,256]{2,1,0:T(8,128)(2,1)} %all_to_all.66.refs_2_), custom_call_target="tpu_custom_call" | custom-call | tf_op jit(solution)/shard_map/pallas_call | solution.py:320
  564.4 4.6 collective-permute-done.9
  569.0 4.3 all-to-all-start.7
  573.3 3.9 collective-permute-start.10
  577.9 18.8 %all-to-all-done.7 = bf16[4,576,256]{2,1,0:T(8,128)(2,1)} async-done(((bf16[4,576,256]{2,1,0:T(8,128)(2,1)}), bf16[4,576,256]{2,1,0:T(8,128)(2,1)}, u32[]{:S(2)}, u32[]{:S(2)}) %all-to-all-start.7) | async-done | bytes 1179680 | tf_op jit(solution)/shard_map/all_to_all | solution.py:53
  597.9 3.7 fusion.44
  612.8 65.9 %collective-permute-done.10 = bf16[192,4096]{1,0:T(8,128)(2,1)} collective-permute-done((bf16[192,4096]{1,0:T(8,128)(2,1)}, bf16[192,4096]{1,0:T(8,128)(2,1)}, u32[]{:S(2)}, u32[]{:S(2)}) %collective-permute-start.10) | collective-permute-done | bytes 1572896 | tf_op jit(solution)/shard_map/ppermute | solution.py:69
  678.7 29.3 %all_to_all.67.refs_1_ = bf16[4,192,256]{2,1,0:T(8,128)(2,1)} all-to-all(bf16[4,192,256]{2,1,0:T(8,128)(2,1)S(1)} %bitcast.155), channel_id=1, replica_groups=mesh['group'=2,'part'=4,'seq'=4] {'part'}, dimensions={0} | all-to-all | bytes 786432 | tf_op jit(solution)/shard_map/all_to_all | solution.py:53
  708.0 19.1 %shard_map.373 = bf16[4,576,256]{2,1,0:T(8,128)(2,1)} custom-call(s32[1]{0:T(128)} %bitcast.11.prefix_ref, bf16[4,960,256]{2,1,0:T(8,128)(2,1)} %copy-done, bf16[4,192,256]{2,1,0:T(8,128)(2,1)} %all_to_all.67.refs_1_), custom_call_target="tpu_custom_call" | custom-call | tf_op jit(solution)/shard_map/pallas_call | solution.py:320
  727.2 4.1 all-to-all-start.9
  732.9 14.3 %all-to-all-done.9 = bf16[4,576,256]{2,1,0:T(8,128)(2,1)S(1)} async-done(((bf16[4,576,256]{2,1,0:T(8,128)(2,1)}), bf16[4,576,256]{2,1,0:T(8,128)(2,1)S(1)}, u32[]{:S(2)}, u32[]{:S(2)}) %all-to-all-start.9) | async-done | bytes 1179680 | tf_op jit(solution)/shard_map/all_to_all | solution.py:53
  747.2 4.0 multiply_reduce_fusion.3
  755.2 29.1 %reduce-scatter.9.cloned.1.call-done.refs_0_ = bf16[96,3072]{1,0:T(8,128)(2,1)} async-done(((bf16[768,3072]{1,0:T(8,128)(2,1)}), bf16[96,3072]{1,0:T(8,128)(2,1)}) %reduce-scatter.9.cloned.1.call-update) | async-done | bytes 589840 | tf_op jit(solution)/shard_map/reduce_scatter | solution.py:557
  786.9 5.3 all-to-all-start.12
  794.2 25.1 %all-to-all-done.12.terms_ref = bf16[4,96,1600]{2,1,0:T(8,128)(2,1)S(1)} async-done(((bf16[4,96,1600]{2,1,0:T(8,128)(2,1)}), bf16[4,96,1600]{2,1,0:T(8,128)(2,1)S(1)}, u32[]{:S(2)}, u32[]{:S(2)}) %all-to-all-start.12) | async-done | bytes 1228832 | tf_op jit(solution)/shard_map/all_to_all | solution.py:53
  819.3 6.7 all-to-all-start.11
  832.2 11.7 %reduce-scatter.11.cloned.1.call-done.refs_0_ = bf16[96,3200]{1,0:T(8,128)(2,1)} async-done(((bf16[768,3200]{1,0:T(8,128)(2,1)}), bf16[96,3200]{1,0:T(8,128)(2,1)}) %reduce-scatter.11.cloned.1.call-update) | async-done | bytes 614416 | tf_op jit(solution)/shard_map/reduce_scatter | solution.py:575
  846.0 8.8 all-to-all-done.11.terms_ref
  854.8 8.1 all-to-all-start.10
  862.8 5.5 add_bitcast_fusion
  875.4 10.4 %all-to-all-done.10.terms_ref = bf16[4,96,896]{2,1,0:T(8,128)(2,1)S(1)} async-done(((bf16[4,96,896]{2,1,0:T(8,128)(2,1)}), bf16[4,96,896]{2,1,0:T(8,128)(2,1)S(1)}, u32[]{:S(2)}, u32[]{:S(2)}) %all-to-all-start.10) | async-done | bytes 688160 | tf_op jit(solution)/shard_map/all_to_all | solution.py:53
  (305 shorter events, 158.4 us)
Async XLA Ops:
  12.6 34.4 %copy-start.34 = (bf16[256,192]{0,1:T(8,128)(2,1)S(1)}, bf16[256,192]{0,1:T(8,128)(2,1)}, u32[]{:S(2)}) copy-start(bf16[256,192]{0,1:T(8,128)(2,1)} %param.41) | copy-start | bytes 294916
  12.6 30.7 %all-to-all-start = ((bf16[4,96,1536]{2,1,0:T(8,128)(2,1)}), bf16[4,96,1536]{2,1,0:T(8,128)(2,1)S(1)}, u32[]{:S(2)}, u32[]{:S(2)}) async-start(bf16[4,96,1536]{2,1,0:T(8,128)(2,1)} %shard_map.365), calls=%async_computation | async-start | bytes 2359296 | tf_op jit(solution)/shard_map/all_to_all | solution.py:53
  18.1 153.7 %all-gather.8.cloned.1.call-start = ((), (), s32[]{:S(2)}) async-start(), calls=%async_computation.17 | async-start | bytes 10838016 | tf_op jit(solution)/shard_map/all_gather | solution.py:133
  47.0 267.8 %all-gather.10.cloned.1.call-start = ((), (), s32[]{:S(2)}) async-start(), calls=%async_computation.18 | async-start | bytes 11059200 | tf_op jit(solution)/shard_map/all_gather | solution.py:133
  49.9 38.8 %copy-start.30 = (bf16[1,256,768]{2,1,0:T(8,128)(2,1)S(1)}, bf16[1,256,768]{2,1,0:T(8,128)(2,1)}, u32[]{:S(2)}) copy-start(bf16[1,256,768]{2,1,0:T(8,128)(2,1)} %param.22) | copy-start | bytes 1179652
  49.9 41.1 %copy-start.31 = (bf16[1,256,768]{2,1,0:T(8,128)(2,1)S(1)}, bf16[1,256,768]{2,1,0:T(8,128)(2,1)}, u32[]{:S(2)}) copy-start(bf16[1,256,768]{2,1,0:T(8,128)(2,1)} %param.23) | copy-start | bytes 1179652
  88.9 82.7 %collective-permute-start = (bf16[256,768]{0,1:T(8,128)(2,1)S(1)}, bf16[256,768]{0,1:T(8,128)(2,1)S(1)}, u32[]{:S(2)}, u32[]{:S(2)}) collective-permute-start(bf16[256,768]{0,1:T(8,128)(2,1)S(1)} %bitcast.153), channel_id=1, source_target_pairs={{0,0},{1,4},{2,8},{3,12},{4,1},{5,5},{6,9},{7,13},{8,2},{9,6},{10,... | collective-permute-start | bytes 1179656 | tf_op jit(solution)/shard_map/ppermute | solution.py:64
  91.2 80.4 %collective-permute-start.1 = (bf16[256,768]{0,1:T(8,128)(2,1)S(1)}, bf16[256,768]{0,1:T(8,128)(2,1)S(1)}, u32[]{:S(2)}, u32[]{:S(2)}) collective-permute-start(bf16[256,768]{0,1:T(8,128)(2,1)S(1)} %bitcast.152), channel_id=1, source_target_pairs={{0,0},{1,4},{2,8},{3,12},{4,1},{5,5},{6,9},{7,13},{8,2},{9,6},{10,... | collective-permute-start | bytes 1179656 | tf_op jit(solution)/shard_map/ppermute | solution.py:64
  95.5 13.6 %collective-permute-start.2 = (s32[3,256]{1,0:T(4,128)S(1)}, s32[3,256]{1,0:T(4,128)S(1)}, u32[]{:S(2)}, u32[]{:S(2)}) collective-permute-start(s32[3,256]{1,0:T(4,128)S(1)} %add_add_fusion.4), channel_id=1, source_target_pairs={{0,0},{1,4},{2,8},{3,12},{4,1},{5,5},{6,9},{7,13},{8,2},{9,6},{10,... | collective-permute-start | bytes 9224 | tf_op jit(solution)/shard_map/ppermute | solution.py:64
  103.1 122.0 %collective-permute-start.3 = (bf16[192,4096]{1,0:T(8,128)(2,1)}, bf16[192,4096]{1,0:T(8,128)(2,1)}, u32[]{:S(2)}, u32[]{:S(2)}) collective-permute-start(bf16[192,4096]{1,0:T(8,128)(2,1)} %get-tuple-element.209), channel_id=1, source_target_pairs={{0,1},{1,2},{2,3},{3,0},{4,5},{5,6},{6,7},{7,4},{8,9},{9,10},{10,1... | collective-permute-start | bytes 4718600 | tf_op jit(solution)/shard_map/ppermute | solution.py:69
  173.6 60.8 %copy-start.37 = (f32[768]{0:T(1024)}, f32[768]{0:T(1024)S(1)}, u32[]{:S(2)}) copy-start(f32[768]{0:T(1024)S(1)} %get-tuple-element.196) | copy-start | bytes 9220
  173.6 140.9 %copy-start.39 = (f32[768]{0:T(1024)}, f32[768]{0:T(1024)S(1)}, u32[]{:S(2)}) copy-start(f32[768]{0:T(1024)S(1)} %get-tuple-element.195) | copy-start | bytes 9220
  181.0 27.8 %all-to-all-start.1 = ((bf16[4,960,256]{2,1,0:T(8,128)(2,1)}), bf16[4,960,256]{2,1,0:T(8,128)(2,1)S(1)}, u32[]{:S(2)}, u32[]{:S(2)}) async-start(bf16[4,960,256]{2,1,0:T(8,128)(2,1)} %pad_maximum_fusion.3), calls=%async_computation.1 | async-start | bytes 3932160 | tf_op jit(solution)/shard_map/all_to_all | solution.py:53
  184.6 102.3 %collective-permute-start.4 = (bf16[192,4096]{1,0:T(8,128)(2,1)}, bf16[192,4096]{1,0:T(8,128)(2,1)}, u32[]{:S(2)}, u32[]{:S(2)}) collective-permute-start(bf16[192,4096]{1,0:T(8,128)(2,1)} %get-tuple-element.209), channel_id=1, source_target_pairs={{0,2},{1,3},{2,0},{3,1},{4,6},{5,7},{6,4},{7,5},{8,10},{9,11},{10,... | collective-permute-start | bytes 4718600 | tf_op jit(solution)/shard_map/ppermute | solution.py:69
  184.6 120.6 %collective-permute-start.5 = (bf16[192,4096]{1,0:T(8,128)(2,1)}, bf16[192,4096]{1,0:T(8,128)(2,1)}, u32[]{:S(2)}, u32[]{:S(2)}) collective-permute-start(bf16[192,4096]{1,0:T(8,128)(2,1)} %get-tuple-element.209), channel_id=1, source_target_pairs={{0,3},{1,0},{2,1},{3,2},{4,7},{5,4},{6,5},{7,6},{8,11},{9,8},{10,9... | collective-permute-start | bytes 4718600 | tf_op jit(solution)/shard_map/ppermute | solution.py:69
  221.6 10.8 %all-to-all-start.2 = ((bf16[4,192,256]{2,1,0:T(8,128)(2,1)}), bf16[4,192,256]{2,1,0:T(8,128)(2,1)S(1)}, u32[]{:S(2)}, u32[]{:S(2)}) async-start(bf16[4,192,256]{2,1,0:T(8,128)(2,1)} %shard_map.367), calls=%async_computation.2 | async-start | bytes 786432 | tf_op jit(solution)/shard_map/all_to_all | solution.py:53
  234.4 78.2 %copy-start.7 = (f32[768,256]{1,0:T(8,128)}, f32[768,256]{1,0:T(8,128)S(1)}, u32[]{:S(2)}) copy-start(f32[768,256]{1,0:T(8,128)S(1)} %get-tuple-element.226) | copy-start | bytes 2359300
  237.4 52.2 %all-to-all-start.3 = ((bf16[4,192,256]{2,1,0:T(8,128)(2,1)}), bf16[4,192,256]{2,1,0:T(8,128)(2,1)S(1)}, u32[]{:S(2)}, u32[]{:S(2)}) async-start(bf16[4,192,256]{2,1,0:T(8,128)(2,1)} %bitcast.16), calls=%async_computation.3 | async-start | bytes 786432 | tf_op jit(solution)/shard_map/all_to_all | solution.py:53
  301.5 11.1 %all-to-all-start.4 = ((bf16[4,192,256]{2,1,0:T(8,128)(2,1)}), bf16[4,192,256]{2,1,0:T(8,128)(2,1)S(1)}, u32[]{:S(2)}, u32[]{:S(2)}) async-start(bf16[4,192,256]{2,1,0:T(8,128)(2,1)} %shard_map.368), calls=%async_computation.4 | async-start | bytes 786432 | tf_op jit(solution)/shard_map/all_to_all | solution.py:53
  305.2 53.9 %all-gather.12.cloned.1.call-start = ((), (), s32[]{:S(2)}) async-start(), calls=%async_computation.19 | async-start | bytes 3538944 | tf_op jit(solution)/shard_map/all_gather | solution.py:468
  324.0 23.0 %copy-start.60 = (f32[256]{0:T(256)}, f32[256]{0:T(256)S(1)}, u32[]{:S(2)}) copy-start(f32[256]{0:T(256)S(1)} %get-tuple-element.231) | copy-start | bytes 3076
  324.1 23.0 %copy-start.43 = (f32[256]{0:T(256)}, f32[256]{0:T(256)S(1)}, u32[]{:S(2)}) copy-start(f32[256]{0:T(256)S(1)} %fusion.90) | copy-start | bytes 3076
  325.9 170.3 %reduce-scatter.5.cloned.1.call-start = ((), (), s32[]{:S(2)}) async-start(), calls=%async_computation.20 | async-start | bytes 3538944 | tf_op jit(solution)/shard_map/reduce_scatter | solution.py:487
  326.0 21.0 %copy-start.42 = (s32[8,1,256]{2,1,0:T(1,128)}, s32[8,1,256]{2,1,0:T(1,128)S(1)}, u32[]{:S(2)}) copy-start(s32[8,1,256]{2,1,0:T(1,128)S(1)} %get-tuple-element.224) | copy-start | bytes 24580
  440.1 287.0 %reduce-scatter.7.cloned.1.call-start = ((), (), s32[]{:S(2)}) async-start(), calls=%async_computation.21 | async-start | bytes 11059200 | tf_op jit(solution)/shard_map/reduce_scatter | solution.py:527
  442.3 56.1 %collective-permute-start.8 = (f32[256,768]{0,1:T(8,128)}, f32[256,768]{0,1:T(8,128)}, u32[]{:S(2)}, u32[]{:S(2)}) collective-permute-start(f32[256,768]{0,1:T(8,128)} %bitcast.143), channel_id=1, source_target_pairs={{0,0},{1,4},{2,8},{3,12},{4,1},{5,5},{6,9},{7,13},{8,2},{9,6},{10,... | collective-permute-start | bytes 2359304 | tf_op jit(solution)/shard_map/ppermute | solution.py:64
  444.7 33.9 %collective-permute-start.6 = (bf16[256,768]{0,1:T(8,128)(2,1)S(1)}, bf16[256,768]{0,1:T(8,128)(2,1)S(1)}, u32[]{:S(2)}, u32[]{:S(2)}) collective-permute-start(bf16[256,768]{0,1:T(8,128)(2,1)S(1)} %copy-done.33), channel_id=1, source_target_pairs={{0,0},{1,4},{2,8},{3,12},{4,1},{5,5},{6,9},{7,13},{8,2},{9,6},{10,... | collective-permute-start | bytes 1179656 | tf_op jit(solution)/shard_map/ppermute | solution.py:64
  448.7 30.0 %collective-permute-start.7 = (f32[1,256]{1,0:T(1,128)S(1)}, f32[1,256]{1,0:T(1,128)S(1)}, u32[]{:S(2)}, u32[]{:S(2)}) collective-permute-start(f32[1,256]{1,0:T(1,128)S(1)} %bitcast.167), channel_id=1, source_target_pairs={{0,0},{1,4},{2,8},{3,12},{4,1},{5,5},{6,9},{7,13},{8,2},{9,6},{10,... | collective-permute-start | bytes 3080 | tf_op jit(solution)/shard_map/ppermute | solution.py:64
  451.1 46.3 %copy-start.44 = (f32[256]{0:T(256)S(1)}, f32[256]{0:T(256)}, u32[]{:S(2)}) copy-start(f32[256]{0:T(256)} %copy-done.43) | copy-start | bytes 3076
  451.1 47.3 %copy-start.61 = (f32[256]{0:T(256)S(1)}, f32[256]{0:T(256)}, u32[]{:S(2)}) copy-start(f32[256]{0:T(256)} %copy-done.60) | copy-start | bytes 3076
  478.7 19.8 %copy-start.32 = (bf16[256,768]{0,1:T(8,128)(2,1)}, bf16[256,768]{0,1:T(8,128)(2,1)S(1)}, u32[]{:S(2)}) copy-start(bf16[256,768]{0,1:T(8,128)(2,1)S(1)} %collective-permute-done.6) | copy-start | bytes 1179652
  530.6 38.4 %collective-permute-start.9 = (bf16[192,4096]{1,0:T(8,128)(2,1)}, bf16[192,4096]{1,0:T(8,128)(2,1)}, u32[]{:S(2)}, u32[]{:S(2)}) collective-permute-start(bf16[192,4096]{1,0:T(8,128)(2,1)} %get-tuple-element.206), channel_id=1, source_target_pairs={{0,1},{1,2},{2,3},{3,0},{4,5},{5,6},{6,7},{7,4},{8,9},{9,10},{10,1... | collective-permute-start | bytes 4718600 | tf_op jit(solution)/shard_map/ppermute | solution.py:69
  545.6 31.8 %copy-start.18 = (bf16[4,192,256]{2,1,0:T(8,128)(2,1)S(1)}, bf16[4,192,256]{2,1,0:T(8,128)(2,1)}, u32[]{:S(2)}) copy-start(bf16[4,192,256]{2,1,0:T(8,128)(2,1)} %copy-done.17) | copy-start | bytes 1179652
  569.0 27.7 %all-to-all-start.7 = ((bf16[4,576,256]{2,1,0:T(8,128)(2,1)}), bf16[4,576,256]{2,1,0:T(8,128)(2,1)}, u32[]{:S(2)}, u32[]{:S(2)}) async-start(bf16[4,576,256]{2,1,0:T(8,128)(2,1)} %shard_map.372), calls=%async_computation.8 | async-start | bytes 2359296 | tf_op jit(solution)/shard_map/all_to_all | solution.py:53
  573.3 211.1 %reduce-scatter.9.cloned.1.call-start = ((), (), s32[]{:S(2)}) async-start(), calls=%async_computation.22 | async-start | bytes 5308416 | tf_op jit(solution)/shard_map/reduce_scatter | solution.py:557
  573.3 105.4 %collective-permute-start.10 = (bf16[192,4096]{1,0:T(8,128)(2,1)}, bf16[192,4096]{1,0:T(8,128)(2,1)}, u32[]{:S(2)}, u32[]{:S(2)}) collective-permute-start(bf16[192,4096]{1,0:T(8,128)(2,1)} %get-tuple-element.205), channel_id=1, source_target_pairs={{0,2},{1,3},{2,0},{3,1},{4,6},{5,7},{6,4},{7,5},{8,10},{9,11},{10,... | collective-permute-start | bytes 4718600 | tf_op jit(solution)/shard_map/ppermute | solution.py:69
  577.2 149.9 %collective-permute-start.11 = (bf16[192,4096]{1,0:T(8,128)(2,1)}, bf16[192,4096]{1,0:T(8,128)(2,1)}, u32[]{:S(2)}, u32[]{:S(2)}) collective-permute-start(bf16[192,4096]{1,0:T(8,128)(2,1)} %get-tuple-element.204), channel_id=1, source_target_pairs={{0,3},{1,0},{2,1},{3,2},{4,7},{5,4},{6,5},{7,6},{8,11},{9,8},{10,9... | collective-permute-start | bytes 4718600 | tf_op jit(solution)/shard_map/ppermute | solution.py:69
  601.7 125.4 %collective-permute-start.12 = (f32[256,768]{1,0:T(8,128)}, f32[256,768]{1,0:T(8,128)}, u32[]{:S(2)}, u32[]{:S(2)}) collective-permute-start(f32[256,768]{1,0:T(8,128)} %fusion.44), channel_id=1, source_target_pairs={{0,0},{1,4},{2,8},{3,12},{4,1},{5,5},{6,9},{7,13},{8,2},{9,6},{10,... | collective-permute-start | bytes 2359304 | tf_op jit(solution)/shard_map/ppermute | solution.py:64
  727.2 20.0 %copy-start.47 = (f32[256]{0:T(256)S(1)}, f32[256]{0:T(256)}, u32[]{:S(2)}) copy-start(f32[256]{0:T(256)} %copy-done.46) | copy-start | bytes 3076
  727.2 20.0 %all-to-all-start.9 = ((bf16[4,576,256]{2,1,0:T(8,128)(2,1)}), bf16[4,576,256]{2,1,0:T(8,128)(2,1)S(1)}, u32[]{:S(2)}, u32[]{:S(2)}) async-start(bf16[4,576,256]{2,1,0:T(8,128)(2,1)} %shard_map.373), calls=%async_computation.11 | async-start | bytes 2359296 | tf_op jit(solution)/shard_map/all_to_all | solution.py:53
  731.3 112.5 %reduce-scatter.11.cloned.1.call-start = ((), (), s32[]{:S(2)}) async-start(), calls=%async_computation.23 | async-start | bytes 5529600 | tf_op jit(solution)/shard_map/reduce_scatter | solution.py:575
  786.9 41.1 %copy-start.52 = (f32[256]{0:T(256)S(1)}, f32[256]{0:T(256)}, u32[]{:S(2)}) copy-start(f32[256]{0:T(256)} %copy-done.51) | copy-start | bytes 3076
  786.9 32.5 %all-to-all-start.12 = ((bf16[4,96,1600]{2,1,0:T(8,128)(2,1)}), bf16[4,96,1600]{2,1,0:T(8,128)(2,1)S(1)}, u32[]{:S(2)}, u32[]{:S(2)}) async-start(bf16[4,96,1600]{2,1,0:T(8,128)(2,1)} %shard_map.378), calls=%async_computation.16 | async-start | bytes 2555904 | tf_op jit(solution)/shard_map/all_to_all | solution.py:53
  819.3 26.6 %copy-start.3 = (bf16[4,96,1600]{2,1,0:T(8,128)(2,1)}, bf16[4,96,1600]{2,1,0:T(8,128)(2,1)S(1)}, u32[]{:S(2)}) copy-start(bf16[4,96,1600]{2,1,0:T(8,128)(2,1)S(1)} %all-to-all-done.12.terms_ref) | copy-start | bytes 3686404
  819.3 35.4 %all-to-all-start.11 = ((bf16[4,96,768]{2,1,0:T(8,128)(2,1)}), bf16[4,96,768]{2,1,0:T(8,128)(2,1)S(1)}, u32[]{:S(2)}, u32[]{:S(2)}) async-start(bf16[4,96,768]{2,1,0:T(8,128)(2,1)} %shard_map.376), calls=%async_computation.15 | async-start | bytes 1179648 | tf_op jit(solution)/shard_map/all_to_all | solution.py:53
  830.2 38.1 %collective-permute-start.13 = (f32[256,768]{0,1:T(8,128)}, f32[256,768]{0,1:T(8,128)S(1)}, u32[]{:S(2)}, u32[]{:S(2)}) collective-permute-start(f32[256,768]{0,1:T(8,128)} %fusion.77), channel_id=1, source_target_pairs={{0,0},{1,4},{2,8},{3,12},{4,1},{5,5},{6,9},{7,13},{8,2},{9,6},{10,... | collective-permute-start | bytes 2359304 | tf_op jit(solution)/shard_map/ppermute | solution.py:64
  854.8 31.1 %all-to-all-start.10 = ((bf16[4,96,896]{2,1,0:T(8,128)(2,1)}), bf16[4,96,896]{2,1,0:T(8,128)(2,1)S(1)}, u32[]{:S(2)}, u32[]{:S(2)}) async-start(bf16[4,96,896]{2,1,0:T(8,128)(2,1)} %shard_map.374), calls=%async_computation.14 | async-start | bytes 1376256 | tf_op jit(solution)/shard_map/all_to_all | solution.py:53
  868.4 21.8 %copy-start.66 = (f32[1,256]{1,0:T(1,128)S(1)}, f32[1,256]{1,0:T(1,128)}, u32[]{:S(2)}) copy-start(f32[1,256]{1,0:T(1,128)} %copy-done.65) | copy-start | bytes 3076
  (60 other events, 295.3 us)
Sparse Core Ops, SparseCore 0:
  47.1 66.0 all-gather.7
  115.1 67.8 all-gather.9
  326.0 32.9 all-gather.11
  440.2 56.0 reduce-scatter.4
  526.0 88.5 reduce-scatter.6
  727.3 57.0 reduce-scatter.8
  787.9 55.9 reduce-scatter.10
